TPU v7x, 256 devices: a whole 4x4x8 slice. The times are simulated.
256 devices in a mesh: base: 16 (over x, z_hi, core), fine: 16 (over z_lo, y).
Axes of the slice: x: 4, y: 4, z: 8 (z_hi: 2, z_lo: 4; z = z_hi * 4 + z_lo), core: 2. Of those that a mesh axis runs over, the one named last changes fastest.
Arguments:
- coarse_level: float32 [9, 128, 256, 128], P(None, 'base', 'fine'), may hold values from -6 to 6
- fine_level: float32 [16, 16, 9, 16, 8, 128], P('base', 'fine'), may hold values from -6 to 6
- box_list: int32 [16, 16, 2], P('base'), may hold values from 0 to 252, as said below
- patch_owner: int32 [16, 16], P('base'), may hold values from 0 to 15, each once within a row
- reaction_table: int32 [9, 2], replicated, may hold values from 0 to 8
- viscosity: float32 [9], replicated, may hold values from 0.01 to 0.08
- reaction_rates: float32 [9], replicated, may hold values from 0.05 to 0.3
Outputs:
- coarse_out: float32 [9, 128, 256, 128], P(None, 'base', 'fine')
- fine_out: float32 [16, 16, 9, 16, 8, 128], P('base', 'fine')
Inputs may be any that keep to these rules, and one draw needn't show every extreme that they name: `box_list`: in each group the boxes are disjoint; the first entry is a multiple of 4 and at most 252, the second is 0 or 64; no block of 16 coarse cells along the second dimension holds more than 2 boxes of a group, and some block holds exactly 2 in every group. `patch_owner`: each group's row is a permutation.
All inputs are finite; a program needn't handle non-finite values.
Results may differ from a plain program's by a relative error of at most 0.0003.
Values sent between devices are 32-bit elements; how exact they have to be, the bound alone decides.
A program may use at most 64 MiB of HBM per device.

v0:
```python
import jax
import jax.numpy as jnp
from jax import lax
from jax.sharding import PartitionSpec as P

BY = 4
MOST = 2
BZ = 64


def with_halo(block, sides, width):
    for axis, dim in sides:
        count = lax.axis_size(axis)
        forward = [(i, i + 1) for i in range(count - 1)]
        forward.append((count - 1, 0))
        backward = [(target, source) for source, target in forward]
        low = lax.ppermute(
            lax.slice_in_dim(block, block.shape[dim] - width, None, axis=dim), axis, forward
        )
        high = lax.ppermute(lax.slice_in_dim(block, 0, width, axis=dim), axis, backward)
        block = jnp.concatenate([low, block, high], axis=dim)
    return block


def reaction(values, reaction_rates, left_ids, right_ids):
    fields = values.shape[0]
    levels = lax.broadcasted_iota(jnp.int32, (fields, fields), 1)
    pick_left = (left_ids[:, None] == levels).astype(jnp.float32)
    pick_right = (right_ids[:, None] == levels).astype(jnp.float32)
    left_term = jnp.einsum("fg,gxyz->fxyz", pick_left, values, precision=lax.Precision.HIGHEST)
    right_term = jnp.einsum("fg,gxyz->fxyz", pick_right, values, precision=lax.Precision.HIGHEST)
    return reaction_rates[:, None, None, None] * left_term * right_term


def coarse_advance(centre, neighbours, viscosity, reaction_rates, left_ids, right_ids):
    return (
        centre
        + viscosity[:, None, None, None] * (neighbours - 6.0 * centre)
        + reaction(centre, reaction_rates, left_ids, right_ids)
    )


def widen_face(face):
    return jnp.repeat(jnp.repeat(face, 2, axis=1), 2, axis=2)


def fine_advance(fine_box, faces, viscosity, reaction_rates, left_ids, right_ids):
    face_xlo, face_xhi, face_ylo, face_yhi, face_zlo, face_zhi = faces
    low_x = widen_face(face_xlo)[:, None]
    high_x = widen_face(face_xhi)[:, None]
    low_y = widen_face(face_ylo)[:, :, None]
    high_y = widen_face(face_yhi)[:, :, None]
    low_z = widen_face(face_zlo)[:, :, :, None]
    high_z = widen_face(face_zhi)[:, :, :, None]
    pair_x = jnp.concatenate([low_x, fine_box[:, :-1]], axis=1) + jnp.concatenate(
        [fine_box[:, 1:], high_x], axis=1
    )
    pair_y = jnp.concatenate([low_y, fine_box[:, :, :-1]], axis=2) + jnp.concatenate(
        [fine_box[:, :, 1:], high_y], axis=2
    )
    cells_z = fine_box.shape[3]
    z_pos = lax.broadcasted_iota(jnp.int32, fine_box.shape, 3)
    below = jnp.where(z_pos == 0, low_z, jnp.roll(fine_box, 1, 3))
    above = jnp.where(z_pos == cells_z - 1, high_z, jnp.roll(fine_box, -1, 3))
    pair_z = below + above
    neighbours = pair_x + pair_y + pair_z
    return (
        fine_box
        + 2.0 * viscosity[:, None, None, None] * (neighbours - 6.0 * fine_box)
        + 0.5 * reaction(fine_box, reaction_rates, left_ids, right_ids)
    )


def coarsen(fine_box):
    fields, cells_x, cells_y, cells_z = fine_box.shape
    pairs_x = fine_box.reshape(fields, cells_x // 2, 2, cells_y, cells_z).sum(axis=2)
    pairs_y = pairs_x.reshape(fields, cells_x // 2, cells_y // 2, 2, cells_z).sum(axis=3)
    pair_z = (
        lax.broadcasted_iota(jnp.int32, (cells_z, cells_z // 2), 0) // 2
        == lax.broadcasted_iota(jnp.int32, (cells_z, cells_z // 2), 1)
    ).astype(jnp.float32)
    summed = jnp.einsum("fxyz,zw->fxyw", pairs_y, pair_z, precision=lax.Precision.HIGHEST)
    return 0.125 * summed


def packed_faces(extended, offset, z_start):
    fields, rows_x, _, cells_z = extended.shape
    window = lax.dynamic_slice(extended, (0, 0, offset, 0), (fields, rows_x, BY + 2, cells_z))
    half = lax.dynamic_slice_in_dim(window, z_start, BZ, axis=3)
    low_x = half[:, 0, 1:-1, :]
    high_x = half[:, -1, 1:-1, :]
    low_y = half[:, 1:-1, 0, :]
    high_y = half[:, 1:-1, -1, :]
    inner = window[:, 1:-1, 1:-1, :]
    low_z = lax.dynamic_index_in_dim(inner, (z_start - 1) % cells_z, 3, keepdims=False)
    high_z = lax.dynamic_index_in_dim(inner, (z_start + BZ) % cells_z, 3, keepdims=False)
    return jnp.concatenate(
        [
            face_part.reshape(fields, -1)
            for face_part in (low_x, high_x, low_y, high_y, low_z, high_z)
        ],
        axis=1,
    )


def unpack_faces(packed, cells_x):
    fields = packed.shape[0]
    widths = [BY * BZ, BY * BZ, cells_x * BZ, cells_x * BZ, cells_x * BY, cells_x * BY]
    shapes = [
        (fields, BY, BZ),
        (fields, BY, BZ),
        (fields, cells_x, BZ),
        (fields, cells_x, BZ),
        (fields, cells_x, BY),
        (fields, cells_x, BY),
    ]
    face_list = []
    offset = 0
    for width_now, shape_now in zip(widths, shapes):
        face_list.append(packed[:, offset : offset + width_now].reshape(shape_now))
        offset = offset + width_now
    return tuple(face_list)


def per_device(
    coarse_level, fine_level, box_list, patch_owner, reaction_table, viscosity, reaction_rates
):
    fields, cells_x, height, cells_z = coarse_level.shape
    devices_fine = lax.axis_size("fine")
    my_index = lax.axis_index("fine")
    left_ids = reaction_table[:, 0]
    right_ids = reaction_table[:, 1]

    def extend(coarse_state):
        return with_halo(coarse_state, (("base", 1), ("fine", 2)), 1)

    corners = box_list[0]
    owners = patch_owner[0]
    y_cell = corners[:, 0]
    z_cell = corners[:, 1]
    y_block = y_cell // height
    row_ids = lax.broadcasted_iota(jnp.int32, (devices_fine, devices_fine), 0)
    col_ids = lax.broadcasted_iota(jnp.int32, (devices_fine, devices_fine), 1)
    holder = jnp.sum(jnp.where(owners[None, :] == row_ids, col_ids, 0), axis=1)
    slot_rank = jnp.sum(
        jnp.where((y_block[:, None] == y_block[None, :]) & (col_ids < row_ids), 1, 0), axis=1
    )
    patch_ids = jnp.arange(devices_fine, dtype=jnp.int32)
    slot_patch = []
    slot_filled = []
    for slot_number in range(MOST):
        is_hit = (y_block == my_index) & (slot_rank == slot_number)
        slot_patch.append(jnp.sum(jnp.where(is_hit, patch_ids, 0)))
        slot_filled.append(jnp.any(is_hit))
    box_of_dest = holder
    dest_here = y_block[box_of_dest] == my_index
    dest_slot = slot_rank[box_of_dest]
    source_of_mine = y_block[holder[my_index]]

    def route_faces(extended):
        slots = []
        for slot_number in range(MOST):
            patch_id = slot_patch[slot_number]
            slots.append(
                packed_faces(extended, y_cell[patch_id] - my_index * height, z_cell[patch_id])
            )
        rows = jnp.where(
            (dest_here & (dest_slot == 0))[:, None],
            slots[0].reshape(1, -1),
            jnp.where(dest_here[:, None], slots[1].reshape(1, -1), 0.0),
        )
        arrived = lax.all_to_all(rows, "fine", 0, 0, tiled=True)
        chosen = lax.dynamic_index_in_dim(arrived, source_of_mine, 0, keepdims=False)
        return chosen.reshape(slots[0].shape)

    old_ext = extend(coarse_level)
    old_shell = route_faces(old_ext)
    centre = old_ext[:, 1:-1, 1:-1, :]
    neighbours = (
        old_ext[:, :-2, 1:-1, :]
        + old_ext[:, 2:, 1:-1, :]
        + (old_ext[:, 1:-1, :-2, :] + old_ext[:, 1:-1, 2:, :])
        + (jnp.roll(centre, 1, 3) + jnp.roll(centre, -1, 3))
    )
    coarse_next = coarse_advance(centre, neighbours, viscosity, reaction_rates, left_ids, right_ids)
    new_ext = extend(coarse_next)
    new_shell = route_faces(new_ext)

    fine_box = fine_level[0, 0]
    old_faces = unpack_faces(old_shell, cells_x)
    fine_box = fine_advance(fine_box, old_faces, viscosity, reaction_rates, left_ids, right_ids)
    mid_faces = unpack_faces(0.5 * (old_shell + new_shell), cells_x)
    fine_box = fine_advance(fine_box, mid_faces, viscosity, reaction_rates, left_ids, right_ids)
    averaged = coarsen(fine_box)

    rows_in = lax.all_gather(averaged.reshape(-1, 128), "fine", axis=0, tiled=False)
    coarse_out = coarse_next
    for slot_number in range(MOST):
        patch_id = slot_patch[slot_number]
        corner = (0, 0, y_cell[patch_id] - my_index * height, z_cell[patch_id])
        incoming = lax.dynamic_index_in_dim(rows_in, owners[patch_id], 0, keepdims=False)
        incoming = incoming.reshape(averaged.shape)
        present = lax.dynamic_slice(coarse_out, corner, incoming.shape)
        coarse_out = lax.dynamic_update_slice(
            coarse_out, jnp.where(slot_filled[slot_number], incoming, present), corner
        )
    return (coarse_out, fine_box[None, None])


def solution(mesh):
    placed = (
        P(None, "base", "fine", None),
        P("base", "fine", None, None, None, None),
        P("base", None, None),
        P("base", None),
        P(),
        P(),
        P(),
    )
    return jax.shard_map(
        per_device,
        mesh=mesh,
        in_specs=placed,
        out_specs=(P(None, "base", "fine", None), P("base", "fine", None, None, None, None)),
        check_vma=False,
    )
```

profile of v0, /device:TPU:120, one launch (start us, length us, event | category | flops | bytes accessed | tf_op | source)
XLA Modules:
  0.0 262.0 jit_solution(8931420418540671804)
XLA Ops:
  7.2 1.4 copy.288
  8.7 7.7 %collective-permute-start.1 = (f32[9,1,16,128]{3,0,2,1:T(8,128)S(1)}, f32[9,1,16,128]{3,0,2,1:T(8,128)S(1)}, u32[]{:S(2)}, u32[]{:S(2)}) collective-permute-start(f32[9,1,16,128]{3,0,2,1:T(8,128)S(1)} %get-tuple-element.72), channel_id=1, source_target_pairs={{16,0},{32,16},{48,32},{64,48},{80,64},{96,80},{112,96},{128,112},... | collective-permute-start | bytes 221192 | tf_op jit(solution)/shard_map/ppermute | solution.py:20
  17.0 1.7 fusion.60
  18.7 1.6 fusion.61
  20.5 0.7 gather_fusion
  21.2 0.7 gather_fusion.1
  21.9 0.7 fusion.49
  22.6 1.9 convolution_multiply_fusion.5
  25.1 0.7 select_reduce_fusion.3
  26.2 0.6 collective-permute-start.2
  26.9 1.5 collective-permute-start.3
  32.5 1.3 constant_dynamic-slice_fusion.22
  42.5 4.1 %fusion.4 = f32[9,8,16,128]{3,0,2,1:T(8,128)S(1)} fusion(f32[9,8,16,128]{3,0,2,1:T(8,128)} %convolution_multiply_fusion.5, f32[9,8,16,128]{3,0,2,1:T(8,128)S(1)} %copy.288, f32[9,10,1,128]{3,0,2,1:T(8,128)} %copy-done.6, f32[9,10,16,128]{3,0,2,1:T(8,128)S(1)} %constant_dynamic-update-slice_fusion, f32[9,10,1,128]{3,0,2,1:T(8,128)} %copy-done.4, ...), kind=kOutput, calls=%fused_computation.17 | convolution fusion | flops 18432080 | bytes 3926088 | tf_op jit(solution)/shard_map/fg,gxyz->fxyz/dot_general | solution.py:31
  46.7 7.7 %collective-permute-start.5 = (f32[9,1,16,128]{3,0,2,1:T(8,128)S(1)}, f32[9,1,16,128]{3,0,2,1:T(8,128)S(1)}, u32[]{:S(2)}, u32[]{:S(2)}) collective-permute-start(f32[9,1,16,128]{3,0,2,1:T(8,128)S(1)} %get-tuple-element.59), channel_id=1, source_target_pairs={{16,0},{32,16},{48,32},{64,48},{80,64},{96,80},{112,96},{128,112},... | collective-permute-start | bytes 221192 | tf_op jit(solution)/shard_map/ppermute | solution.py:20
  54.8 3.5 %collective-permute-done.4 = f32[9,1,16,128]{3,0,2,1:T(8,128)S(1)} collective-permute-done((f32[9,1,16,128]{3,0,2,1:T(8,128)S(1)}, f32[9,1,16,128]{3,0,2,1:T(8,128)S(1)}, u32[]{:S(2)}, u32[]{:S(2)}) %collective-permute-start.4) | collective-permute-done | bytes 73760 | tf_op jit(solution)/shard_map/ppermute | solution.py:17
  58.3 4.9 %collective-permute-start.6 = (f32[9,10,1,128]{3,0,2,1:T(8,128)S(1)}, f32[9,10,1,128]{3,0,2,1:T(8,128)S(1)}, u32[]{:S(2)}, u32[]{:S(2)}) collective-permute-start(f32[9,10,1,128]{3,0,2,1:T(8,128)S(1)} %get-tuple-element.44), channel_id=1, source_target_pairs={{0,1},{1,2},{2,3},{3,4},{4,5},{5,6},{6,7},{7,8},{8,9},{9,10},{10,1... | collective-permute-start | bytes 138248 | tf_op jit(solution)/shard_map/ppermute | solution.py:17
  63.3 0.7 dynamic-slice_reduce_fusion.6
  65.5 6.1 %collective-permute-done.7 = f32[9,10,1,128]{3,0,2,1:T(8,128)S(1)} collective-permute-done((f32[9,10,1,128]{3,0,2,1:T(8,128)S(1)}, f32[9,10,1,128]{3,0,2,1:T(8,128)S(1)}, u32[]{:S(2)}, u32[]{:S(2)}) %collective-permute-start.7) | collective-permute-done | bytes 46112 | tf_op jit(solution)/shard_map/ppermute | solution.py:20
  71.7 0.7 dynamic-slice_reduce_fusion.2
  74.1 3.0 %broadcast_select_fusion = (f32[16,1,14400]{2,1,0:T(1,128)}, f32[16,1,14400]{2,1,0:T(1,128)}) fusion(pred[16]{0:T(512)(128)(4,1)S(1)} %copy-done.20, pred[16]{0:T(512)(128)(4,1)S(1)} %copy-done.21, f32[14400]{0:T(1024)S(1)} %broadcast_in_dim.221, f32[14400]{0:T(1024)S(1)} %broadcast_in_dim.219, f32[14400]{0:T(1024)S(1)} %broadcast_in_dim.200, ...), kind=kLoop, calls=%fused_computation.2 | loop fusion | flops 921600 | bytes 2073632 | tf_op jit(solution)/shard_map/jit(_where)/select_n | solution.py:167
  77.2 7.4 %all-to-all-start.1 = ((f32[16,1,14400]{2,1,0:T(1,128)}), f32[16,1,14400]{2,1,0:T(1,128)S(1)}, u32[]{:S(2)}, u32[]{:S(2)}) async-start(f32[16,1,14400]{2,1,0:T(1,128)} %get-tuple-element.86), calls=%async_computation.1 | async-start | bytes 1851392 | tf_op jit(solution)/shard_map/all_to_all | solution.py:172
  85.6 18.4 %all-to-all-done.1 = f32[16,1,14400]{2,1,0:T(1,128)S(1)} async-done(((f32[16,1,14400]{2,1,0:T(1,128)}), f32[16,1,14400]{2,1,0:T(1,128)S(1)}, u32[]{:S(2)}, u32[]{:S(2)}) %all-to-all-start.1) | async-done | bytes 921632 | tf_op jit(solution)/shard_map/all_to_all | solution.py:172
  104.0 7.7 %all-to-all-start = ((f32[16,1,14400]{2,1,0:T(1,128)}), f32[16,1,14400]{2,1,0:T(1,128)}, u32[]{:S(2)}, u32[]{:S(2)}) async-start(f32[16,1,14400]{2,1,0:T(1,128)} %get-tuple-element.87), calls=%async_computation | async-start | bytes 1851392 | tf_op jit(solution)/shard_map/all_to_all | solution.py:172
  117.3 1.9 convolution_multiply_fusion.3
  119.2 1.3 fusion.58
  120.5 1.5 fusion.59
  122.1 1.6 fusion.56
  123.7 1.7 fusion.57
  125.4 1.0 dynamic-slice_reduce_fusion.8
  126.4 5.1 %all-to-all-done = f32[16,1,14400]{2,1,0:T(1,128)} async-done(((f32[16,1,14400]{2,1,0:T(1,128)}), f32[16,1,14400]{2,1,0:T(1,128)}, u32[]{:S(2)}, u32[]{:S(2)}) %all-to-all-start) | async-done | bytes 921632 | tf_op jit(solution)/shard_map/all_to_all | solution.py:172
  131.5 1.0 dynamic-slice_reduce_fusion.9
  135.9 5.1 %fusion.3 = f32[9,16,8,128]{3,0,2,1:T(8,128)S(1)} fusion(f32[9,16,8,128]{3,0,2,1:T(8,128)} %convolution_multiply_fusion.3, f32[9,15,8,128]{3,0,2,1:T(8,128)} %get-tuple-element.67, f32[9,1,8,128]{3,0,2,1:T(8,128)S(1)} %copy.305, f32[9,1,8,128]{3,0,2,1:T(8,128)S(1)} %copy.307, f32[9,15,8,128]{3,0,2,1:T(8,128)} %get-tuple-element.66, ...), kind=kOutput, calls=%fused_computation.14 | convolution fusion | flops 18874448 | bytes 5317960 | tf_op jit(solution)/shard_map/fg,gxyz->fxyz/dot_general | solution.py:31
  141.0 1.7 fusion.51
  142.6 1.7 fusion.52
  144.3 1.5 fusion.54
  145.9 1.4 fusion.53
  147.3 1.6 convolution_multiply_fusion.1
  152.0 5.4 %bitcast_reduce_fusion = (f32[9,8,8,128]{3,0,2,1:T(8,128)}, f32[9,16,8,128]{3,0,2,1:T(8,128)S(1)}) fusion(f32[9,16,8,128]{3,0,2,1:T(8,128)} %convolution_multiply_fusion.1, f32[9,16,8,128]{3,0,2,1:T(8,128)S(1)} %fusion.3, s32[9]{0:T(128)} %copy-done.8, f32[9,16,8,1]{3,0,2,1:T(8,128)} %get-tuple-element.52, f32[9,16,8,127]{3,0,2,1:T(8,128)} %get-tuple-element.50, ...), kind=kOutput, calls=%fused_computation.52 | convolution fusion | flops 18948176 | bytes 5612872 | tf_op jit(solution)/shard_map/fg,gxyz->fxyz/dot_general | solution.py:31
  157.4 1.1 reduce_sum.62
  158.8 0.8 all_gather_reshape.3
  164.1 1.0 copy.341
  165.1 76.8 %all-gather.2.cloned.1.call-done = f32[16,144,128]{2,1,0:T(8,128)} async-done(((f32[1,144,128]{2,1,0:T(8,128)}), f32[16,144,128]{2,1,0:T(8,128)}) %all-gather.2.cloned.1.call-update) | async-done | bytes 1179664 | tf_op jit(solution)/shard_map/all_gather | solution.py:196
  241.8 0.9 constant_dynamic-slice_fusion.10
  242.9 0.8 copy_select_fusion.1
  243.7 4.8 %dynamic_update_slice.6 = f32[9,8,16,128]{3,0,2,1:T(8,128)S(1)} dynamic-update-slice(f32[9,8,16,128]{3,0,2,1:T(8,128)S(1)} %fusion.4, f32[9,8,4,64]{3,0,2,1:T(8,128)S(1)} %copy_select_fusion.1, s32[]{:T(128)} %constant.194.clone.1, s32[]{:T(128)} %constant.194.clone.1, s32[]{:T(128)S(6)} %select_n.267, s32[]{:T(128)S(6)} %select_n.238) | dynamic-update-slice | bytes 147460 | tf_op jit(solution)/shard_map/dynamic_update_slice | solution.py:204
  248.6 0.7 copy_select_fusion
  249.4 4.8 %dynamic_update_slice.7 = f32[9,8,16,128]{3,0,2,1:T(8,128)S(1)} dynamic-update-slice(f32[9,8,16,128]{3,0,2,1:T(8,128)S(1)} %dynamic_update_slice.6, f32[9,8,4,64]{3,0,2,1:T(8,128)S(1)} %copy_select_fusion, s32[]{:T(128)} %constant.194.clone.1, s32[]{:T(128)} %constant.194.clone.1, s32[]{:T(128)S(6)} %select_n.271, s32[]{:T(128)S(6)} %select_n.248) | dynamic-update-slice | bytes 147460 | tf_op jit(solution)/shard_map/dynamic_update_slice | solution.py:204
  254.2 1.0 copy.340
  (212 shorter events, 17.3 us)
Async XLA Ops:
  7.2 9.3 %copy-start.16 = (s32[1,16,2]{1,2,0:T(2,128)S(1)}, s32[1,16,2]{1,2,0:T(2,128)}, u32[]{:S(2)}) copy-start(s32[1,16,2]{1,2,0:T(2,128)} %param.9) | copy-start | bytes 388
  8.6 17.1 %collective-permute-start = (f32[9,1,16,128]{3,0,2,1:T(8,128)S(1)}, f32[9,1,16,128]{3,0,2,1:T(8,128)S(1)}, u32[]{:S(2)}, u32[]{:S(2)}) collective-permute-start(f32[9,1,16,128]{3,0,2,1:T(8,128)S(1)} %get-tuple-element.73), channel_id=1, source_target_pairs={{0,16},{16,32},{32,48},{48,64},{64,80},{80,96},{96,112},{112,128},... | collective-permute-start | bytes 221192 | tf_op jit(solution)/shard_map/ppermute | solution.py:17
  8.7 17.4 %collective-permute-start.1 = (f32[9,1,16,128]{3,0,2,1:T(8,128)S(1)}, f32[9,1,16,128]{3,0,2,1:T(8,128)S(1)}, u32[]{:S(2)}, u32[]{:S(2)}) collective-permute-start(f32[9,1,16,128]{3,0,2,1:T(8,128)S(1)} %get-tuple-element.72), channel_id=1, source_target_pairs={{16,0},{32,16},{48,32},{64,48},{80,64},{96,80},{112,96},{128,112},... | collective-permute-start | bytes 221192 | tf_op jit(solution)/shard_map/ppermute | solution.py:20
  18.7 1.7 copy-start.12
  18.7 3.9 %copy-start.22 = (s32[9,2]{0,1:T(2,128)S(1)}, s32[9,2]{0,1:T(2,128)}, u32[]{:S(2)}) copy-start(s32[9,2]{0,1:T(2,128)} %param.11) | copy-start | bytes 220
  18.7 3.9 %copy-start.14 = (f32[9]{0:T(128)S(1)}, f32[9]{0:T(128)}, u32[]{:S(2)}) copy-start(f32[9]{0:T(128)} %param.13) | copy-start | bytes 112
  20.3 2.3 copy-start.1
  20.5 0.7 copy-start.27
  22.6 19.9 %copy-start.8 = (s32[9]{0:T(128)}, s32[9]{0:T(128)S(1)}, u32[]{:S(2)}) copy-start(s32[9]{0:T(128)S(1)} %get-tuple-element.93) | copy-start | bytes 112
  22.6 94.6 %copy-start.10 = (s32[9]{0:T(128)}, s32[9]{0:T(128)S(1)}, u32[]{:S(2)}) copy-start(s32[9]{0:T(128)S(1)} %get-tuple-element.94) | copy-start | bytes 112
  26.2 15.7 %copy-start.3 = (f32[9,1,16,128]{3,0,2,1:T(8,128)}, f32[9,1,16,128]{3,0,2,1:T(8,128)S(1)}, u32[]{:S(2)}) copy-start(f32[9,1,16,128]{3,0,2,1:T(8,128)S(1)} %collective-permute-done.1) | copy-start | bytes 221188
  26.2 15.6 %collective-permute-start.2 = (f32[9,10,1,128]{3,0,2,1:T(8,128)S(1)}, f32[9,10,1,128]{3,0,2,1:T(8,128)S(1)}, u32[]{:S(2)}, u32[]{:S(2)}) collective-permute-start(f32[9,10,1,128]{3,0,2,1:T(8,128)S(1)} %get-tuple-element.46), channel_id=1, source_target_pairs={{0,1},{1,2},{2,3},{3,4},{4,5},{5,6},{6,7},{7,8},{8,9},{9,10},{10,1... | collective-permute-start | bytes 138248 | tf_op jit(solution)/shard_map/ppermute | solution.py:17
  26.9 15.0 %collective-permute-start.3 = (f32[9,10,1,128]{3,0,2,1:T(8,128)S(1)}, f32[9,10,1,128]{3,0,2,1:T(8,128)S(1)}, u32[]{:S(2)}, u32[]{:S(2)}) collective-permute-start(f32[9,10,1,128]{3,0,2,1:T(8,128)S(1)} %get-tuple-element.47), channel_id=1, source_target_pairs={{1,0},{2,1},{3,2},{4,3},{5,4},{6,5},{7,6},{8,7},{9,8},{10,9},{11,1... | collective-permute-start | bytes 138248 | tf_op jit(solution)/shard_map/ppermute | solution.py:20
  41.8 0.6 copy-start.4
  41.9 0.6 copy-start.6
  42.5 12.0 %copy-start.5 = (f32[9,10,1,128]{3,0,2,1:T(8,128)S(1)}, f32[9,10,1,128]{3,0,2,1:T(8,128)}, u32[]{:S(2)}) copy-start(f32[9,10,1,128]{3,0,2,1:T(8,128)} %copy-done.4) | copy-start | bytes 138244
  42.5 12.0 %copy-start.7 = (f32[9,10,1,128]{3,0,2,1:T(8,128)S(1)}, f32[9,10,1,128]{3,0,2,1:T(8,128)}, u32[]{:S(2)}) copy-start(f32[9,10,1,128]{3,0,2,1:T(8,128)} %copy-done.6) | copy-start | bytes 138244
  46.6 11.6 %collective-permute-start.4 = (f32[9,1,16,128]{3,0,2,1:T(8,128)S(1)}, f32[9,1,16,128]{3,0,2,1:T(8,128)S(1)}, u32[]{:S(2)}, u32[]{:S(2)}) collective-permute-start(f32[9,1,16,128]{3,0,2,1:T(8,128)S(1)} %get-tuple-element.58), channel_id=1, source_target_pairs={{0,16},{16,32},{32,48},{48,64},{64,80},{80,96},{96,112},{112,128},... | collective-permute-start | bytes 221192 | tf_op jit(solution)/shard_map/ppermute | solution.py:17
  46.7 11.5 %collective-permute-start.5 = (f32[9,1,16,128]{3,0,2,1:T(8,128)S(1)}, f32[9,1,16,128]{3,0,2,1:T(8,128)S(1)}, u32[]{:S(2)}, u32[]{:S(2)}) collective-permute-start(f32[9,1,16,128]{3,0,2,1:T(8,128)S(1)} %get-tuple-element.59), channel_id=1, source_target_pairs={{16,0},{32,16},{48,32},{64,48},{80,64},{96,80},{112,96},{128,112},... | collective-permute-start | bytes 221192 | tf_op jit(solution)/shard_map/ppermute | solution.py:20
  58.3 7.2 %collective-permute-start.6 = (f32[9,10,1,128]{3,0,2,1:T(8,128)S(1)}, f32[9,10,1,128]{3,0,2,1:T(8,128)S(1)}, u32[]{:S(2)}, u32[]{:S(2)}) collective-permute-start(f32[9,10,1,128]{3,0,2,1:T(8,128)S(1)} %get-tuple-element.44), channel_id=1, source_target_pairs={{0,1},{1,2},{2,3},{3,4},{4,5},{5,6},{6,7},{7,8},{8,9},{9,10},{10,1... | collective-permute-start | bytes 138248 | tf_op jit(solution)/shard_map/ppermute | solution.py:17
  63.2 8.3 %collective-permute-start.7 = (f32[9,10,1,128]{3,0,2,1:T(8,128)S(1)}, f32[9,10,1,128]{3,0,2,1:T(8,128)S(1)}, u32[]{:S(2)}, u32[]{:S(2)}) collective-permute-start(f32[9,10,1,128]{3,0,2,1:T(8,128)S(1)} %get-tuple-element.45), channel_id=1, source_target_pairs={{1,0},{2,1},{3,2},{4,3},{5,4},{6,5},{7,6},{8,7},{9,8},{10,9},{11,1... | collective-permute-start | bytes 138248 | tf_op jit(solution)/shard_map/ppermute | solution.py:20
  72.4 1.7 copy-start.20
  72.4 1.7 copy-start.21
  77.2 34.6 %copy-start.28 = (s32[16]{0:T(128)S(1)}, s32[16]{0:T(128)}, u32[]{:S(2)}) copy-start(s32[16]{0:T(128)} %copy-done.27) | copy-start | bytes 196
  77.2 39.0 %copy-start = (f32[1,1,9,16,8,128]{5,4,3,2,1,0:T(8,128)S(1)}, f32[1,1,9,16,8,128]{5,4,3,2,1,0:T(8,128)}, u32[]{:S(2)}) copy-start(f32[1,1,9,16,8,128]{5,4,3,2,1,0:T(8,128)} %param.8) | copy-start | bytes 1769476
  77.2 26.8 %all-to-all-start.1 = ((f32[16,1,14400]{2,1,0:T(1,128)}), f32[16,1,14400]{2,1,0:T(1,128)S(1)}, u32[]{:S(2)}, u32[]{:S(2)}) async-start(f32[16,1,14400]{2,1,0:T(1,128)} %get-tuple-element.86), calls=%async_computation.1 | async-start | bytes 1851392 | tf_op jit(solution)/shard_map/all_to_all | solution.py:172
  85.1 50.8 %copy-start.17 = (pred[128]{0:T(512)(128)(4,1)}, pred[128]{0:T(512)(128)(4,1)S(1)}, u32[]{:S(2)}) copy-start(pred[128]{0:T(512)(128)(4,1)S(1)} %get-tuple-element.106) | copy-start | bytes 388
  104.0 11.5 %copy-start.2 = (f32[16,1,14400]{2,1,0:T(1,128)}, f32[16,1,14400]{2,1,0:T(1,128)S(1)}, u32[]{:S(2)}) copy-start(f32[16,1,14400]{2,1,0:T(1,128)S(1)} %all-to-all-done.1) | copy-start | bytes 2764804
  104.0 13.2 %copy-start.23 = (f32[9]{0:T(128)S(1)}, f32[9]{0:T(128)}, u32[]{:S(2)}) copy-start(f32[9]{0:T(128)} %param.12) | copy-start | bytes 112
  104.0 13.2 %copy-start.15 = (f32[9]{0:T(128)S(1)}, f32[9]{0:T(128)}, u32[]{:S(2)}) copy-start(f32[9]{0:T(128)} %param.13) | copy-start | bytes 112
  104.0 27.5 %all-to-all-start = ((f32[16,1,14400]{2,1,0:T(1,128)}), f32[16,1,14400]{2,1,0:T(1,128)}, u32[]{:S(2)}, u32[]{:S(2)}) async-start(f32[16,1,14400]{2,1,0:T(1,128)} %get-tuple-element.87), calls=%async_computation | async-start | bytes 1851392 | tf_op jit(solution)/shard_map/all_to_all | solution.py:172
  111.7 130.1 %all-gather.2.cloned.1.call-start = ((), (), s32[]{:S(2)}) async-start(), calls=%async_computation.2 | async-start | bytes 1253376 | tf_op jit(solution)/shard_map/all_gather | solution.py:196
  111.7 24.1 %copy-start.18 = (pred[128]{0:T(512)(128)(4,1)}, pred[128]{0:T(512)(128)(4,1)S(1)}, u32[]{:S(2)}) copy-start(pred[128]{0:T(512)(128)(4,1)S(1)} %iota_compare_fusion.5) | copy-start | bytes 388
  117.3 18.6 %copy-start.19 = (f32[9]{0:T(128)}, f32[9]{0:T(128)S(1)}, u32[]{:S(2)}) copy-start(f32[9]{0:T(128)S(1)} %broadcast_multiply_fusion) | copy-start | bytes 112
  134.7 1.1 copy-start.9
  145.9 1.4 copy-start.11
  151.9 6.6 %copy-start.24 = (pred[128]{0:T(512)(128)(4,1)S(1)}, pred[128]{0:T(512)(128)(4,1)}, u32[]{:S(2)}) copy-start(pred[128]{0:T(512)(128)(4,1)} %get-tuple-element.105) | copy-start | bytes 388
  151.9 6.6 %copy-start.25 = (s32[128]{0:T(128)S(1)}, s32[128]{0:T(128)}, u32[]{:S(2)}) copy-start(s32[128]{0:T(128)} %get-tuple-element.107) | copy-start | bytes 1540
  152.0 6.6 %copy-start.26 = (s32[128]{0:T(128)S(1)}, s32[128]{0:T(128)}, u32[]{:S(2)}) copy-start(s32[128]{0:T(128)} %get-tuple-element.108) | copy-start | bytes 1540
  157.4 2.2 copy-start.13
Sparse Core Ops, SparseCore 0:
  159.7 82.0 all-gather.1
where the time goes:
time: 263 us; the launch traced here: 262 us
  waiting for transfers between devices  110 us (42%)
  local copies, waits for them, and re-layouts  50.1 us (19%)
  starting transfers between devices  37.8 us (14%)
  between operations  33.7 us (13%)
  matrix products  20.3 us (8%)
  other arithmetic  10.3 us (4%)
    all_gather x1, waiting for transfers between devices, per_device(): lax.all_gather(averaged.reshape(-1, 128), 'fine', axis=0, tiled=False)  76.8 us
    all_to_all x2, waiting for transfers between devices, route_faces(): arrived = lax.all_to_all(rows, 'fine', 0, 0, tiled=True)  23.5 us
    ppermute x4, starting transfers between devices, with_halo(): lax.ppermute(lax.slice_in_dim(block, 0, width, axis=dim), axis, backward)  17 us
    all_to_all x2, starting transfers between devices, route_faces(): arrived = lax.all_to_all(rows, 'fine', 0, 0, tiled=True)  15 us
    dot_general x3, matrix products, reaction(): jnp.einsum('fg,gxyz->fxyz', pick_right, values, precision=lax.Precision.H...  14.6 us
    dynamic_update_slice x2, local copies, waits for them, and re-layouts, per_device(): lax.dynamic_update_slice(coarse_out, jnp.where(slot_filled[slot_number],...  9.66 us
    slice x4, local copies, waits for them, and re-layouts, fine_advance(): above = jnp.where(z_pos == cells_z - 1, high_z, jnp.roll(fine_box, -1, 3))  6.7 us
    ppermute x4, waiting for transfers between devices, with_halo(): lax.ppermute(lax.slice_in_dim(block, 0, width, axis=dim), axis, backward)  6.09 us
  transfers between devices with their start and end apart: 11, of which 5 were waited for; matrix products, arithmetic and copies ran while one was open for 11% of the time, Pallas kernels for 0%

commit v1 on v0

--- a/solution.py
+++ b/solution.py
@@ -193,7 +193,9 @@
     fine_box = fine_advance(fine_box, mid_faces, viscosity, reaction_rates, left_ids, right_ids)
     averaged = coarsen(fine_box)
 
-    rows_in = lax.all_gather(averaged.reshape(-1, 128), "fine", axis=0, tiled=False)
+    dest_ids = lax.broadcasted_iota(jnp.int32, (devices_fine, 1), 0)
+    sent = jnp.where(dest_ids == source_of_mine, averaged.reshape(1, -1), 0.0)
+    rows_in = lax.all_to_all(sent, "fine", 0, 0, tiled=True)
     coarse_out = coarse_next
     for slot_number in range(MOST):
         patch_id = slot_patch[slot_number]

time: 263 us -> 207 us (0.79)
  the two profiles are of different devices: /device:TPU:120 before, /device:TPU:34 now
where the time goes in v1:
time: 207 us; the launch traced here: 206 us
  waiting for transfers between devices  56.4 us (27%)
  local copies, waits for them, and re-layouts  50 us (24%)
  starting transfers between devices  45.2 us (22%)
  between operations  20.9 us (10%)
  matrix products  20.1 us (10%)
  other arithmetic  13.4 us (6%)
    all_to_all x2, waiting for transfers between devices, route_faces(): arrived = lax.all_to_all(rows, 'fine', 0, 0, tiled=True)  30.5 us
    all_to_all x1, waiting for transfers between devices, per_device(): rows_in = lax.all_to_all(sent, 'fine', 0, 0, tiled=True)  22.2 us
    ppermute x4, starting transfers between devices, with_halo(): lax.ppermute(lax.slice_in_dim(block, 0, width, axis=dim), axis, backward)  19.8 us
    all_to_all x2, starting transfers between devices, route_faces(): arrived = lax.all_to_all(rows, 'fine', 0, 0, tiled=True)  18.4 us
    dot_general x3, matrix products, reaction(): jnp.einsum('fg,gxyz->fxyz', pick_right, values, precision=lax.Precision.H...  14.4 us
    dynamic_update_slice x2, local copies, waits for them, and re-layouts, per_device(): lax.dynamic_update_slice(coarse_out, jnp.where(slot_filled[slot_number],...  9.66 us
    slice x4, local copies, waits for them, and re-layouts, fine_advance(): above = jnp.where(z_pos == cells_z - 1, high_z, jnp.roll(fine_box, -1, 3))  6.7 us
    dot_general x3, matrix products, reaction(): jnp.einsum('fg,gxyz->fxyz', pick_left, values, precision=lax.Precision.HI...  5.42 us
  transfers between devices with their start and end apart: 11, of which 6 were waited for; matrix products, arithmetic and copies ran while one was open for 14% of the time, Pallas kernels for 0%

profile of v1, /device:TPU:34, one launch (start us, length us, event | category | flops | bytes accessed | tf_op | source)
XLA Modules:
  0.0 206.0 jit_solution(15899225163870362579)
XLA Ops:
  0.6 1.4 copy.288
  2.2 6.5 %collective-permute-start.1 = (f32[9,1,16,128]{3,0,2,1:T(8,128)S(1)}, f32[9,1,16,128]{3,0,2,1:T(8,128)S(1)}, u32[]{:S(2)}, u32[]{:S(2)}) collective-permute-start(f32[9,1,16,128]{3,0,2,1:T(8,128)S(1)} %get-tuple-element.72), channel_id=1, source_target_pairs={{16,0},{32,16},{48,32},{64,48},{80,64},{96,80},{112,96},{128,112},... | collective-permute-start | bytes 221192 | tf_op jit(solution)/shard_map/ppermute | solution.py:20
  9.3 1.7 fusion.60
  10.9 1.6 fusion.61
  14.1 0.7 fusion.49
  14.9 1.9 convolution_multiply_fusion.5
  17.3 0.7 select_reduce_fusion.3
  18.5 1.7 collective-permute-start.2
  20.2 2.6 %collective-permute-start.3 = (f32[9,10,1,128]{3,0,2,1:T(8,128)S(1)}, f32[9,10,1,128]{3,0,2,1:T(8,128)S(1)}, u32[]{:S(2)}, u32[]{:S(2)}) collective-permute-start(f32[9,10,1,128]{3,0,2,1:T(8,128)S(1)} %get-tuple-element.49), channel_id=1, source_target_pairs={{1,0},{2,1},{3,2},{4,3},{5,4},{6,5},{7,6},{8,7},{9,8},{10,9},{11,1... | collective-permute-start | bytes 138248 | tf_op jit(solution)/shard_map/ppermute | solution.py:20
  27.1 1.4 constant_dynamic-slice_fusion.20
  37.6 4.1 %fusion.4 = f32[9,8,16,128]{3,0,2,1:T(8,128)S(1)} fusion(f32[9,8,16,128]{3,0,2,1:T(8,128)} %convolution_multiply_fusion.5, f32[9,8,16,128]{3,0,2,1:T(8,128)S(1)} %copy.288, f32[9,10,1,128]{3,0,2,1:T(8,128)} %copy-done.6, f32[9,10,16,128]{3,0,2,1:T(8,128)S(1)} %constant_dynamic-update-slice_fusion, f32[9,10,1,128]{3,0,2,1:T(8,128)} %copy-done.4, ...), kind=kOutput, calls=%fused_computation.18 | convolution fusion | flops 18432080 | bytes 3926088 | tf_op jit(solution)/shard_map/fg,gxyz->fxyz/dot_general | solution.py:31
  41.8 6.5 %collective-permute-start.5 = (f32[9,1,16,128]{3,0,2,1:T(8,128)S(1)}, f32[9,1,16,128]{3,0,2,1:T(8,128)S(1)}, u32[]{:S(2)}, u32[]{:S(2)}) collective-permute-start(f32[9,1,16,128]{3,0,2,1:T(8,128)S(1)} %get-tuple-element.59), channel_id=1, source_target_pairs={{16,0},{32,16},{48,32},{64,48},{80,64},{96,80},{112,96},{128,112},... | collective-permute-start | bytes 221192 | tf_op jit(solution)/shard_map/ppermute | solution.py:20
  48.6 2.4 %collective-permute-done.4 = f32[9,1,16,128]{3,0,2,1:T(8,128)S(1)} collective-permute-done((f32[9,1,16,128]{3,0,2,1:T(8,128)S(1)}, f32[9,1,16,128]{3,0,2,1:T(8,128)S(1)}, u32[]{:S(2)}, u32[]{:S(2)}) %collective-permute-start.4) | collective-permute-done | bytes 73760 | tf_op jit(solution)/shard_map/ppermute | solution.py:17
  51.1 1.1 collective-permute-done.5
  52.2 4.1 %collective-permute-start.7 = (f32[9,10,1,128]{3,0,2,1:T(8,128)S(1)}, f32[9,10,1,128]{3,0,2,1:T(8,128)S(1)}, u32[]{:S(2)}, u32[]{:S(2)}) collective-permute-start(f32[9,10,1,128]{3,0,2,1:T(8,128)S(1)} %get-tuple-element.47), channel_id=1, source_target_pairs={{1,0},{2,1},{3,2},{4,3},{5,4},{6,5},{7,6},{8,7},{9,8},{10,9},{11,1... | collective-permute-start | bytes 138248 | tf_op jit(solution)/shard_map/ppermute | solution.py:20
  56.5 0.7 dynamic-slice_reduce_fusion.6
  58.9 0.7 dynamic-slice_reduce_fusion.2
  61.4 3.0 %broadcast_select_fusion.1 = (f32[16,1,14400]{2,1,0:T(1,128)}, f32[16,1,14400]{2,1,0:T(1,128)}) fusion(pred[16]{0:T(512)(128)(4,1)S(1)} %copy-done.20, pred[16]{0:T(512)(128)(4,1)S(1)} %copy-done.21, f32[14400]{0:T(1024)S(1)} %broadcast_in_dim.244, f32[14400]{0:T(1024)S(1)} %broadcast_in_dim.242, f32[14400]{0:T(1024)S(1)} %broadcast_in_dim.223, ...), kind=kLoop, calls=%fused_computation.3 | loop fusion | flops 921600 | bytes 2073632 | tf_op jit(solution)/shard_map/jit(_where)/select_n | solution.py:167
  64.4 12.6 %all-to-all-start.1 = ((f32[16,1,14400]{2,1,0:T(1,128)}), f32[16,1,14400]{2,1,0:T(1,128)S(1)}, u32[]{:S(2)}, u32[]{:S(2)}) async-start(f32[16,1,14400]{2,1,0:T(1,128)} %get-tuple-element.86), calls=%async_computation.1 | async-start | bytes 1851392 | tf_op jit(solution)/shard_map/all_to_all | solution.py:172
  81.3 19.7 %all-to-all-done.1 = f32[16,1,14400]{2,1,0:T(1,128)S(1)} async-done(((f32[16,1,14400]{2,1,0:T(1,128)}), f32[16,1,14400]{2,1,0:T(1,128)S(1)}, u32[]{:S(2)}, u32[]{:S(2)}) %all-to-all-start.1) | async-done | bytes 921632 | tf_op jit(solution)/shard_map/all_to_all | solution.py:172
  101.0 5.7 %all-to-all-start = ((f32[16,1,14400]{2,1,0:T(1,128)}), f32[16,1,14400]{2,1,0:T(1,128)}, u32[]{:S(2)}, u32[]{:S(2)}) async-start(f32[16,1,14400]{2,1,0:T(1,128)} %get-tuple-element.87), calls=%async_computation | async-start | bytes 1851392 | tf_op jit(solution)/shard_map/all_to_all | solution.py:172
  106.8 1.2 iota_compare_fusion.7
  110.3 1.9 convolution_multiply_fusion.3
  112.2 1.3 fusion.58
  113.6 1.5 fusion.59
  115.1 1.7 fusion.56
  116.8 1.7 fusion.57
  118.5 1.0 dynamic-slice_reduce_fusion.10
  119.5 10.8 %all-to-all-done = f32[16,1,14400]{2,1,0:T(1,128)} async-done(((f32[16,1,14400]{2,1,0:T(1,128)}), f32[16,1,14400]{2,1,0:T(1,128)}, u32[]{:S(2)}, u32[]{:S(2)}) %all-to-all-start) | async-done | bytes 921632 | tf_op jit(solution)/shard_map/all_to_all | solution.py:172
  130.3 1.0 dynamic-slice_reduce_fusion.11
  134.6 4.9 %fusion.3 = f32[9,16,8,128]{3,0,2,1:T(8,128)S(1)} fusion(f32[9,16,8,128]{3,0,2,1:T(8,128)} %convolution_multiply_fusion.3, f32[9,15,8,128]{3,0,2,1:T(8,128)} %get-tuple-element.67, f32[9,1,8,128]{3,0,2,1:T(8,128)S(1)} %copy.305, f32[9,1,8,128]{3,0,2,1:T(8,128)S(1)} %copy.307, f32[9,15,8,128]{3,0,2,1:T(8,128)} %get-tuple-element.66, ...), kind=kOutput, calls=%fused_computation.15 | convolution fusion | flops 18874448 | bytes 5317960 | tf_op jit(solution)/shard_map/fg,gxyz->fxyz/dot_general | solution.py:31
  139.5 1.7 fusion.51
  141.2 1.7 fusion.52
  142.9 1.5 fusion.54
  144.4 1.4 fusion.53
  145.8 1.6 convolution_multiply_fusion.1
  150.5 5.4 %bitcast_reduce_fusion = (f32[9,8,8,128]{3,0,2,1:T(8,128)}, f32[9,16,8,128]{3,0,2,1:T(8,128)S(1)}) fusion(f32[9,16,8,128]{3,0,2,1:T(8,128)} %convolution_multiply_fusion.1, f32[9,16,8,128]{3,0,2,1:T(8,128)S(1)} %fusion.3, s32[9]{0:T(128)} %copy-done.8, f32[9,16,8,1]{3,0,2,1:T(8,128)} %get-tuple-element.52, f32[9,16,8,127]{3,0,2,1:T(8,128)} %get-tuple-element.50, ...), kind=kOutput, calls=%fused_computation.53 | convolution fusion | flops 18948176 | bytes 5612872 | tf_op jit(solution)/shard_map/fg,gxyz->fxyz/dot_general | solution.py:31
  155.9 1.1 reduce_sum.62
  157.5 1.7 broadcast_select_fusion
  159.2 5.2 %all-to-all-start.2 = ((f32[16,1,18432]{2,1,0:T(1,128)}), f32[16,1,18432]{2,1,0:T(1,128)}, u32[]{:S(2)}, u32[]{:S(2)}) async-start(f32[16,1,18432]{2,1,0:T(1,128)} %broadcast_select_fusion), calls=%async_computation.2 | async-start | bytes 2359296 | tf_op jit(solution)/shard_map/all_to_all | solution.py:198
  168.9 1.0 copy.341
  169.9 22.2 %all-to-all-done.2 = f32[16,1,18432]{2,1,0:T(1,128)} async-done(((f32[16,1,18432]{2,1,0:T(1,128)}), f32[16,1,18432]{2,1,0:T(1,128)}, u32[]{:S(2)}, u32[]{:S(2)}) %all-to-all-start.2) | async-done | bytes 1179680 | tf_op jit(solution)/shard_map/all_to_all | solution.py:198
  192.1 1.3 dynamic-slice_reduce_fusion.8
  193.6 0.8 copy_select_fusion.1
  194.4 4.8 %dynamic_update_slice.6 = f32[9,8,16,128]{3,0,2,1:T(8,128)S(1)} dynamic-update-slice(f32[9,8,16,128]{3,0,2,1:T(8,128)S(1)} %fusion.4, f32[9,8,4,64]{3,0,2,1:T(8,128)S(1)} %copy_select_fusion.1, s32[]{:T(128)} %constant.196.clone.1, s32[]{:T(128)} %constant.196.clone.1, s32[]{:T(128)S(6)} %select_n.279, s32[]{:T(128)S(6)} %select_n.251) | dynamic-update-slice | bytes 147460 | tf_op jit(solution)/shard_map/dynamic_update_slice | solution.py:206
  199.4 0.8 copy_select_fusion
  200.2 4.8 %dynamic_update_slice.7 = f32[9,8,16,128]{3,0,2,1:T(8,128)S(1)} dynamic-update-slice(f32[9,8,16,128]{3,0,2,1:T(8,128)S(1)} %dynamic_update_slice.6, f32[9,8,4,64]{3,0,2,1:T(8,128)S(1)} %copy_select_fusion, s32[]{:T(128)} %constant.196.clone.1, s32[]{:T(128)} %constant.196.clone.1, s32[]{:T(128)S(6)} %select_n.283, s32[]{:T(128)S(6)} %select_n.261) | dynamic-update-slice | bytes 147460 | tf_op jit(solution)/shard_map/dynamic_update_slice | solution.py:206
  205.0 1.0 copy.340
  (215 shorter events, 19.0 us)
Async XLA Ops:
  0.6 8.1 %copy-start.16 = (s32[1,16,2]{1,2,0:T(2,128)S(1)}, s32[1,16,2]{1,2,0:T(2,128)}, u32[]{:S(2)}) copy-start(s32[1,16,2]{1,2,0:T(2,128)} %param.9) | copy-start | bytes 388
  2.1 15.9 %collective-permute-start = (f32[9,1,16,128]{3,0,2,1:T(8,128)S(1)}, f32[9,1,16,128]{3,0,2,1:T(8,128)S(1)}, u32[]{:S(2)}, u32[]{:S(2)}) collective-permute-start(f32[9,1,16,128]{3,0,2,1:T(8,128)S(1)} %get-tuple-element.73), channel_id=1, source_target_pairs={{0,16},{16,32},{32,48},{48,64},{64,80},{80,96},{96,112},{112,128},... | collective-permute-start | bytes 221192 | tf_op jit(solution)/shard_map/ppermute | solution.py:17
  2.2 16.2 %collective-permute-start.1 = (f32[9,1,16,128]{3,0,2,1:T(8,128)S(1)}, f32[9,1,16,128]{3,0,2,1:T(8,128)S(1)}, u32[]{:S(2)}, u32[]{:S(2)}) collective-permute-start(f32[9,1,16,128]{3,0,2,1:T(8,128)S(1)} %get-tuple-element.72), channel_id=1, source_target_pairs={{16,0},{32,16},{48,32},{64,48},{80,64},{96,80},{112,96},{128,112},... | collective-permute-start | bytes 221192 | tf_op jit(solution)/shard_map/ppermute | solution.py:20
  10.9 1.7 copy-start.12
  10.9 3.9 %copy-start.22 = (s32[9,2]{0,1:T(2,128)S(1)}, s32[9,2]{0,1:T(2,128)}, u32[]{:S(2)}) copy-start(s32[9,2]{0,1:T(2,128)} %param.11) | copy-start | bytes 220
  10.9 3.9 %copy-start.14 = (f32[9]{0:T(128)S(1)}, f32[9]{0:T(128)}, u32[]{:S(2)}) copy-start(f32[9]{0:T(128)} %param.13) | copy-start | bytes 112
  12.6 2.3 %copy-start.1 = (f32[9,8,16,128]{3,2,1,0:T(8,128)S(1)}, f32[9,8,16,128]{3,2,1,0:T(8,128)}, u32[]{:S(2)}) copy-start(f32[9,8,16,128]{3,2,1,0:T(8,128)} %param.7) | copy-start | bytes 1769476
  12.8 0.7 copy-start.28
  14.9 22.7 %copy-start.8 = (s32[9]{0:T(128)}, s32[9]{0:T(128)S(1)}, u32[]{:S(2)}) copy-start(s32[9]{0:T(128)S(1)} %get-tuple-element.93) | copy-start | bytes 112
  14.9 95.4 %copy-start.10 = (s32[9]{0:T(128)}, s32[9]{0:T(128)S(1)}, u32[]{:S(2)}) copy-start(s32[9]{0:T(128)S(1)} %get-tuple-element.94) | copy-start | bytes 112
  18.4 18.5 %copy-start.3 = (f32[9,1,16,128]{3,0,2,1:T(8,128)}, f32[9,1,16,128]{3,0,2,1:T(8,128)S(1)}, u32[]{:S(2)}) copy-start(f32[9,1,16,128]{3,0,2,1:T(8,128)S(1)} %collective-permute-done.1) | copy-start | bytes 221188
  18.5 18.4 %collective-permute-start.2 = (f32[9,10,1,128]{3,0,2,1:T(8,128)S(1)}, f32[9,10,1,128]{3,0,2,1:T(8,128)S(1)}, u32[]{:S(2)}, u32[]{:S(2)}) collective-permute-start(f32[9,10,1,128]{3,0,2,1:T(8,128)S(1)} %get-tuple-element.48), channel_id=1, source_target_pairs={{0,1},{1,2},{2,3},{3,4},{4,5},{5,6},{6,7},{7,8},{8,9},{9,10},{10,1... | collective-permute-start | bytes 138248 | tf_op jit(solution)/shard_map/ppermute | solution.py:17
  20.2 16.8 %collective-permute-start.3 = (f32[9,10,1,128]{3,0,2,1:T(8,128)S(1)}, f32[9,10,1,128]{3,0,2,1:T(8,128)S(1)}, u32[]{:S(2)}, u32[]{:S(2)}) collective-permute-start(f32[9,10,1,128]{3,0,2,1:T(8,128)S(1)} %get-tuple-element.49), channel_id=1, source_target_pairs={{1,0},{2,1},{3,2},{4,3},{5,4},{6,5},{7,6},{8,7},{9,8},{10,9},{11,1... | collective-permute-start | bytes 138248 | tf_op jit(solution)/shard_map/ppermute | solution.py:20
  36.9 0.6 copy-start.4
  36.9 0.6 copy-start.6
  37.6 10.8 %copy-start.5 = (f32[9,10,1,128]{3,0,2,1:T(8,128)S(1)}, f32[9,10,1,128]{3,0,2,1:T(8,128)}, u32[]{:S(2)}) copy-start(f32[9,10,1,128]{3,0,2,1:T(8,128)} %copy-done.4) | copy-start | bytes 138244
  37.6 10.8 %copy-start.7 = (f32[9,10,1,128]{3,0,2,1:T(8,128)S(1)}, f32[9,10,1,128]{3,0,2,1:T(8,128)}, u32[]{:S(2)}) copy-start(f32[9,10,1,128]{3,0,2,1:T(8,128)} %copy-done.6) | copy-start | bytes 138244
  41.7 9.4 %collective-permute-start.4 = (f32[9,1,16,128]{3,0,2,1:T(8,128)S(1)}, f32[9,1,16,128]{3,0,2,1:T(8,128)S(1)}, u32[]{:S(2)}, u32[]{:S(2)}) collective-permute-start(f32[9,1,16,128]{3,0,2,1:T(8,128)S(1)} %get-tuple-element.58), channel_id=1, source_target_pairs={{0,16},{16,32},{32,48},{48,64},{64,80},{80,96},{96,112},{112,128},... | collective-permute-start | bytes 221192 | tf_op jit(solution)/shard_map/ppermute | solution.py:17
  41.8 10.3 %collective-permute-start.5 = (f32[9,1,16,128]{3,0,2,1:T(8,128)S(1)}, f32[9,1,16,128]{3,0,2,1:T(8,128)S(1)}, u32[]{:S(2)}, u32[]{:S(2)}) collective-permute-start(f32[9,1,16,128]{3,0,2,1:T(8,128)S(1)} %get-tuple-element.59), channel_id=1, source_target_pairs={{16,0},{32,16},{48,32},{64,48},{80,64},{96,80},{112,96},{128,112},... | collective-permute-start | bytes 221192 | tf_op jit(solution)/shard_map/ppermute | solution.py:20
  52.1 6.6 %collective-permute-start.6 = (f32[9,10,1,128]{3,0,2,1:T(8,128)S(1)}, f32[9,10,1,128]{3,0,2,1:T(8,128)S(1)}, u32[]{:S(2)}, u32[]{:S(2)}) collective-permute-start(f32[9,10,1,128]{3,0,2,1:T(8,128)S(1)} %get-tuple-element.46), channel_id=1, source_target_pairs={{0,1},{1,2},{2,3},{3,4},{4,5},{5,6},{6,7},{7,8},{8,9},{9,10},{10,1... | collective-permute-start | bytes 138248 | tf_op jit(solution)/shard_map/ppermute | solution.py:17
  52.2 6.5 %collective-permute-start.7 = (f32[9,10,1,128]{3,0,2,1:T(8,128)S(1)}, f32[9,10,1,128]{3,0,2,1:T(8,128)S(1)}, u32[]{:S(2)}, u32[]{:S(2)}) collective-permute-start(f32[9,10,1,128]{3,0,2,1:T(8,128)S(1)} %get-tuple-element.47), channel_id=1, source_target_pairs={{1,0},{2,1},{3,2},{4,3},{5,4},{6,5},{7,6},{8,7},{9,8},{10,9},{11,1... | collective-permute-start | bytes 138248 | tf_op jit(solution)/shard_map/ppermute | solution.py:20
  59.6 1.7 copy-start.20
  59.6 1.7 copy-start.21
  61.4 15.7 %copy-start.29 = (s32[16]{0:T(128)S(1)}, s32[16]{0:T(128)}, u32[]{:S(2)}) copy-start(s32[16]{0:T(128)} %copy-done.28) | copy-start | bytes 196
  64.4 44.8 %copy-start = (f32[1,1,9,16,8,128]{5,4,3,2,1,0:T(8,128)S(1)}, f32[1,1,9,16,8,128]{5,4,3,2,1,0:T(8,128)}, u32[]{:S(2)}) copy-start(f32[1,1,9,16,8,128]{5,4,3,2,1,0:T(8,128)} %param.8) | copy-start | bytes 1769476
  64.4 36.6 %all-to-all-start.1 = ((f32[16,1,14400]{2,1,0:T(1,128)}), f32[16,1,14400]{2,1,0:T(1,128)S(1)}, u32[]{:S(2)}, u32[]{:S(2)}) async-start(f32[16,1,14400]{2,1,0:T(1,128)} %get-tuple-element.86), calls=%async_computation.1 | async-start | bytes 1851392 | tf_op jit(solution)/shard_map/all_to_all | solution.py:172
  80.2 54.4 %copy-start.17 = (pred[128]{0:T(512)(128)(4,1)}, pred[128]{0:T(512)(128)(4,1)S(1)}, u32[]{:S(2)}) copy-start(pred[128]{0:T(512)(128)(4,1)S(1)} %iota_compare_fusion.5) | copy-start | bytes 388
  80.7 53.9 %copy-start.18 = (pred[128]{0:T(512)(128)(4,1)}, pred[128]{0:T(512)(128)(4,1)S(1)}, u32[]{:S(2)}) copy-start(pred[128]{0:T(512)(128)(4,1)S(1)} %get-tuple-element.106) | copy-start | bytes 388
  101.0 7.6 %copy-start.2 = (f32[16,1,14400]{2,1,0:T(1,128)}, f32[16,1,14400]{2,1,0:T(1,128)S(1)}, u32[]{:S(2)}) copy-start(f32[16,1,14400]{2,1,0:T(1,128)S(1)} %all-to-all-done.1) | copy-start | bytes 2764804
  101.0 9.2 %copy-start.23 = (f32[9]{0:T(128)S(1)}, f32[9]{0:T(128)}, u32[]{:S(2)}) copy-start(f32[9]{0:T(128)} %param.12) | copy-start | bytes 112
  101.0 9.3 %copy-start.15 = (f32[9]{0:T(128)S(1)}, f32[9]{0:T(128)}, u32[]{:S(2)}) copy-start(f32[9]{0:T(128)} %param.13) | copy-start | bytes 112
  101.0 29.3 %all-to-all-start = ((f32[16,1,14400]{2,1,0:T(1,128)}), f32[16,1,14400]{2,1,0:T(1,128)}, u32[]{:S(2)}, u32[]{:S(2)}) async-start(f32[16,1,14400]{2,1,0:T(1,128)} %get-tuple-element.87), calls=%async_computation | async-start | bytes 1851392 | tf_op jit(solution)/shard_map/all_to_all | solution.py:172
  110.3 24.3 %copy-start.19 = (f32[9]{0:T(128)}, f32[9]{0:T(128)S(1)}, u32[]{:S(2)}) copy-start(f32[9]{0:T(128)S(1)} %broadcast_multiply_fusion) | copy-start | bytes 112
  133.5 1.1 copy-start.9
  144.4 1.4 copy-start.11
  150.4 6.6 %copy-start.24 = (pred[128]{0:T(512)(128)(4,1)S(1)}, pred[128]{0:T(512)(128)(4,1)}, u32[]{:S(2)}) copy-start(pred[128]{0:T(512)(128)(4,1)} %get-tuple-element.105) | copy-start | bytes 388
  150.5 6.6 %copy-start.25 = (s32[128]{0:T(128)S(1)}, s32[128]{0:T(128)}, u32[]{:S(2)}) copy-start(s32[128]{0:T(128)} %get-tuple-element.107) | copy-start | bytes 1540
  150.5 6.6 %copy-start.26 = (s32[128]{0:T(128)S(1)}, s32[128]{0:T(128)}, u32[]{:S(2)}) copy-start(s32[128]{0:T(128)} %get-tuple-element.108) | copy-start | bytes 1540
  155.9 1.6 copy-start.27
  159.2 5.2 %copy-start.13 = (s32[1,16]{1,0:T(1,128)S(1)}, s32[1,16]{1,0:T(1,128)}, u32[]{:S(2)}) copy-start(s32[1,16]{1,0:T(1,128)} %param.10) | copy-start | bytes 196
  159.2 32.9 %all-to-all-start.2 = ((f32[16,1,18432]{2,1,0:T(1,128)}), f32[16,1,18432]{2,1,0:T(1,128)}, u32[]{:S(2)}, u32[]{:S(2)}) async-start(f32[16,1,18432]{2,1,0:T(1,128)} %broadcast_select_fusion), calls=%async_computation.2 | async-start | bytes 2359296 | tf_op jit(solution)/shard_map/all_to_all | solution.py:198

commit v2 on v1

--- a/solution.py
+++ b/solution.py
@@ -8,18 +8,25 @@
 BZ = 64
 
 
-def with_halo(block, sides, width):
-    for axis, dim in sides:
-        count = lax.axis_size(axis)
-        forward = [(i, i + 1) for i in range(count - 1)]
-        forward.append((count - 1, 0))
-        backward = [(target, source) for source, target in forward]
-        low = lax.ppermute(
-            lax.slice_in_dim(block, block.shape[dim] - width, None, axis=dim), axis, forward
-        )
-        high = lax.ppermute(lax.slice_in_dim(block, 0, width, axis=dim), axis, backward)
-        block = jnp.concatenate([low, block, high], axis=dim)
-    return block
+def ring_pairs(axis):
+    count = lax.axis_size(axis)
+    forward = [(i, (i + 1) % count) for i in range(count)]
+    backward = [(target, source) for source, target in forward]
+    return forward, backward
+
+
+def with_halo(block):
+    x_forward, x_backward = ring_pairs("base")
+    y_forward, y_backward = ring_pairs("fine")
+    low_x = lax.ppermute(block[:, -1:], "base", x_forward)
+    high_x = lax.ppermute(block[:, :1], "base", x_backward)
+    low_y = lax.ppermute(block[:, :, -1:], "fine", y_forward)
+    high_y = lax.ppermute(block[:, :, :1], "fine", y_backward)
+    corner = jnp.zeros_like(block[:, :1, :1])
+    low_y = jnp.concatenate([corner, low_y, corner], axis=1)
+    high_y = jnp.concatenate([corner, high_y, corner], axis=1)
+    block = jnp.concatenate([low_x, block, high_x], axis=1)
+    return jnp.concatenate([low_y, block, high_y], axis=2)
 
 
 def reaction(values, reaction_rates, left_ids, right_ids):
@@ -131,9 +138,6 @@
     left_ids = reaction_table[:, 0]
     right_ids = reaction_table[:, 1]
 
-    def extend(coarse_state):
-        return with_halo(coarse_state, (("base", 1), ("fine", 2)), 1)
-
     corners = box_list[0]
     owners = patch_owner[0]
     y_cell = corners[:, 0]
@@ -157,24 +161,11 @@
     dest_slot = slot_rank[box_of_dest]
     source_of_mine = y_block[holder[my_index]]
 
-    def route_faces(extended):
-        slots = []
-        for slot_number in range(MOST):
-            patch_id = slot_patch[slot_number]
-            slots.append(
-                packed_faces(extended, y_cell[patch_id] - my_index * height, z_cell[patch_id])
-            )
-        rows = jnp.where(
-            (dest_here & (dest_slot == 0))[:, None],
-            slots[0].reshape(1, -1),
-            jnp.where(dest_here[:, None], slots[1].reshape(1, -1), 0.0),
-        )
-        arrived = lax.all_to_all(rows, "fine", 0, 0, tiled=True)
-        chosen = lax.dynamic_index_in_dim(arrived, source_of_mine, 0, keepdims=False)
-        return chosen.reshape(slots[0].shape)
-
-    old_ext = extend(coarse_level)
-    old_shell = route_faces(old_ext)
+    def slot_faces(extended, slot_number):
+        patch_id = slot_patch[slot_number]
+        return packed_faces(extended, y_cell[patch_id] - my_index * height, z_cell[patch_id])
+
+    old_ext = with_halo(coarse_level)
     centre = old_ext[:, 1:-1, 1:-1, :]
     neighbours = (
         old_ext[:, :-2, 1:-1, :]
@@ -183,8 +174,21 @@
         + (jnp.roll(centre, 1, 3) + jnp.roll(centre, -1, 3))
     )
     coarse_next = coarse_advance(centre, neighbours, viscosity, reaction_rates, left_ids, right_ids)
-    new_ext = extend(coarse_next)
-    new_shell = route_faces(new_ext)
+    new_ext = with_halo(coarse_next)
+    slots = [
+        jnp.stack([slot_faces(old_ext, slot_number), slot_faces(new_ext, slot_number)])
+        for slot_number in range(MOST)
+    ]
+    rows = jnp.where(
+        (dest_here & (dest_slot == 0))[:, None],
+        slots[0].reshape(1, -1),
+        jnp.where(dest_here[:, None], slots[1].reshape(1, -1), 0.0),
+    )
+    arrived = lax.all_to_all(rows, "fine", 0, 0, tiled=True)
+    shell_pair = lax.dynamic_index_in_dim(arrived, source_of_mine, 0, keepdims=False)
+    shell_pair = shell_pair.reshape(slots[0].shape)
+    old_shell = shell_pair[0]
+    new_shell = shell_pair[1]
 
     fine_box = fine_level[0, 0]
     old_faces = unpack_faces(old_shell, cells_x)

time: 207 us -> 185 us (0.89)
  starting transfers between devices: 45.2 us -> 36.6 us
  waiting for transfers between devices: 56.4 us -> 48.4 us
  matrix products: 20.1 us -> 17.2 us
    all_to_all x2 -> x1, starting transfers between devices: 18.4 us -> 9.15 us  [per_device(): arrived = lax.all_to_all(rows, 'fine', 0, 0, tiled=True)]
    all_to_all x2 -> x1, waiting for transfers between devices: 30.5 us -> 26.4 us  [per_device(): arrived = lax.all_to_all(rows, 'fine', 0, 0, tiled=True)]
    ppermute x8, waiting for transfers between devices: 3.69 us -> 0.02 us  [the longest x2 0.01 us: with_halo(): low_x = lax.ppermute(block[:, -1:], 'base', x_forward)]
    unnamed x66 -> x50, local copies, waits for them, and re-layouts: 4.91 us -> 4.86 us
  transfers between devices with their start and end apart: 11 -> 10, of which waited for: 6 -> 2; matrix products, arithmetic and copies ran while one was open for 14% -> 13% of each run, Pallas kernels for 0% -> 0%
where the time goes in v2:
time: 185 us; the launch traced here: 184 us
  local copies, waits for them, and re-layouts  49.7 us (27%)
  waiting for transfers between devices  48.4 us (26%)
  starting transfers between devices  36.6 us (20%)
  between operations  20.6 us (11%)
  matrix products  17.2 us (9%)
  other arithmetic  11.7 us (6%)
    all_to_all x1, waiting for transfers between devices, per_device(): arrived = lax.all_to_all(rows, 'fine', 0, 0, tiled=True)  26.4 us
    all_to_all x1, waiting for transfers between devices, per_device(): rows_in = lax.all_to_all(sent, 'fine', 0, 0, tiled=True)  22.1 us
    ppermute x2, starting transfers between devices, with_halo(): high_x = lax.ppermute(block[:, :1], 'base', x_backward)  13.1 us
    dot_general x3, matrix products, reaction(): jnp.einsum('fg,gxyz->fxyz', pick_right, values, precision=lax.Precision.H...  12.6 us
    dynamic_update_slice x2, local copies, waits for them, and re-layouts, per_device(): lax.dynamic_update_slice(coarse_out, jnp.where(slot_filled[slot_number],...  9.66 us
    all_to_all x1, starting transfers between devices, per_device(): arrived = lax.all_to_all(rows, 'fine', 0, 0, tiled=True)  9.15 us
    slice x4, local copies, waits for them, and re-layouts, fine_advance(): above = jnp.where(z_pos == cells_z - 1, high_z, jnp.roll(fine_box, -1, 3))  6.76 us
    ppermute x2, starting transfers between devices, with_halo(): high_y = lax.ppermute(block[:, :, :1], 'fine', y_backward)  6.69 us
  transfers between devices with their start and end apart: 10, of which 2 were waited for; matrix products, arithmetic and copies ran while one was open for 13% of the time, Pallas kernels for 0%

profile of v2, /device:TPU:34, one launch (start us, length us, event | category | flops | bytes accessed | tf_op | source)
XLA Modules:
  0.0 184.3 jit_solution(9616335581314718545)
XLA Ops:
  0.6 1.4 copy.433
  2.2 6.5 %collective-permute-start.1 = (f32[9,1,16,128]{3,0,2,1:T(8,128)S(1)}, f32[9,1,16,128]{3,0,2,1:T(8,128)S(1)}, u32[]{:S(2)}, u32[]{:S(2)}) collective-permute-start(f32[9,1,16,128]{3,0,2,1:T(8,128)S(1)} %get-tuple-element.78), channel_id=1, source_target_pairs={{16,0},{32,16},{48,32},{64,48},{80,64},{96,80},{112,96},{128,112},... | collective-permute-start | bytes 221192 | tf_op jit(solution)/shard_map/ppermute | solution.py:22
  8.7 0.7 fusion.66
  9.4 1.6 collective-permute-start.2
  11.0 2.6 %collective-permute-start.3 = (f32[9,8,1,128]{3,0,2,1:T(8,128)}, f32[9,8,1,128]{3,0,2,1:T(8,128)}, u32[]{:S(2)}, u32[]{:S(2)}) collective-permute-start(f32[9,8,1,128]{3,0,2,1:T(8,128)} %get-tuple-element.77), channel_id=1, source_target_pairs={{1,0},{2,1},{3,2},{4,3},{5,4},{6,5},{7,6},{8,7},{9,8},{10,9},{11,1... | collective-permute-start | bytes 110600 | tf_op jit(solution)/shard_map/ppermute | solution.py:24
  14.1 1.7 fusion.64
  15.8 1.7 fusion.65
  17.7 0.7 gather_fusion
  18.4 0.7 gather_fusion.1
  19.0 0.7 fusion.53
  19.8 0.9 convolution_multiply_fusion.5
  21.3 0.6 select_reduce_fusion.3
  22.4 0.6 copy-done.7
  23.0 2.3 %fusion.8 = f32[9,8,16,128]{3,0,2,1:T(8,128)S(1)} fusion(f32[9,8,16,128]{3,0,2,1:T(8,128)S(1)} %convolution_multiply_fusion.5, f32[9,8,16,128]{3,0,2,1:T(8,128)S(1)} %copy.433, f32[9,10,16,128]{3,0,2,1:T(8,128)S(1)} %constant_dynamic-update-slice_fusion, f32[9,1,1,128]{3,0,2,1:T(8,128)S(1)} %broadcast.243, f32[9,8,1,128]{3,0,2,1:T(8,128)} %collective-permute-done.3, ...), kind=kOutput, calls=%fused_computation.26 | convolution fusion | flops 19021904 | bytes 3912264 | tf_op jit(solution)/shard_map/fg,gxyz->fxyz/dot_general | solution.py:38
  25.5 6.5 %collective-permute-start.6 = (f32[9,1,16,128]{3,0,2,1:T(8,128)S(1)}, f32[9,1,16,128]{3,0,2,1:T(8,128)S(1)}, u32[]{:S(2)}, u32[]{:S(2)}) collective-permute-start(f32[9,1,16,128]{3,0,2,1:T(8,128)S(1)} %get-tuple-element.71), channel_id=1, source_target_pairs={{16,0},{32,16},{48,32},{64,48},{80,64},{96,80},{112,96},{128,112},... | collective-permute-start | bytes 221192 | tf_op jit(solution)/shard_map/ppermute | solution.py:22
  32.0 4.1 %collective-permute-start.7 = (f32[9,8,1,128]{3,0,2,1:T(8,128)S(1)}, f32[9,8,1,128]{3,0,2,1:T(8,128)S(1)}, u32[]{:S(2)}, u32[]{:S(2)}) collective-permute-start(f32[9,8,1,128]{3,0,2,1:T(8,128)S(1)} %get-tuple-element.69), channel_id=1, source_target_pairs={{1,0},{2,1},{3,2},{4,3},{5,4},{6,5},{7,6},{8,7},{9,8},{10,9},{11,1... | collective-permute-start | bytes 110600 | tf_op jit(solution)/shard_map/ppermute | solution.py:24
  36.2 0.6 select_reduce_fusion.2
  40.4 1.4 constant_dynamic-slice_fusion.20
  44.4 1.3 constant_dynamic-slice_fusion.21
  50.8 1.1 fusion.1
  51.9 0.7 dynamic-slice_reduce_fusion.6
  52.7 0.7 dynamic-slice_reduce_fusion.4
  56.7 3.3 %broadcast_select_fusion = f32[16,1,28800]{2,1,0:T(1,128)} fusion(pred[16]{0:T(512)(128)(4,1)S(1)} %copy-done.15, pred[16]{0:T(512)(128)(4,1)S(1)} %copy-done.16, f32[28800]{0:T(1024)S(1)} %broadcast_in_dim.200, f32[28800]{0:T(1024)S(1)} %broadcast_in_dim.197), kind=kLoop, calls=%fused_computation.2 | loop fusion | flops 921600 | bytes 2073632 | tf_op jit(solution)/shard_map/jit(_where)/select_n | solution.py:182
  60.0 9.2 %all-to-all-start = ((f32[16,1,28800]{2,1,0:T(1,128)}), f32[16,1,28800]{2,1,0:T(1,128)}, u32[]{:S(2)}, u32[]{:S(2)}) async-start(f32[16,1,28800]{2,1,0:T(1,128)} %broadcast_select_fusion), calls=%async_computation | async-start | bytes 3686400 | tf_op jit(solution)/shard_map/all_to_all | solution.py:187
  74.7 0.7 iota_compare_fusion.7
  75.4 1.9 %convolution_multiply_fusion.3 = f32[9,16,8,128]{3,0,2,1:T(8,128)} fusion(f32[9]{0:T(128)S(1)} %copy-done.13, f32[1,1,9,16,8,128]{5,4,3,2,1,0:T(8,128)S(1)} %copy-done, s32[9]{0:T(128)S(1)} %get-tuple-element.100), kind=kOutput, calls=%fused_computation.24 | convolution fusion | flops 16072785 | bytes 1179720 | tf_op jit(solution)/shard_map/fg,gxyz->fxyz/dot_general | solution.py:37
  77.3 1.4 fusion.60
  78.7 1.5 fusion.61
  80.2 1.7 fusion.58
  81.9 1.7 fusion.59
  83.6 26.4 %all-to-all-done = f32[16,1,28800]{2,1,0:T(1,128)} async-done(((f32[16,1,28800]{2,1,0:T(1,128)}), f32[16,1,28800]{2,1,0:T(1,128)}, u32[]{:S(2)}, u32[]{:S(2)}) %all-to-all-start) | async-done | bytes 1843232 | tf_op jit(solution)/shard_map/all_to_all | solution.py:187
  110.0 0.9 dynamic-slice_bitcast_fusion
  114.6 4.9 %fusion.7 = f32[9,16,8,128]{3,0,2,1:T(8,128)S(1)} fusion(f32[9,16,8,128]{3,0,2,1:T(8,128)} %convolution_multiply_fusion.3, f32[9,15,8,128]{3,0,2,1:T(8,128)} %get-tuple-element.67, f32[9,1,8,128]{3,0,2,1:T(8,128)S(1)} %copy.462, f32[9,1,8,128]{3,0,2,1:T(8,128)S(1)} %copy.464, f32[9,15,8,128]{3,0,2,1:T(8,128)} %get-tuple-element.66, ...), kind=kOutput, calls=%fused_computation.23 | convolution fusion | flops 18874448 | bytes 5317960 | tf_op jit(solution)/shard_map/fg,gxyz->fxyz/dot_general | solution.py:38
  119.5 1.7 fusion.54
  121.2 1.7 fusion.55
  122.9 1.5 fusion.57
  124.4 1.4 fusion.56
  125.8 1.6 convolution_multiply_fusion.1
  130.5 5.3 %bitcast_reduce_fusion = (f32[9,8,8,128]{3,0,2,1:T(8,128)S(1)}, f32[9,16,8,128]{3,0,2,1:T(8,128)}) fusion(f32[9,16,8,128]{3,0,2,1:T(8,128)} %convolution_multiply_fusion.1, f32[9,16,8,128]{3,0,2,1:T(8,128)S(1)} %fusion.7, s32[9]{0:T(128)S(1)} %copy-done.9, f32[9,16,8,1]{3,0,2,1:T(8,128)} %get-tuple-element.54, f32[9,16,8,127]{3,0,2,1:T(8,128)} %get-tuple-element.52, ...), kind=kOutput, calls=%fused_computation.65 | convolution fusion | flops 18948176 | bytes 5612872 | tf_op jit(solution)/shard_map/fg,gxyz->fxyz/dot_general | solution.py:38
  136.3 1.7 broadcast_select_fusion.2
  138.0 6.0 %all-to-all-start.1 = ((f32[16,1,18432]{2,1,0:T(1,128)}), f32[16,1,18432]{2,1,0:T(1,128)S(1)}, u32[]{:S(2)}, u32[]{:S(2)}) async-start(f32[16,1,18432]{2,1,0:T(1,128)} %broadcast_select_fusion.2), calls=%async_computation.1 | async-start | bytes 2359296 | tf_op jit(solution)/shard_map/all_to_all | solution.py:202
  148.5 1.0 copy.486
  149.5 22.1 %all-to-all-done.1 = f32[16,1,18432]{2,1,0:T(1,128)S(1)} async-done(((f32[16,1,18432]{2,1,0:T(1,128)}), f32[16,1,18432]{2,1,0:T(1,128)S(1)}, u32[]{:S(2)}, u32[]{:S(2)}) %all-to-all-start.1) | async-done | bytes 1179680 | tf_op jit(solution)/shard_map/all_to_all | solution.py:202
  172.1 0.7 copy_select_fusion.1
  172.8 4.8 %dynamic_update_slice.6 = f32[9,8,16,128]{3,0,2,1:T(8,128)S(1)} dynamic-update-slice(f32[9,8,16,128]{3,0,2,1:T(8,128)S(1)} %fusion.8, f32[9,8,4,64]{3,0,2,1:T(8,128)S(1)} %copy_select_fusion.1, s32[]{:T(128)} %constant.195.clone.1, s32[]{:T(128)} %constant.195.clone.1, s32[]{:T(128)S(6)} %select_n.256, s32[]{:T(128)S(6)} %select_n.230) | dynamic-update-slice | bytes 147460 | tf_op jit(solution)/shard_map/dynamic_update_slice | solution.py:210
  177.8 0.7 copy_select_fusion
  178.5 4.8 %dynamic_update_slice.7 = f32[9,8,16,128]{3,0,2,1:T(8,128)S(1)} dynamic-update-slice(f32[9,8,16,128]{3,0,2,1:T(8,128)S(1)} %dynamic_update_slice.6, f32[9,8,4,64]{3,0,2,1:T(8,128)S(1)} %copy_select_fusion, s32[]{:T(128)} %constant.195.clone.1, s32[]{:T(128)} %constant.195.clone.1, s32[]{:T(128)S(6)} %select_n.260, s32[]{:T(128)S(6)} %select_n.240) | dynamic-update-slice | bytes 147460 | tf_op jit(solution)/shard_map/dynamic_update_slice | solution.py:210
  183.3 1.0 copy.485
  (197 shorter events, 14.9 us)
Async XLA Ops:
  0.6 12.9 %copy-start.14 = (s32[1,16,2]{1,2,0:T(2,128)S(1)}, s32[1,16,2]{1,2,0:T(2,128)}, u32[]{:S(2)}) copy-start(s32[1,16,2]{1,2,0:T(2,128)} %param.9) | copy-start | bytes 388
  2.1 19.8 %collective-permute-start = (f32[9,1,16,128]{3,0,2,1:T(8,128)S(1)}, f32[9,1,16,128]{3,0,2,1:T(8,128)S(1)}, u32[]{:S(2)}, u32[]{:S(2)}) collective-permute-start(f32[9,1,16,128]{3,0,2,1:T(8,128)S(1)} %get-tuple-element.79), channel_id=1, source_target_pairs={{0,16},{16,32},{32,48},{48,64},{64,80},{80,96},{96,112},{112,128},... | collective-permute-start | bytes 221192 | tf_op jit(solution)/shard_map/ppermute | solution.py:21
  2.2 20.1 %collective-permute-start.1 = (f32[9,1,16,128]{3,0,2,1:T(8,128)S(1)}, f32[9,1,16,128]{3,0,2,1:T(8,128)S(1)}, u32[]{:S(2)}, u32[]{:S(2)}) collective-permute-start(f32[9,1,16,128]{3,0,2,1:T(8,128)S(1)} %get-tuple-element.78), channel_id=1, source_target_pairs={{16,0},{32,16},{48,32},{64,48},{80,64},{96,80},{112,96},{128,112},... | collective-permute-start | bytes 221192 | tf_op jit(solution)/shard_map/ppermute | solution.py:22
  9.4 12.9 %collective-permute-start.2 = (f32[9,8,1,128]{3,0,2,1:T(8,128)}, f32[9,8,1,128]{3,0,2,1:T(8,128)}, u32[]{:S(2)}, u32[]{:S(2)}) collective-permute-start(f32[9,8,1,128]{3,0,2,1:T(8,128)} %get-tuple-element.76), channel_id=1, source_target_pairs={{0,1},{1,2},{2,3},{3,4},{4,5},{5,6},{6,7},{7,8},{8,9},{9,10},{10,1... | collective-permute-start | bytes 110600 | tf_op jit(solution)/shard_map/ppermute | solution.py:23
  11.0 11.4 %collective-permute-start.3 = (f32[9,8,1,128]{3,0,2,1:T(8,128)}, f32[9,8,1,128]{3,0,2,1:T(8,128)}, u32[]{:S(2)}, u32[]{:S(2)}) collective-permute-start(f32[9,8,1,128]{3,0,2,1:T(8,128)} %get-tuple-element.77), channel_id=1, source_target_pairs={{1,0},{2,1},{3,2},{4,3},{5,4},{6,5},{7,6},{8,7},{9,8},{10,9},{11,1... | collective-permute-start | bytes 110600 | tf_op jit(solution)/shard_map/ppermute | solution.py:24
  15.8 1.7 copy-start.10
  15.8 3.9 %copy-start.17 = (s32[9,2]{0,1:T(2,128)S(1)}, s32[9,2]{0,1:T(2,128)}, u32[]{:S(2)}) copy-start(s32[9,2]{0,1:T(2,128)} %param.11) | copy-start | bytes 220
  15.8 3.9 %copy-start.12 = (f32[9]{0:T(128)S(1)}, f32[9]{0:T(128)}, u32[]{:S(2)}) copy-start(f32[9]{0:T(128)} %param.13) | copy-start | bytes 112
  17.5 2.2 %copy-start.1 = (f32[9,8,16,128]{3,2,1,0:T(8,128)S(1)}, f32[9,8,16,128]{3,2,1,0:T(8,128)}, u32[]{:S(2)}) copy-start(f32[9,8,16,128]{3,2,1,0:T(8,128)} %param.7) | copy-start | bytes 1769476
  17.7 3.0 %copy-start.18 = (s32[16]{0:T(128)}, s32[16]{0:T(128)S(1)}, u32[]{:S(2)}) copy-start(s32[16]{0:T(128)S(1)} %get-tuple-element.109) | copy-start | bytes 196
  19.7 3.2 %copy-start.8 = (s32[9]{0:T(128)}, s32[9]{0:T(128)S(1)}, u32[]{:S(2)}) copy-start(s32[9]{0:T(128)S(1)} %get-tuple-element.99) | copy-start | bytes 112
  19.7 3.2 %copy-start.5 = (f32[9,8,16,1]{3,0,2,1:T(8,128)S(1)}, f32[9,8,16,1]{3,0,2,1:T(8,128)}, u32[]{:S(2)}) copy-start(f32[9,8,16,1]{3,0,2,1:T(8,128)} %get-tuple-element.74) | copy-start | bytes 13828
  19.7 3.2 %copy-start.6 = (f32[9,8,16,1]{3,0,2,1:T(8,128)S(1)}, f32[9,8,16,1]{3,0,2,1:T(8,128)}, u32[]{:S(2)}) copy-start(f32[9,8,16,1]{3,0,2,1:T(8,128)} %get-tuple-element.75) | copy-start | bytes 13828
  20.7 2.3 %copy-start.3 = (f32[9,8,16,127]{3,0,2,1:T(8,128)S(1)}, f32[9,8,16,127]{3,0,2,1:T(8,128)}, u32[]{:S(2)}) copy-start(f32[9,8,16,127]{3,0,2,1:T(8,128)} %get-tuple-element.72) | copy-start | bytes 1755652
  20.7 2.3 %copy-start.4 = (f32[9,8,16,127]{3,0,2,1:T(8,128)S(1)}, f32[9,8,16,127]{3,0,2,1:T(8,128)}, u32[]{:S(2)}) copy-start(f32[9,8,16,127]{3,0,2,1:T(8,128)} %get-tuple-element.73) | copy-start | bytes 1755652
  20.7 2.3 %copy-start.20 = (f32[9]{0:T(128)S(1)}, f32[9]{0:T(128)}, u32[]{:S(2)}) copy-start(f32[9]{0:T(128)} %param.12) | copy-start | bytes 112
  22.3 0.7 copy-start.7
  25.4 25.4 %collective-permute-start.5 = (f32[9,1,16,128]{3,0,2,1:T(8,128)S(1)}, f32[9,1,16,128]{3,0,2,1:T(8,128)S(1)}, u32[]{:S(2)}, u32[]{:S(2)}) collective-permute-start(f32[9,1,16,128]{3,0,2,1:T(8,128)S(1)} %get-tuple-element.70), channel_id=1, source_target_pairs={{0,16},{16,32},{32,48},{48,64},{64,80},{80,96},{96,112},{112,128},... | collective-permute-start | bytes 221192 | tf_op jit(solution)/shard_map/ppermute | solution.py:21
  25.5 25.3 %collective-permute-start.6 = (f32[9,1,16,128]{3,0,2,1:T(8,128)S(1)}, f32[9,1,16,128]{3,0,2,1:T(8,128)S(1)}, u32[]{:S(2)}, u32[]{:S(2)}) collective-permute-start(f32[9,1,16,128]{3,0,2,1:T(8,128)S(1)} %get-tuple-element.71), channel_id=1, source_target_pairs={{16,0},{32,16},{48,32},{64,48},{80,64},{96,80},{112,96},{128,112},... | collective-permute-start | bytes 221192 | tf_op jit(solution)/shard_map/ppermute | solution.py:22
  32.0 18.7 %collective-permute-start.4 = (f32[9,8,1,128]{3,0,2,1:T(8,128)S(1)}, f32[9,8,1,128]{3,0,2,1:T(8,128)S(1)}, u32[]{:S(2)}, u32[]{:S(2)}) collective-permute-start(f32[9,8,1,128]{3,0,2,1:T(8,128)S(1)} %get-tuple-element.68), channel_id=1, source_target_pairs={{0,1},{1,2},{2,3},{3,4},{4,5},{5,6},{6,7},{7,8},{8,9},{9,10},{10,1... | collective-permute-start | bytes 110600 | tf_op jit(solution)/shard_map/ppermute | solution.py:23
  32.0 18.8 %collective-permute-start.7 = (f32[9,8,1,128]{3,0,2,1:T(8,128)S(1)}, f32[9,8,1,128]{3,0,2,1:T(8,128)S(1)}, u32[]{:S(2)}, u32[]{:S(2)}) collective-permute-start(f32[9,8,1,128]{3,0,2,1:T(8,128)S(1)} %get-tuple-element.69), channel_id=1, source_target_pairs={{1,0},{2,1},{3,2},{4,3},{5,4},{6,5},{7,6},{8,7},{9,8},{10,9},{11,1... | collective-permute-start | bytes 110600 | tf_op jit(solution)/shard_map/ppermute | solution.py:24
  55.2 1.5 copy-start.15
  55.2 1.5 copy-start.16
  60.0 9.2 %copy-start.19 = (s32[16]{0:T(128)S(1)}, s32[16]{0:T(128)}, u32[]{:S(2)}) copy-start(s32[16]{0:T(128)} %copy-done.18) | copy-start | bytes 196
  60.0 13.6 %copy-start = (f32[1,1,9,16,8,128]{5,4,3,2,1,0:T(8,128)S(1)}, f32[1,1,9,16,8,128]{5,4,3,2,1,0:T(8,128)}, u32[]{:S(2)}) copy-start(f32[1,1,9,16,8,128]{5,4,3,2,1,0:T(8,128)} %param.8) | copy-start | bytes 1769476
  60.0 50.0 %all-to-all-start = ((f32[16,1,28800]{2,1,0:T(1,128)}), f32[16,1,28800]{2,1,0:T(1,128)}, u32[]{:S(2)}, u32[]{:S(2)}) async-start(f32[16,1,28800]{2,1,0:T(1,128)} %broadcast_select_fusion), calls=%async_computation | async-start | bytes 3686400 | tf_op jit(solution)/shard_map/all_to_all | solution.py:187
  69.2 6.2 %copy-start.21 = (f32[9]{0:T(128)S(1)}, f32[9]{0:T(128)}, u32[]{:S(2)}) copy-start(f32[9]{0:T(128)} %param.12) | copy-start | bytes 112
  69.2 6.2 %copy-start.13 = (f32[9]{0:T(128)S(1)}, f32[9]{0:T(128)}, u32[]{:S(2)}) copy-start(f32[9]{0:T(128)} %param.13) | copy-start | bytes 112
  113.5 1.1 copy-start.9
  138.0 6.0 %copy-start.11 = (s32[1,16]{1,0:T(1,128)S(1)}, s32[1,16]{1,0:T(1,128)}, u32[]{:S(2)}) copy-start(s32[1,16]{1,0:T(1,128)} %param.10) | copy-start | bytes 196
  138.0 10.5 %copy-start.2 = (f32[9,16,8,128]{3,0,2,1:T(8,128)S(1)}, f32[9,16,8,128]{3,0,2,1:T(8,128)}, u32[]{:S(2)}) copy-start(f32[9,16,8,128]{3,0,2,1:T(8,128)} %get-tuple-element.108) | copy-start | bytes 1769476
  138.0 33.5 %all-to-all-start.1 = ((f32[16,1,18432]{2,1,0:T(1,128)}), f32[16,1,18432]{2,1,0:T(1,128)S(1)}, u32[]{:S(2)}, u32[]{:S(2)}) async-start(f32[16,1,18432]{2,1,0:T(1,128)} %broadcast_select_fusion.2), calls=%async_computation.1 | async-start | bytes 2359296 | tf_op jit(solution)/shard_map/all_to_all | solution.py:202

commit v3 on v2

--- a/solution.py
+++ b/solution.py
@@ -15,18 +15,39 @@
     return forward, backward
 
 
-def with_halo(block):
+def diagonal_pairs(step_x, step_y):
+    count_x = lax.axis_size("base")
+    count_y = lax.axis_size("fine")
+    return [
+        (
+            x * count_y + y,
+            ((x + step_x) % count_x) * count_y + (y + step_y) % count_y,
+        )
+        for x in range(count_x)
+        for y in range(count_y)
+    ]
+
+
+def with_deep_halo(block):
     x_forward, x_backward = ring_pairs("base")
     y_forward, y_backward = ring_pairs("fine")
-    low_x = lax.ppermute(block[:, -1:], "base", x_forward)
-    high_x = lax.ppermute(block[:, :1], "base", x_backward)
-    low_y = lax.ppermute(block[:, :, -1:], "fine", y_forward)
-    high_y = lax.ppermute(block[:, :, :1], "fine", y_backward)
-    corner = jnp.zeros_like(block[:, :1, :1])
-    low_y = jnp.concatenate([corner, low_y, corner], axis=1)
-    high_y = jnp.concatenate([corner, high_y, corner], axis=1)
-    block = jnp.concatenate([low_x, block, high_x], axis=1)
-    return jnp.concatenate([low_y, block, high_y], axis=2)
+    both = ("base", "fine")
+    low_x = lax.ppermute(block[:, -2:], "base", x_forward)
+    high_x = lax.ppermute(block[:, :2], "base", x_backward)
+    low_y = lax.ppermute(block[:, :, -2:], "fine", y_forward)
+    high_y = lax.ppermute(block[:, :, :2], "fine", y_backward)
+    low_low = lax.ppermute(block[:, -1:, -1:], both, diagonal_pairs(1, 1))
+    low_high = lax.ppermute(block[:, -1:, :1], both, diagonal_pairs(1, -1))
+    high_low = lax.ppermute(block[:, :1, -1:], both, diagonal_pairs(-1, 1))
+    high_high = lax.ppermute(block[:, :1, :1], both, diagonal_pairs(-1, -1))
+    blank = jnp.zeros_like(block[:, :1, :1])
+    blank_pair = jnp.zeros_like(block[:, :1, :2])
+    middle = jnp.concatenate([low_y, block, high_y], axis=2)
+    row_m2 = jnp.concatenate([blank_pair, low_x[:, 0:1], blank_pair], axis=2)
+    row_m1 = jnp.concatenate([blank, low_low, low_x[:, 1:2], low_high, blank], axis=2)
+    row_p0 = jnp.concatenate([blank, high_low, high_x[:, 0:1], high_high, blank], axis=2)
+    row_p1 = jnp.concatenate([blank_pair, high_x[:, 1:2], blank_pair], axis=2)
+    return jnp.concatenate([row_m2, row_m1, middle, row_p0, row_p1], axis=1)
 
 
 def reaction(values, reaction_rates, left_ids, right_ids):
@@ -165,16 +186,16 @@
         patch_id = slot_patch[slot_number]
         return packed_faces(extended, y_cell[patch_id] - my_index * height, z_cell[patch_id])
 
-    old_ext = with_halo(coarse_level)
-    centre = old_ext[:, 1:-1, 1:-1, :]
+    deep = with_deep_halo(coarse_level)
+    old_ext = deep[:, 1:-1, 1:-1, :]
     neighbours = (
-        old_ext[:, :-2, 1:-1, :]
-        + old_ext[:, 2:, 1:-1, :]
-        + (old_ext[:, 1:-1, :-2, :] + old_ext[:, 1:-1, 2:, :])
-        + (jnp.roll(centre, 1, 3) + jnp.roll(centre, -1, 3))
-    )
-    coarse_next = coarse_advance(centre, neighbours, viscosity, reaction_rates, left_ids, right_ids)
-    new_ext = with_halo(coarse_next)
+        deep[:, :-2, 1:-1, :]
+        + deep[:, 2:, 1:-1, :]
+        + (deep[:, 1:-1, :-2, :] + deep[:, 1:-1, 2:, :])
+        + (jnp.roll(old_ext, 1, 3) + jnp.roll(old_ext, -1, 3))
+    )
+    new_ext = coarse_advance(old_ext, neighbours, viscosity, reaction_rates, left_ids, right_ids)
+    coarse_next = new_ext[:, 1:-1, 1:-1, :]
     slots = [
         jnp.stack([slot_faces(old_ext, slot_number), slot_faces(new_ext, slot_number)])
         for slot_number in range(MOST)

time: 185 us -> 197 us (1.065)
  the two profiles are of different devices: /device:TPU:34 before, /device:TPU:198 now
where the time goes in v3:
time: 197 us; the launch traced here: 196 us
  waiting for transfers between devices  61.3 us (31%)
  local copies, waits for them, and re-layouts  56.7 us (29%)
  starting transfers between devices  27.5 us (14%)
  between operations  21.3 us (11%)
  matrix products  16.6 us (8%)
  other arithmetic  12.4 us (6%)
    all_to_all x1, waiting for transfers between devices, per_device(): arrived = lax.all_to_all(rows, 'fine', 0, 0, tiled=True)  24.1 us
    all_to_all x1, waiting for transfers between devices, per_device(): rows_in = lax.all_to_all(sent, 'fine', 0, 0, tiled=True)  20.9 us
    dot_general x3, matrix products, reaction(): jnp.einsum('fg,gxyz->fxyz', pick_right, values, precision=lax.Precision.H...  12.1 us
    dynamic_update_slice x2, local copies, waits for them, and re-layouts, per_device(): lax.dynamic_update_slice(coarse_out, jnp.where(slot_filled[slot_number],...  9.66 us
    ppermute x1, waiting for transfers between devices, with_deep_halo(): low_low = lax.ppermute(block[:, -1:, -1:], both, diagonal_pairs(1, 1))  8.17 us
    ppermute x1, waiting for transfers between devices, with_deep_halo(): low_x = lax.ppermute(block[:, -2:], 'base', x_forward)  8.07 us
    slice x4, local copies, waits for them, and re-layouts, fine_advance(): above = jnp.where(z_pos == cells_z - 1, high_z, jnp.roll(fine_box, -1, 3))  6.77 us
    ppermute x1, starting transfers between devices, with_deep_halo(): high_high = lax.ppermute(block[:, :1, :1], both, diagonal_pairs(-1, -1))  6.36 us
  transfers between devices with their start and end apart: 10, of which 4 were waited for; matrix products, arithmetic and copies ran while one was open for 12% of the time, Pallas kernels for 0%

profile of v3, /device:TPU:198, one launch (start us, length us, event | category | flops | bytes accessed | tf_op | source)
XLA Modules:
  0.0 195.7 jit_solution(1072716738482590582)
XLA Ops:
  0.7 1.0 fusion.63
  1.9 0.9 fusion.62
  2.8 1.7 collective-permute-start.5
  4.5 6.4 %collective-permute-start.7 = (f32[9,1,1,128]{3,0,2,1:T(8,128)S(1)}, f32[9,1,1,128]{3,0,2,1:T(8,128)S(1)}, u32[]{:S(2)}, u32[]{:S(2)}) collective-permute-start(f32[9,1,1,128]{3,0,2,1:T(8,128)S(1)} %copy.455), channel_id=1, source_target_pairs={{0,255},{1,240},{2,241},{3,242},{4,243},{5,244},{6,245},{7,246},{8... | collective-permute-start | bytes 13832 | tf_op jit(solution)/shard_map/ppermute | solution.py:42
  10.8 1.1 fusion.64
  12.5 3.8 %collective-permute-start.4 = (f32[9,8,2,128]{3,0,2,1:T(8,128)S(1)}, f32[9,8,2,128]{3,0,2,1:T(8,128)S(1)}, u32[]{:S(2)}, u32[]{:S(2)}) collective-permute-start(f32[9,8,2,128]{3,0,2,1:T(8,128)S(1)} %copy.457), channel_id=1, source_target_pairs={{1,0},{2,1},{3,2},{4,3},{5,4},{6,5},{7,6},{8,7},{9,8},{10,9},{11,1... | collective-permute-start | bytes 221192 | tf_op jit(solution)/shard_map/ppermute | solution.py:38
  17.9 0.7 fusion.51
  33.1 8.2 %collective-permute-done = f32[9,1,1,128]{3,0,2,1:T(8,128)S(1)} collective-permute-done((f32[9,1,1,128]{3,0,2,1:T(8,128)S(1)}, f32[9,1,1,128]{3,0,2,1:T(8,128)S(1)}, u32[]{:S(2)}, u32[]{:S(2)}) %collective-permute-start) | collective-permute-done | bytes 4640 | tf_op jit(solution)/shard_map/ppermute | solution.py:39
  41.3 4.1 %collective-permute-start.2 = (f32[9,1,1,128]{3,0,2,1:T(8,128)S(1)}, f32[9,1,1,128]{3,0,2,1:T(8,128)S(1)}, u32[]{:S(2)}, u32[]{:S(2)}) collective-permute-start(f32[9,1,1,128]{3,0,2,1:T(8,128)S(1)} %copy.460), channel_id=1, source_target_pairs={{0,31},{1,16},{2,17},{3,18},{4,19},{5,20},{6,21},{7,22},{8,23},{9,... | collective-permute-start | bytes 13832 | tf_op jit(solution)/shard_map/ppermute | solution.py:40
  45.9 8.1 %collective-permute-done.1 = f32[9,2,16,128]{3,0,2,1:T(8,128)S(1)} collective-permute-done((f32[9,2,16,128]{3,0,2,1:T(8,128)S(1)}, f32[9,2,16,128]{3,0,2,1:T(8,128)S(1)}, u32[]{:S(2)}, u32[]{:S(2)}) %collective-permute-start.1) | collective-permute-done | bytes 147488 | tf_op jit(solution)/shard_map/ppermute | solution.py:35
  55.3 0.8 fusion.33
  56.2 1.7 fusion.5
  58.5 0.7 dynamic-slice_reduce_fusion.4
  59.2 0.7 dynamic-slice_reduce_fusion.6
  62.6 3.3 %broadcast_select_fusion = f32[16,1,28800]{2,1,0:T(1,128)} fusion(pred[16]{0:T(512)(128)(4,1)S(1)} %get-tuple-element.34, pred[16]{0:T(512)(128)(4,1)S(1)} %get-tuple-element.35, f32[28800]{0:T(1024)S(1)} %broadcast_in_dim.208, f32[28800]{0:T(1024)S(1)} %broadcast_in_dim.205), kind=kLoop, calls=%fused_computation.2 | loop fusion | flops 921600 | bytes 2073632 | tf_op jit(solution)/shard_map/jit(_where)/select_n | solution.py:203
  66.0 5.6 %all-to-all-start = ((f32[16,1,28800]{2,1,0:T(1,128)}), f32[16,1,28800]{2,1,0:T(1,128)}, u32[]{:S(2)}, u32[]{:S(2)}) async-start(f32[16,1,28800]{2,1,0:T(1,128)} %broadcast_select_fusion), calls=%async_computation | async-start | bytes 3686400 | tf_op jit(solution)/shard_map/all_to_all | solution.py:208
  77.0 1.2 iota_compare_fusion.7
  80.4 1.9 convolution_multiply_fusion.3
  82.3 1.4 fusion.60
  83.7 1.5 fusion.61
  85.2 1.7 fusion.58
  86.9 1.8 fusion.59
  88.7 24.1 %all-to-all-done = f32[16,1,28800]{2,1,0:T(1,128)} async-done(((f32[16,1,28800]{2,1,0:T(1,128)}), f32[16,1,28800]{2,1,0:T(1,128)}, u32[]{:S(2)}, u32[]{:S(2)}) %all-to-all-start) | async-done | bytes 1843232 | tf_op jit(solution)/shard_map/all_to_all | solution.py:208
  112.8 0.9 dynamic-slice_bitcast_fusion
  113.7 0.8 slice_reduce_fusion
  116.2 0.9 copy.416
  119.0 5.0 %fusion.11 = f32[9,16,8,128]{3,0,2,1:T(8,128)S(1)} fusion(f32[9,16,8,128]{3,0,2,1:T(8,128)} %convolution_multiply_fusion.3, f32[9,15,8,128]{3,0,2,1:T(8,128)} %get-tuple-element.71, f32[9,1,8,128]{3,0,2,1:T(8,128)S(1)} %copy.414, f32[9,1,8,128]{3,0,2,1:T(8,128)} %copy.416, f32[9,15,8,128]{3,0,2,1:T(8,128)} %get-tuple-element.70, ...), kind=kOutput, calls=%fused_computation.29 | convolution fusion | flops 18874448 | bytes 5317960 | tf_op jit(solution)/shard_map/fg,gxyz->fxyz/dot_general | solution.py:59
  124.0 1.6 convolution_multiply_fusion.1
  125.6 1.7 fusion.55
  127.2 1.7 fusion.54
  129.7 1.4 fusion.56
  131.8 1.6 fusion.57
  135.5 0.8 reshape.389
  137.0 0.8 reshape.387
  138.3 0.8 reshape.385
  139.6 0.7 broadcast_in_dim.239
  140.4 0.7 broadcast_in_dim.235
  141.2 5.4 %bitcast_reduce_fusion = (f32[9,8,8,128]{3,0,2,1:T(8,128)S(1)}, f32[9,16,8,128]{3,0,2,1:T(8,128)}) fusion(f32[9,16,8,128]{3,0,2,1:T(8,128)} %convolution_multiply_fusion.1, f32[9,16,8,128]{3,0,2,1:T(8,128)S(1)} %fusion.11, s32[9]{0:T(128)S(1)} %copy-done.6, f32[9,16,8,1]{3,0,2,1:T(8,128)} %get-tuple-element.58, f32[9,16,8,127]{3,0,2,1:T(8,128)} %get-tuple-element.56, ...), kind=kOutput, calls=%fused_computation.52 | convolution fusion | flops 18948176 | bytes 5612872 | tf_op jit(solution)/shard_map/fg,gxyz->fxyz/dot_general | solution.py:59
  147.2 1.7 broadcast_select_fusion.2
  148.9 5.3 %all-to-all-start.1 = ((f32[16,1,18432]{2,1,0:T(1,128)}), f32[16,1,18432]{2,1,0:T(1,128)}, u32[]{:S(2)}, u32[]{:S(2)}) async-start(f32[16,1,18432]{2,1,0:T(1,128)} %broadcast_select_fusion.2), calls=%async_computation.1 | async-start | bytes 2359296 | tf_op jit(solution)/shard_map/all_to_all | solution.py:223
  158.8 2.2 %copy.438 = f32[1,1,9,16,8,128]{5,4,3,2,1,0:T(8,128)} copy(f32[1,1,9,16,8,128]{5,2,4,3,1,0:T(8,128)} %bitcast.159) | data formatting | bytes 1179648
  161.0 20.9 %all-to-all-done.1 = f32[16,1,18432]{2,1,0:T(1,128)} async-done(((f32[16,1,18432]{2,1,0:T(1,128)}), f32[16,1,18432]{2,1,0:T(1,128)}, u32[]{:S(2)}, u32[]{:S(2)}) %all-to-all-start.1) | async-done | bytes 1179680 | tf_op jit(solution)/shard_map/all_to_all | solution.py:223
  181.9 1.3 dynamic-slice_reduce_fusion.8
  183.4 0.8 copy_select_fusion.1
  184.2 4.8 %dynamic_update_slice.6 = f32[9,8,16,128]{3,0,2,1:T(8,128)S(1)} dynamic-update-slice(f32[9,8,16,128]{3,0,2,1:T(8,128)S(1)} %slice.346, f32[9,8,4,64]{3,0,2,1:T(8,128)S(1)} %copy_select_fusion.1, s32[]{:T(128)} %constant.196.clone.1, s32[]{:T(128)} %constant.196.clone.1, s32[]{:T(128)S(6)} %select_n.256, s32[]{:T(128)S(6)} %select_n.230) | dynamic-update-slice | bytes 147460 | tf_op jit(solution)/shard_map/dynamic_update_slice | solution.py:231
  189.1 0.8 copy_select_fusion
  189.9 4.8 %dynamic_update_slice.7 = f32[9,8,16,128]{3,0,2,1:T(8,128)S(1)} dynamic-update-slice(f32[9,8,16,128]{3,0,2,1:T(8,128)S(1)} %dynamic_update_slice.6, f32[9,8,4,64]{3,0,2,1:T(8,128)S(1)} %copy_select_fusion, s32[]{:T(128)} %constant.196.clone.1, s32[]{:T(128)} %constant.196.clone.1, s32[]{:T(128)S(6)} %select_n.260, s32[]{:T(128)S(6)} %select_n.240) | dynamic-update-slice | bytes 147460 | tf_op jit(solution)/shard_map/dynamic_update_slice | solution.py:231
  194.7 1.0 copy.437
  (213 shorter events, 23.6 us)
Async XLA Ops:
  0.6 15.7 %copy-start.9 = (s32[1,16,2]{1,2,0:T(2,128)S(1)}, s32[1,16,2]{1,2,0:T(2,128)}, u32[]{:S(2)}) copy-start(s32[1,16,2]{1,2,0:T(2,128)} %param.9) | copy-start | bytes 388
  0.6 15.7 %copy-start.7 = (s32[1,16]{1,0:T(1,128)S(1)}, s32[1,16]{1,0:T(1,128)}, u32[]{:S(2)}) copy-start(s32[1,16]{1,0:T(1,128)} %param.10) | copy-start | bytes 196
  0.7 25.0 %copy-start.15 = (s32[9,2]{0,1:T(2,128)S(1)}, s32[9,2]{0,1:T(2,128)}, u32[]{:S(2)}) copy-start(s32[9,2]{0,1:T(2,128)} %param.11) | copy-start | bytes 220
  1.8 43.7 %copy-start.1 = (f32[9,8,16,128]{3,2,1,0:T(8,128)S(1)}, f32[9,8,16,128]{3,2,1,0:T(8,128)}, u32[]{:S(2)}) copy-start(f32[9,8,16,128]{3,2,1,0:T(8,128)} %param.7) | copy-start | bytes 1769476
  1.8 44.0 %collective-permute-start.6 = (f32[9,2,16,128]{3,0,2,1:T(8,128)S(1)}, f32[9,2,16,128]{3,0,2,1:T(8,128)S(1)}, u32[]{:S(2)}, u32[]{:S(2)}) collective-permute-start(f32[9,2,16,128]{3,0,2,1:T(8,128)S(1)} %copy.454), channel_id=1, source_target_pairs={{16,0},{32,16},{48,32},{64,48},{80,64},{96,80},{112,96},{128,112},... | collective-permute-start | bytes 442376 | tf_op jit(solution)/shard_map/ppermute | solution.py:36
  2.8 30.2 %collective-permute-start.5 = (f32[9,1,1,128]{3,0,2,1:T(8,128)S(1)}, f32[9,1,1,128]{3,0,2,1:T(8,128)S(1)}, u32[]{:S(2)}, u32[]{:S(2)}) collective-permute-start(f32[9,1,1,128]{3,0,2,1:T(8,128)S(1)} %copy.453), channel_id=1, source_target_pairs={{0,241},{1,242},{2,243},{3,244},{4,245},{5,246},{6,247},{7,248},{8... | collective-permute-start | bytes 13832 | tf_op jit(solution)/shard_map/ppermute | solution.py:41
  4.5 41.4 %collective-permute-start.7 = (f32[9,1,1,128]{3,0,2,1:T(8,128)S(1)}, f32[9,1,1,128]{3,0,2,1:T(8,128)S(1)}, u32[]{:S(2)}, u32[]{:S(2)}) collective-permute-start(f32[9,1,1,128]{3,0,2,1:T(8,128)S(1)} %copy.455), channel_id=1, source_target_pairs={{0,255},{1,240},{2,241},{3,242},{4,243},{5,244},{6,245},{7,246},{8... | collective-permute-start | bytes 13832 | tf_op jit(solution)/shard_map/ppermute | solution.py:42
  12.0 29.3 %collective-permute-start.3 = (f32[9,8,2,128]{3,0,2,1:T(8,128)S(1)}, f32[9,8,2,128]{3,0,2,1:T(8,128)S(1)}, u32[]{:S(2)}, u32[]{:S(2)}) collective-permute-start(f32[9,8,2,128]{3,0,2,1:T(8,128)S(1)} %copy.456), channel_id=1, source_target_pairs={{0,1},{1,2},{2,3},{3,4},{4,5},{5,6},{6,7},{7,8},{8,9},{9,10},{10,1... | collective-permute-start | bytes 221192 | tf_op jit(solution)/shard_map/ppermute | solution.py:37
  12.5 33.4 %collective-permute-start.4 = (f32[9,8,2,128]{3,0,2,1:T(8,128)S(1)}, f32[9,8,2,128]{3,0,2,1:T(8,128)S(1)}, u32[]{:S(2)}, u32[]{:S(2)}) collective-permute-start(f32[9,8,2,128]{3,0,2,1:T(8,128)S(1)} %copy.457), channel_id=1, source_target_pairs={{1,0},{2,1},{3,2},{4,3},{5,4},{6,5},{7,6},{8,7},{9,8},{10,9},{11,1... | collective-permute-start | bytes 221192 | tf_op jit(solution)/shard_map/ppermute | solution.py:38
  25.7 30.5 %copy-start.5 = (s32[9]{0:T(128)}, s32[9]{0:T(128)S(1)}, u32[]{:S(2)}) copy-start(s32[9]{0:T(128)S(1)} %get-tuple-element.101) | copy-start | bytes 112
  33.0 8.3 %collective-permute-start = (f32[9,1,1,128]{3,0,2,1:T(8,128)S(1)}, f32[9,1,1,128]{3,0,2,1:T(8,128)S(1)}, u32[]{:S(2)}, u32[]{:S(2)}) collective-permute-start(f32[9,1,1,128]{3,0,2,1:T(8,128)S(1)} %copy.458), channel_id=1, source_target_pairs={{0,17},{1,18},{2,19},{3,20},{4,21},{5,22},{6,23},{7,24},{8,25},{9,... | collective-permute-start | bytes 13832 | tf_op jit(solution)/shard_map/ppermute | solution.py:39
  41.3 12.7 %collective-permute-start.1 = (f32[9,2,16,128]{3,0,2,1:T(8,128)S(1)}, f32[9,2,16,128]{3,0,2,1:T(8,128)S(1)}, u32[]{:S(2)}, u32[]{:S(2)}) collective-permute-start(f32[9,2,16,128]{3,0,2,1:T(8,128)S(1)} %copy.459), channel_id=1, source_target_pairs={{0,16},{16,32},{32,48},{48,64},{64,80},{80,96},{96,112},{112,128},... | collective-permute-start | bytes 442376 | tf_op jit(solution)/shard_map/ppermute | solution.py:35
  41.3 12.7 %collective-permute-start.2 = (f32[9,1,1,128]{3,0,2,1:T(8,128)S(1)}, f32[9,1,1,128]{3,0,2,1:T(8,128)S(1)}, u32[]{:S(2)}, u32[]{:S(2)}) collective-permute-start(f32[9,1,1,128]{3,0,2,1:T(8,128)S(1)} %copy.460), channel_id=1, source_target_pairs={{0,31},{1,16},{2,17},{3,18},{4,19},{5,20},{6,21},{7,22},{8,23},{9,... | collective-permute-start | bytes 13832 | tf_op jit(solution)/shard_map/ppermute | solution.py:40
  55.3 0.9 copy-start.13
  55.3 0.9 copy-start.20
  66.0 10.0 %copy-start = (f32[1,1,9,16,8,128]{5,4,3,2,1,0:T(8,128)S(1)}, f32[1,1,9,16,8,128]{5,4,3,2,1,0:T(8,128)}, u32[]{:S(2)}) copy-start(f32[1,1,9,16,8,128]{5,4,3,2,1,0:T(8,128)} %param.8) | copy-start | bytes 1769476
  66.0 46.8 %all-to-all-start = ((f32[16,1,28800]{2,1,0:T(1,128)}), f32[16,1,28800]{2,1,0:T(1,128)}, u32[]{:S(2)}, u32[]{:S(2)}) async-start(f32[16,1,28800]{2,1,0:T(1,128)} %broadcast_select_fusion), calls=%async_computation | async-start | bytes 3686400 | tf_op jit(solution)/shard_map/all_to_all | solution.py:208
  117.6 1.1 copy-start.4
  117.6 1.2 copy-start.3
  117.6 1.4 copy-start.6
  119.0 5.0 %copy-start.14 = (f32[9]{0:T(128)S(1)}, f32[9]{0:T(128)}, u32[]{:S(2)}) copy-start(f32[9]{0:T(128)} %param.13) | copy-start | bytes 112
  127.2 1.7 copy-start.2
  138.1 3.1 %copy-start.10 = (pred[128]{0:T(512)(128)(4,1)S(1)}, pred[128]{0:T(512)(128)(4,1)}, u32[]{:S(2)}) copy-start(pred[128]{0:T(512)(128)(4,1)} %iota_compare_fusion.5) | copy-start | bytes 388
  138.1 3.1 %copy-start.11 = (pred[128]{0:T(512)(128)(4,1)S(1)}, pred[128]{0:T(512)(128)(4,1)}, u32[]{:S(2)}) copy-start(pred[128]{0:T(512)(128)(4,1)} %get-tuple-element.114) | copy-start | bytes 388
  138.1 3.1 %copy-start.12 = (f32[9]{0:T(128)S(1)}, f32[9]{0:T(128)}, u32[]{:S(2)}) copy-start(f32[9]{0:T(128)} %broadcast_multiply_fusion) | copy-start | bytes 112
  141.2 5.5 %copy-start.17 = (pred[128]{0:T(512)(128)(4,1)S(1)}, pred[128]{0:T(512)(128)(4,1)}, u32[]{:S(2)}) copy-start(pred[128]{0:T(512)(128)(4,1)} %get-tuple-element.113) | copy-start | bytes 388
  141.2 5.5 %copy-start.18 = (s32[128]{0:T(128)S(1)}, s32[128]{0:T(128)}, u32[]{:S(2)}) copy-start(s32[128]{0:T(128)} %get-tuple-element.115) | copy-start | bytes 1540
  141.2 5.5 %copy-start.19 = (s32[128]{0:T(128)S(1)}, s32[128]{0:T(128)}, u32[]{:S(2)}) copy-start(s32[128]{0:T(128)} %get-tuple-element.116) | copy-start | bytes 1540
  146.6 0.6 copy-start.16
  148.9 5.3 %copy-start.8 = (s32[1,16]{1,0:T(1,128)S(1)}, s32[1,16]{1,0:T(1,128)}, u32[]{:S(2)}) copy-start(s32[1,16]{1,0:T(1,128)} %param.10) | copy-start | bytes 196
  148.9 33.0 %all-to-all-start.1 = ((f32[16,1,18432]{2,1,0:T(1,128)}), f32[16,1,18432]{2,1,0:T(1,128)}, u32[]{:S(2)}, u32[]{:S(2)}) async-start(f32[16,1,18432]{2,1,0:T(1,128)} %broadcast_select_fusion.2), calls=%async_computation.1 | async-start | bytes 2359296 | tf_op jit(solution)/shard_map/all_to_all | solution.py:223

commit v4 on v2

--- a/solution.py
+++ b/solution.py
@@ -48,17 +48,17 @@
 
 
 def widen_face(face):
-    return jnp.repeat(jnp.repeat(face, 2, axis=1), 2, axis=2)
+    return jnp.repeat(jnp.repeat(face, 2, axis=-2), 2, axis=-1)
 
 
 def fine_advance(fine_box, faces, viscosity, reaction_rates, left_ids, right_ids):
-    face_xlo, face_xhi, face_ylo, face_yhi, face_zlo, face_zhi = faces
-    low_x = widen_face(face_xlo)[:, None]
-    high_x = widen_face(face_xhi)[:, None]
-    low_y = widen_face(face_ylo)[:, :, None]
-    high_y = widen_face(face_yhi)[:, :, None]
-    low_z = widen_face(face_zlo)[:, :, :, None]
-    high_z = widen_face(face_zhi)[:, :, :, None]
+    low_x, high_x, low_y, high_y, low_z, high_z = faces
+    low_x = low_x[:, None]
+    high_x = high_x[:, None]
+    low_y = low_y[:, :, None]
+    high_y = high_y[:, :, None]
+    low_z = low_z[:, :, :, None]
+    high_z = high_z[:, :, :, None]
     pair_x = jnp.concatenate([low_x, fine_box[:, :-1]], axis=1) + jnp.concatenate(
         [fine_box[:, 1:], high_x], axis=1
     )
@@ -111,22 +111,16 @@
 
 
 def unpack_faces(packed, cells_x):
-    fields = packed.shape[0]
+    pairs, fields = packed.shape[:2]
     widths = [BY * BZ, BY * BZ, cells_x * BZ, cells_x * BZ, cells_x * BY, cells_x * BY]
-    shapes = [
-        (fields, BY, BZ),
-        (fields, BY, BZ),
-        (fields, cells_x, BZ),
-        (fields, cells_x, BZ),
-        (fields, cells_x, BY),
-        (fields, cells_x, BY),
-    ]
+    shapes = [(BY, BZ), (BY, BZ), (cells_x, BZ), (cells_x, BZ), (cells_x, BY), (cells_x, BY)]
     face_list = []
     offset = 0
     for width_now, shape_now in zip(widths, shapes):
-        face_list.append(packed[:, offset : offset + width_now].reshape(shape_now))
+        part = packed[:, :, offset : offset + width_now].reshape((pairs, fields) + shape_now)
+        face_list.append(widen_face(part))
         offset = offset + width_now
-    return tuple(face_list)
+    return face_list
 
 
 def per_device(
@@ -187,29 +181,36 @@
     arrived = lax.all_to_all(rows, "fine", 0, 0, tiled=True)
     shell_pair = lax.dynamic_index_in_dim(arrived, source_of_mine, 0, keepdims=False)
     shell_pair = shell_pair.reshape(slots[0].shape)
-    old_shell = shell_pair[0]
-    new_shell = shell_pair[1]
+    wide_pair = unpack_faces(shell_pair, cells_x)
+    old_faces = [wide[0] for wide in wide_pair]
+    mid_faces = [0.5 * (wide[0] + wide[1]) for wide in wide_pair]
 
     fine_box = fine_level[0, 0]
-    old_faces = unpack_faces(old_shell, cells_x)
     fine_box = fine_advance(fine_box, old_faces, viscosity, reaction_rates, left_ids, right_ids)
-    mid_faces = unpack_faces(0.5 * (old_shell + new_shell), cells_x)
     fine_box = fine_advance(fine_box, mid_faces, viscosity, reaction_rates, left_ids, right_ids)
     averaged = coarsen(fine_box)
 
     dest_ids = lax.broadcasted_iota(jnp.int32, (devices_fine, 1), 0)
     sent = jnp.where(dest_ids == source_of_mine, averaged.reshape(1, -1), 0.0)
     rows_in = lax.all_to_all(sent, "fine", 0, 0, tiled=True)
+    y_ids = lax.broadcasted_iota(jnp.int32, (height, cells_z), 0)
+    z_ids = lax.broadcasted_iota(jnp.int32, (height, cells_z), 1)
     coarse_out = coarse_next
     for slot_number in range(MOST):
         patch_id = slot_patch[slot_number]
-        corner = (0, 0, y_cell[patch_id] - my_index * height, z_cell[patch_id])
+        offset = y_cell[patch_id] - my_index * height
+        z_start = z_cell[patch_id]
         incoming = lax.dynamic_index_in_dim(rows_in, owners[patch_id], 0, keepdims=False)
         incoming = incoming.reshape(averaged.shape)
-        present = lax.dynamic_slice(coarse_out, corner, incoming.shape)
-        coarse_out = lax.dynamic_update_slice(
-            coarse_out, jnp.where(slot_filled[slot_number], incoming, present), corner
+        tiled = jnp.tile(incoming, (1, 1, height // BY, cells_z // BZ))
+        covered = (
+            slot_filled[slot_number]
+            & (y_ids >= offset)
+            & (y_ids < offset + BY)
+            & (z_ids >= z_start)
+            & (z_ids < z_start + BZ)
         )
+        coarse_out = jnp.where(covered[None, None], tiled, coarse_out)
     return (coarse_out, fine_box[None, None])
 
 

time: 185 us -> 179 us (0.968)
  local copies, waits for them, and re-layouts: 49.7 us -> 43.7 us
  waiting for transfers between devices: 48.4 us -> 43.1 us
  other arithmetic: 11.7 us -> 16.5 us
    dynamic_update_slice x2 -> x0, local copies, waits for them, and re-layouts: 9.66 us -> none  [per_device(): lax.dynamic_update_slice(coarse_out, jnp.where(slot_filled[slot_number],...]
    broadcast_in_dim x24 -> x40, local copies, waits for them, and re-layouts: 1.59 us -> 4.84 us  [widen_face(): return jnp.repeat(jnp.repeat(face, 2, axis=-2), 2, axis=-1)]
    all_to_all x1, waiting for transfers between devices: 26.4 us -> 23.6 us  [per_device(): arrived = lax.all_to_all(rows, 'fine', 0, 0, tiled=True)]
    all_to_all x1, waiting for transfers between devices: 22.1 us -> 19.4 us  [per_device(): rows_in = lax.all_to_all(sent, 'fine', 0, 0, tiled=True)]
    slice x11 -> x19, local copies, waits for them, and re-layouts: 0.84 us -> 2.78 us  [the longest x11 2.03 us: per_device(): mid_faces = [0.5 * (wide[0] + wide[1]) for wide in wide_pair]]
    reshape x18 -> x1, local copies, waits for them, and re-layouts: 1.97 us -> 0.11 us  [per_device(): shell_pair = shell_pair.reshape(slots[0].shape)]
    unnamed x50 -> x78, local copies, waits for them, and re-layouts: 4.86 us -> 5.16 us
  transfers between devices with their start and end apart: 10 -> 10, of which waited for: 2 -> 2; matrix products, arithmetic and copies ran while one was open for 13% -> 17% of each run, Pallas kernels for 0% -> 0%
where the time goes in v4:
time: 179 us; the launch traced here: 178 us
  local copies, waits for them, and re-layouts  43.7 us (24%)
  waiting for transfers between devices  43.1 us (24%)
  starting transfers between devices  36.6 us (20%)
  between operations  20.8 us (12%)
  matrix products  17.3 us (10%)
  other arithmetic  16.5 us (9%)
    all_to_all x1, waiting for transfers between devices, per_device(): arrived = lax.all_to_all(rows, 'fine', 0, 0, tiled=True)  23.6 us
    all_to_all x1, waiting for transfers between devices, per_device(): rows_in = lax.all_to_all(sent, 'fine', 0, 0, tiled=True)  19.4 us
    ppermute x2, starting transfers between devices, with_halo(): high_x = lax.ppermute(block[:, :1], 'base', x_backward)  13.1 us
    dot_general x3, matrix products, reaction(): jnp.einsum('fg,gxyz->fxyz', pick_right, values, precision=lax.Precision.H...  12.6 us
    all_to_all x1, starting transfers between devices, per_device(): arrived = lax.all_to_all(rows, 'fine', 0, 0, tiled=True)  9.15 us
    slice x4, local copies, waits for them, and re-layouts, fine_advance(): above = jnp.where(z_pos == cells_z - 1, high_z, jnp.roll(fine_box, -1, 3))  6.72 us
    ppermute x2, starting transfers between devices, with_halo(): high_y = lax.ppermute(block[:, :, :1], 'fine', y_backward)  6.69 us
    all_to_all x1, starting transfers between devices, per_device(): rows_in = lax.all_to_all(sent, 'fine', 0, 0, tiled=True)  5.95 us
  transfers between devices with their start and end apart: 10, of which 2 were waited for; matrix products, arithmetic and copies ran while one was open for 17% of the time, Pallas kernels for 0%

profile of v4, /device:TPU:34, one launch (start us, length us, event | category | flops | bytes accessed | tf_op | source)
XLA Modules:
  0.0 178.1 jit_solution(4052551298348544324)
XLA Ops:
  0.6 1.4 copy.375
  2.2 6.5 %collective-permute-start.2 = (f32[9,1,16,128]{3,0,2,1:T(8,128)S(1)}, f32[9,1,16,128]{3,0,2,1:T(8,128)S(1)}, u32[]{:S(2)}, u32[]{:S(2)}) collective-permute-start(f32[9,1,16,128]{3,0,2,1:T(8,128)S(1)} %get-tuple-element.74), channel_id=1, source_target_pairs={{16,0},{32,16},{48,32},{64,48},{80,64},{96,80},{112,96},{128,112},... | collective-permute-start | bytes 221192 | tf_op jit(solution)/shard_map/ppermute | solution.py:22
  8.7 0.6 fusion.66
  9.4 1.6 collective-permute-start
  11.0 2.6 %collective-permute-start.3 = (f32[9,8,1,128]{3,0,2,1:T(8,128)}, f32[9,8,1,128]{3,0,2,1:T(8,128)}, u32[]{:S(2)}, u32[]{:S(2)}) collective-permute-start(f32[9,8,1,128]{3,0,2,1:T(8,128)} %get-tuple-element.73), channel_id=1, source_target_pairs={{1,0},{2,1},{3,2},{4,3},{5,4},{6,5},{7,6},{8,7},{9,8},{10,9},{11,1... | collective-permute-start | bytes 110600 | tf_op jit(solution)/shard_map/ppermute | solution.py:24
  14.1 1.7 fusion.64
  15.8 1.6 fusion.65
  17.7 0.7 gather_fusion
  18.3 0.7 gather_fusion.1
  19.0 0.7 fusion.53
  19.7 0.9 convolution_multiply_fusion.5
  21.3 0.7 select_reduce_fusion.3
  23.0 2.3 %fusion.8 = f32[9,8,16,128]{3,0,2,1:T(8,128)S(1)} fusion(f32[9,8,16,128]{3,0,2,1:T(8,128)S(1)} %convolution_multiply_fusion.5, f32[9,8,16,128]{3,0,2,1:T(8,128)S(1)} %copy.375, f32[9,10,16,128]{3,0,2,1:T(8,128)S(1)} %constant_dynamic-update-slice_fusion, f32[9,1,1,128]{3,0,2,1:T(8,128)S(1)} %broadcast.475, f32[9,8,1,128]{3,0,2,1:T(8,128)} %collective-permute-done.3, ...), kind=kOutput, calls=%fused_computation.26 | convolution fusion | flops 19021904 | bytes 3912264 | tf_op jit(solution)/shard_map/fg,gxyz->fxyz/dot_general | solution.py:38
  25.5 6.5 %collective-permute-start.6 = (f32[9,1,16,128]{3,0,2,1:T(8,128)S(1)}, f32[9,1,16,128]{3,0,2,1:T(8,128)S(1)}, u32[]{:S(2)}, u32[]{:S(2)}) collective-permute-start(f32[9,1,16,128]{3,0,2,1:T(8,128)S(1)} %get-tuple-element.67), channel_id=1, source_target_pairs={{16,0},{32,16},{48,32},{64,48},{80,64},{96,80},{112,96},{128,112},... | collective-permute-start | bytes 221192 | tf_op jit(solution)/shard_map/ppermute | solution.py:22
  32.0 4.1 %collective-permute-start.7 = (f32[9,8,1,128]{3,0,2,1:T(8,128)S(1)}, f32[9,8,1,128]{3,0,2,1:T(8,128)S(1)}, u32[]{:S(2)}, u32[]{:S(2)}) collective-permute-start(f32[9,8,1,128]{3,0,2,1:T(8,128)S(1)} %get-tuple-element.65), channel_id=1, source_target_pairs={{1,0},{2,1},{3,2},{4,3},{5,4},{6,5},{7,6},{8,7},{9,8},{10,9},{11,1... | collective-permute-start | bytes 110600 | tf_op jit(solution)/shard_map/ppermute | solution.py:24
  36.2 0.6 select_reduce_fusion.2
  40.6 1.4 constant_dynamic-slice_fusion.18
  44.5 1.2 constant_dynamic-slice_fusion.19
  50.8 1.1 fusion.1
  51.9 0.7 dynamic-slice_reduce_fusion.6
  52.6 0.7 dynamic-slice_reduce_fusion.4
  56.7 3.3 %broadcast_select_fusion = f32[16,1,28800]{2,1,0:T(1,128)} fusion(pred[16]{0:T(512)(128)(4,1)S(1)} %copy-done.25, pred[16]{0:T(512)(128)(4,1)S(1)} %copy-done.26, f32[28800]{0:T(1024)S(1)} %broadcast_in_dim.250, f32[28800]{0:T(1024)S(1)} %broadcast_in_dim.247), kind=kLoop, calls=%fused_computation.2 | loop fusion | flops 921600 | bytes 2073632 | tf_op jit(solution)/shard_map/jit(_where)/select_n | solution.py:176
  60.0 9.2 %all-to-all-start = ((f32[16,1,28800]{2,1,0:T(1,128)}), f32[16,1,28800]{2,1,0:T(1,128)}, u32[]{:S(2)}, u32[]{:S(2)}) async-start(f32[16,1,28800]{2,1,0:T(1,128)} %broadcast_select_fusion), calls=%async_computation | async-start | bytes 3686400 | tf_op jit(solution)/shard_map/all_to_all | solution.py:181
  75.2 1.2 iota_compare_fusion.9
  78.1 1.9 %convolution_multiply_fusion.3 = f32[9,16,8,128]{3,0,2,1:T(8,128)} fusion(f32[9]{0:T(128)S(1)} %copy-done.20, f32[1,1,9,16,8,128]{5,4,3,2,1,0:T(8,128)S(1)} %copy-done, s32[9]{0:T(128)S(1)} %get-tuple-element.96), kind=kOutput, calls=%fused_computation.24 | convolution fusion | flops 16072785 | bytes 1179720 | tf_op jit(solution)/shard_map/fg,gxyz->fxyz/dot_general | solution.py:37
  80.0 1.4 fusion.60
  81.4 1.5 fusion.61
  82.9 1.7 fusion.58
  84.6 1.7 fusion.59
  86.3 23.6 %all-to-all-done = f32[16,1,28800]{2,1,0:T(1,128)} async-done(((f32[16,1,28800]{2,1,0:T(1,128)}), f32[16,1,28800]{2,1,0:T(1,128)}, u32[]{:S(2)}, u32[]{:S(2)}) %all-to-all-start) | async-done | bytes 1843232 | tf_op jit(solution)/shard_map/all_to_all | solution.py:181
  110.0 1.2 dynamic-slice_reduce_fusion.8
  111.9 0.7 fusion.68
  116.5 4.9 %fusion.7 = f32[9,16,8,128]{3,0,2,1:T(8,128)S(1)} fusion(f32[9,16,8,128]{3,0,2,1:T(8,128)} %convolution_multiply_fusion.3, f32[9,15,8,128]{3,0,2,1:T(8,128)} %get-tuple-element.63, f32[9,1,8,128]{3,0,2,1:T(8,128)S(1)} %copy.415, f32[9,1,8,128]{3,0,2,1:T(8,128)S(1)} %copy.417, f32[9,15,8,128]{3,0,2,1:T(8,128)} %get-tuple-element.62, ...), kind=kOutput, calls=%fused_computation.23 | convolution fusion | flops 18874448 | bytes 5317960 | tf_op jit(solution)/shard_map/fg,gxyz->fxyz/dot_general | solution.py:38
  121.4 1.7 fusion.54
  123.1 1.7 fusion.55
  124.8 1.5 fusion.57
  126.3 1.4 fusion.56
  127.7 1.6 convolution_multiply_fusion.1
  132.5 5.4 %bitcast_reduce_fusion = (f32[9,8,8,128]{3,0,2,1:T(8,128)S(1)}, f32[9,16,8,128]{3,0,2,1:T(8,128)}) fusion(f32[9,16,8,128]{3,0,2,1:T(8,128)} %convolution_multiply_fusion.1, f32[9,16,8,128]{3,0,2,1:T(8,128)S(1)} %fusion.7, s32[9]{0:T(128)S(1)} %copy-done.16, f32[9,16,8,1]{3,0,2,1:T(8,128)} %get-tuple-element.50, f32[9,16,8,127]{3,0,2,1:T(8,128)} %get-tuple-element.48, ...), kind=kOutput, calls=%fused_computation.65 | convolution fusion | flops 18948176 | bytes 5612872 | tf_op jit(solution)/shard_map/fg,gxyz->fxyz/dot_general | solution.py:38
  138.6 1.7 broadcast_select_fusion.2
  140.3 6.0 %all-to-all-start.1 = ((f32[16,1,18432]{2,1,0:T(1,128)}), f32[16,1,18432]{2,1,0:T(1,128)S(1)}, u32[]{:S(2)}, u32[]{:S(2)}) async-start(f32[16,1,18432]{2,1,0:T(1,128)} %broadcast_select_fusion.2), calls=%async_computation.1 | async-start | bytes 2359296 | tf_op jit(solution)/shard_map/all_to_all | solution.py:195
  152.6 0.6 compare_and_fusion.4
  153.4 1.0 copy.447
  154.4 19.4 %all-to-all-done.1 = f32[16,1,18432]{2,1,0:T(1,128)S(1)} async-done(((f32[16,1,18432]{2,1,0:T(1,128)}), f32[16,1,18432]{2,1,0:T(1,128)S(1)}, u32[]{:S(2)}, u32[]{:S(2)}) %all-to-all-start.1) | async-done | bytes 1179680 | tf_op jit(solution)/shard_map/all_to_all | solution.py:195
  174.7 0.6 tile.22
  175.7 0.6 tile.25
  176.4 0.7 copy_select_fusion
  177.1 1.0 copy.446
  (242 shorter events, 21.5 us)
Async XLA Ops:
  0.6 12.9 %copy-start.21 = (s32[1,16,2]{1,2,0:T(2,128)S(1)}, s32[1,16,2]{1,2,0:T(2,128)}, u32[]{:S(2)}) copy-start(s32[1,16,2]{1,2,0:T(2,128)} %param.9) | copy-start | bytes 388
  2.1 19.8 %collective-permute-start.1 = (f32[9,1,16,128]{3,0,2,1:T(8,128)S(1)}, f32[9,1,16,128]{3,0,2,1:T(8,128)S(1)}, u32[]{:S(2)}, u32[]{:S(2)}) collective-permute-start(f32[9,1,16,128]{3,0,2,1:T(8,128)S(1)} %get-tuple-element.75), channel_id=1, source_target_pairs={{0,16},{16,32},{32,48},{48,64},{64,80},{80,96},{96,112},{112,128},... | collective-permute-start | bytes 221192 | tf_op jit(solution)/shard_map/ppermute | solution.py:21
  2.2 20.1 %collective-permute-start.2 = (f32[9,1,16,128]{3,0,2,1:T(8,128)S(1)}, f32[9,1,16,128]{3,0,2,1:T(8,128)S(1)}, u32[]{:S(2)}, u32[]{:S(2)}) collective-permute-start(f32[9,1,16,128]{3,0,2,1:T(8,128)S(1)} %get-tuple-element.74), channel_id=1, source_target_pairs={{16,0},{32,16},{48,32},{64,48},{80,64},{96,80},{112,96},{128,112},... | collective-permute-start | bytes 221192 | tf_op jit(solution)/shard_map/ppermute | solution.py:22
  9.4 13.0 %collective-permute-start = (f32[9,8,1,128]{3,0,2,1:T(8,128)}, f32[9,8,1,128]{3,0,2,1:T(8,128)}, u32[]{:S(2)}, u32[]{:S(2)}) collective-permute-start(f32[9,8,1,128]{3,0,2,1:T(8,128)} %get-tuple-element.72), channel_id=1, source_target_pairs={{0,1},{1,2},{2,3},{3,4},{4,5},{5,6},{6,7},{7,8},{8,9},{9,10},{10,1... | collective-permute-start | bytes 110600 | tf_op jit(solution)/shard_map/ppermute | solution.py:23
  11.0 11.4 %collective-permute-start.3 = (f32[9,8,1,128]{3,0,2,1:T(8,128)}, f32[9,8,1,128]{3,0,2,1:T(8,128)}, u32[]{:S(2)}, u32[]{:S(2)}) collective-permute-start(f32[9,8,1,128]{3,0,2,1:T(8,128)} %get-tuple-element.73), channel_id=1, source_target_pairs={{1,0},{2,1},{3,2},{4,3},{5,4},{6,5},{7,6},{8,7},{9,8},{10,9},{11,1... | collective-permute-start | bytes 110600 | tf_op jit(solution)/shard_map/ppermute | solution.py:24
  15.8 1.6 copy-start.17
  15.8 3.9 %copy-start.27 = (s32[9,2]{0,1:T(2,128)S(1)}, s32[9,2]{0,1:T(2,128)}, u32[]{:S(2)}) copy-start(s32[9,2]{0,1:T(2,128)} %param.11) | copy-start | bytes 220
  15.8 3.9 %copy-start.19 = (f32[9]{0:T(128)S(1)}, f32[9]{0:T(128)}, u32[]{:S(2)}) copy-start(f32[9]{0:T(128)} %param.13) | copy-start | bytes 112
  17.5 2.2 %copy-start.1 = (f32[9,8,16,128]{3,2,1,0:T(8,128)S(1)}, f32[9,8,16,128]{3,2,1,0:T(8,128)}, u32[]{:S(2)}) copy-start(f32[9,8,16,128]{3,2,1,0:T(8,128)} %param.7) | copy-start | bytes 1769476
  17.6 3.0 %copy-start.32 = (s32[16]{0:T(128)}, s32[16]{0:T(128)S(1)}, u32[]{:S(2)}) copy-start(s32[16]{0:T(128)S(1)} %get-tuple-element.105) | copy-start | bytes 196
  19.7 3.3 %copy-start.14 = (s32[9]{0:T(128)}, s32[9]{0:T(128)S(1)}, u32[]{:S(2)}) copy-start(s32[9]{0:T(128)S(1)} %get-tuple-element.95) | copy-start | bytes 112
  19.7 58.5 %copy-start.12 = (s32[9]{0:T(128)}, s32[9]{0:T(128)S(1)}, u32[]{:S(2)}) copy-start(s32[9]{0:T(128)S(1)} %get-tuple-element.96) | copy-start | bytes 112
  19.7 3.3 %copy-start.5 = (f32[9,8,16,1]{3,0,2,1:T(8,128)S(1)}, f32[9,8,16,1]{3,0,2,1:T(8,128)}, u32[]{:S(2)}) copy-start(f32[9,8,16,1]{3,0,2,1:T(8,128)} %get-tuple-element.70) | copy-start | bytes 13828
  19.7 3.3 %copy-start.6 = (f32[9,8,16,1]{3,0,2,1:T(8,128)S(1)}, f32[9,8,16,1]{3,0,2,1:T(8,128)}, u32[]{:S(2)}) copy-start(f32[9,8,16,1]{3,0,2,1:T(8,128)} %get-tuple-element.71) | copy-start | bytes 13828
  20.7 2.3 %copy-start.3 = (f32[9,8,16,127]{3,0,2,1:T(8,128)S(1)}, f32[9,8,16,127]{3,0,2,1:T(8,128)}, u32[]{:S(2)}) copy-start(f32[9,8,16,127]{3,0,2,1:T(8,128)} %get-tuple-element.68) | copy-start | bytes 1755652
  20.7 2.3 %copy-start.4 = (f32[9,8,16,127]{3,0,2,1:T(8,128)S(1)}, f32[9,8,16,127]{3,0,2,1:T(8,128)}, u32[]{:S(2)}) copy-start(f32[9,8,16,127]{3,0,2,1:T(8,128)} %get-tuple-element.69) | copy-start | bytes 1755652
  20.7 2.3 %copy-start.34 = (f32[9]{0:T(128)S(1)}, f32[9]{0:T(128)}, u32[]{:S(2)}) copy-start(f32[9]{0:T(128)} %param.12) | copy-start | bytes 112
  22.3 0.7 copy-start.7
  25.4 25.3 %collective-permute-start.5 = (f32[9,1,16,128]{3,0,2,1:T(8,128)S(1)}, f32[9,1,16,128]{3,0,2,1:T(8,128)S(1)}, u32[]{:S(2)}, u32[]{:S(2)}) collective-permute-start(f32[9,1,16,128]{3,0,2,1:T(8,128)S(1)} %get-tuple-element.66), channel_id=1, source_target_pairs={{0,16},{16,32},{32,48},{48,64},{64,80},{80,96},{96,112},{112,128},... | collective-permute-start | bytes 221192 | tf_op jit(solution)/shard_map/ppermute | solution.py:21
  25.5 25.3 %collective-permute-start.6 = (f32[9,1,16,128]{3,0,2,1:T(8,128)S(1)}, f32[9,1,16,128]{3,0,2,1:T(8,128)S(1)}, u32[]{:S(2)}, u32[]{:S(2)}) collective-permute-start(f32[9,1,16,128]{3,0,2,1:T(8,128)S(1)} %get-tuple-element.67), channel_id=1, source_target_pairs={{16,0},{32,16},{48,32},{64,48},{80,64},{96,80},{112,96},{128,112},... | collective-permute-start | bytes 221192 | tf_op jit(solution)/shard_map/ppermute | solution.py:22
  32.0 18.7 %collective-permute-start.4 = (f32[9,8,1,128]{3,0,2,1:T(8,128)S(1)}, f32[9,8,1,128]{3,0,2,1:T(8,128)S(1)}, u32[]{:S(2)}, u32[]{:S(2)}) collective-permute-start(f32[9,8,1,128]{3,0,2,1:T(8,128)S(1)} %get-tuple-element.64), channel_id=1, source_target_pairs={{0,1},{1,2},{2,3},{3,4},{4,5},{5,6},{6,7},{7,8},{8,9},{9,10},{10,1... | collective-permute-start | bytes 110600 | tf_op jit(solution)/shard_map/ppermute | solution.py:23
  32.0 18.7 %collective-permute-start.7 = (f32[9,8,1,128]{3,0,2,1:T(8,128)S(1)}, f32[9,8,1,128]{3,0,2,1:T(8,128)S(1)}, u32[]{:S(2)}, u32[]{:S(2)}) collective-permute-start(f32[9,8,1,128]{3,0,2,1:T(8,128)S(1)} %get-tuple-element.65), channel_id=1, source_target_pairs={{1,0},{2,1},{3,2},{4,3},{5,4},{6,5},{7,6},{8,7},{9,8},{10,9},{11,1... | collective-permute-start | bytes 110600 | tf_op jit(solution)/shard_map/ppermute | solution.py:24
  55.1 1.5 copy-start.25
  55.1 1.5 copy-start.26
  60.0 9.2 %copy-start.33 = (s32[16]{0:T(128)S(1)}, s32[16]{0:T(128)}, u32[]{:S(2)}) copy-start(s32[16]{0:T(128)} %copy-done.32) | copy-start | bytes 196
  60.0 13.6 %copy-start = (f32[1,1,9,16,8,128]{5,4,3,2,1,0:T(8,128)S(1)}, f32[1,1,9,16,8,128]{5,4,3,2,1,0:T(8,128)}, u32[]{:S(2)}) copy-start(f32[1,1,9,16,8,128]{5,4,3,2,1,0:T(8,128)} %param.8) | copy-start | bytes 1769476
  60.0 50.0 %all-to-all-start = ((f32[16,1,28800]{2,1,0:T(1,128)}), f32[16,1,28800]{2,1,0:T(1,128)}, u32[]{:S(2)}, u32[]{:S(2)}) async-start(f32[16,1,28800]{2,1,0:T(1,128)} %broadcast_select_fusion), calls=%async_computation | async-start | bytes 3686400 | tf_op jit(solution)/shard_map/all_to_all | solution.py:181
  69.1 8.5 %copy-start.35 = (f32[9]{0:T(128)S(1)}, f32[9]{0:T(128)}, u32[]{:S(2)}) copy-start(f32[9]{0:T(128)} %param.12) | copy-start | bytes 112
  69.1 9.0 %copy-start.20 = (f32[9]{0:T(128)S(1)}, f32[9]{0:T(128)}, u32[]{:S(2)}) copy-start(f32[9]{0:T(128)} %param.13) | copy-start | bytes 112
  115.4 1.1 copy-start.15
  126.3 1.4 copy-start.13
  127.7 1.6 copy-start.9
  129.3 0.7 copy-start.8
  131.3 0.9 copy-start.11
  131.4 0.9 copy-start.10
  131.5 1.0 copy-start.16
  131.5 1.0 copy-start.22
  131.5 1.0 copy-start.23
  131.5 1.0 copy-start.24
  132.5 5.4 %copy-start.29 = (pred[128]{0:T(512)(128)(4,1)S(1)}, pred[128]{0:T(512)(128)(4,1)}, u32[]{:S(2)}) copy-start(pred[128]{0:T(512)(128)(4,1)} %get-tuple-element.107) | copy-start | bytes 388
  132.5 5.4 %copy-start.30 = (s32[128]{0:T(128)S(1)}, s32[128]{0:T(128)}, u32[]{:S(2)}) copy-start(s32[128]{0:T(128)} %get-tuple-element.109) | copy-start | bytes 1540
  132.5 5.4 %copy-start.31 = (s32[128]{0:T(128)S(1)}, s32[128]{0:T(128)}, u32[]{:S(2)}) copy-start(s32[128]{0:T(128)} %get-tuple-element.110) | copy-start | bytes 1540
  137.9 0.7 copy-start.28
  140.3 6.0 %copy-start.18 = (s32[1,16]{1,0:T(1,128)S(1)}, s32[1,16]{1,0:T(1,128)}, u32[]{:S(2)}) copy-start(s32[1,16]{1,0:T(1,128)} %param.10) | copy-start | bytes 196
  140.3 13.1 %copy-start.2 = (f32[9,16,8,128]{3,0,2,1:T(8,128)S(1)}, f32[9,16,8,128]{3,0,2,1:T(8,128)}, u32[]{:S(2)}) copy-start(f32[9,16,8,128]{3,0,2,1:T(8,128)} %get-tuple-element.104) | copy-start | bytes 1769476
  140.3 33.5 %all-to-all-start.1 = ((f32[16,1,18432]{2,1,0:T(1,128)}), f32[16,1,18432]{2,1,0:T(1,128)S(1)}, u32[]{:S(2)}, u32[]{:S(2)}) async-start(f32[16,1,18432]{2,1,0:T(1,128)} %broadcast_select_fusion.2), calls=%async_computation.1 | async-start | bytes 2359296 | tf_op jit(solution)/shard_map/all_to_all | solution.py:195

commit v5 on v4

--- a/solution.py
+++ b/solution.py
@@ -34,8 +34,8 @@
     levels = lax.broadcasted_iota(jnp.int32, (fields, fields), 1)
     pick_left = (left_ids[:, None] == levels).astype(jnp.float32)
     pick_right = (right_ids[:, None] == levels).astype(jnp.float32)
-    left_term = jnp.einsum("fg,gxyz->fxyz", pick_left, values, precision=lax.Precision.HIGHEST)
-    right_term = jnp.einsum("fg,gxyz->fxyz", pick_right, values, precision=lax.Precision.HIGHEST)
+    left_term = jnp.einsum("fg,gxyz->fxyz", pick_left, values, precision=lax.Precision.HIGH)
+    right_term = jnp.einsum("fg,gxyz->fxyz", pick_right, values, precision=lax.Precision.HIGH)
     return reaction_rates[:, None, None, None] * left_term * right_term
 
 

time: 179 us -> 178 us (level)
  no operation moved by 1% of the time
where the time goes in v5:
time: 178 us
  local copies, waits for them, and re-layouts  43.7 us (25%)
  waiting for transfers between devices  43.3 us (24%)
  starting transfers between devices  36.6 us (21%)
  between operations  20.8 us (12%)
  matrix products  16.6 us (9%)
  other arithmetic  16.5 us (9%)
    all_to_all x1, waiting for transfers between devices, per_device(): arrived = lax.all_to_all(rows, 'fine', 0, 0, tiled=True)  23.8 us
    all_to_all x1, waiting for transfers between devices, per_device(): rows_in = lax.all_to_all(sent, 'fine', 0, 0, tiled=True)  19.4 us
    ppermute x2, starting transfers between devices, with_halo(): high_x = lax.ppermute(block[:, :1], 'base', x_backward)  13.1 us
    dot_general x3, matrix products, reaction(): jnp.einsum('fg,gxyz->fxyz', pick_right, values, precision=lax.Precision.H...  12.5 us
    all_to_all x1, starting transfers between devices, per_device(): arrived = lax.all_to_all(rows, 'fine', 0, 0, tiled=True)  9.15 us
    slice x4, local copies, waits for them, and re-layouts, fine_advance(): above = jnp.where(z_pos == cells_z - 1, high_z, jnp.roll(fine_box, -1, 3))  6.72 us
    ppermute x2, starting transfers between devices, with_halo(): high_y = lax.ppermute(block[:, :, :1], 'fine', y_backward)  6.69 us
    all_to_all x1, starting transfers between devices, per_device(): rows_in = lax.all_to_all(sent, 'fine', 0, 0, tiled=True)  5.96 us
  transfers between devices with their start and end apart: 10, of which 2 were waited for; matrix products, arithmetic and copies ran while one was open for 17% of the time, Pallas kernels for 0%

profile of v5, /device:TPU:34, one launch (start us, length us, event | category | flops | bytes accessed | tf_op | source)
XLA Modules:
  0.0 177.6 jit_solution(14950290774414439574)
XLA Ops:
  0.6 1.4 copy.375
  2.2 6.5 %collective-permute-start.2 = (f32[9,1,16,128]{3,0,2,1:T(8,128)S(1)}, f32[9,1,16,128]{3,0,2,1:T(8,128)S(1)}, u32[]{:S(2)}, u32[]{:S(2)}) collective-permute-start(f32[9,1,16,128]{3,0,2,1:T(8,128)S(1)} %get-tuple-element.74), channel_id=1, source_target_pairs={{16,0},{32,16},{48,32},{64,48},{80,64},{96,80},{112,96},{128,112},... | collective-permute-start | bytes 221192 | tf_op jit(solution)/shard_map/ppermute | solution.py:22
  8.7 0.6 fusion.66
  9.4 1.6 collective-permute-start
  11.0 2.6 %collective-permute-start.3 = (f32[9,8,1,128]{3,0,2,1:T(8,128)}, f32[9,8,1,128]{3,0,2,1:T(8,128)}, u32[]{:S(2)}, u32[]{:S(2)}) collective-permute-start(f32[9,8,1,128]{3,0,2,1:T(8,128)} %get-tuple-element.73), channel_id=1, source_target_pairs={{1,0},{2,1},{3,2},{4,3},{5,4},{6,5},{7,6},{8,7},{9,8},{10,9},{11,1... | collective-permute-start | bytes 110600 | tf_op jit(solution)/shard_map/ppermute | solution.py:24
  14.1 1.7 fusion.64
  15.8 1.6 fusion.65
  17.7 0.7 gather_fusion
  18.3 0.7 gather_fusion.1
  19.0 0.7 fusion.53
  19.7 0.7 convolution_multiply_fusion.5
  21.1 0.7 select_reduce_fusion.3
  22.8 2.2 %fusion.8 = f32[9,8,16,128]{3,0,2,1:T(8,128)S(1)} fusion(f32[9,8,16,128]{3,0,2,1:T(8,128)S(1)} %convolution_multiply_fusion.5, f32[9,8,16,128]{3,0,2,1:T(8,128)S(1)} %copy.375, f32[9,10,16,128]{3,0,2,1:T(8,128)S(1)} %constant_dynamic-update-slice_fusion, f32[9,1,1,128]{3,0,2,1:T(8,128)S(1)} %broadcast.475, f32[9,8,1,128]{3,0,2,1:T(8,128)} %collective-permute-done.3, ...), kind=kOutput, calls=%fused_computation.26 | convolution fusion | flops 11059281 | bytes 3912264 | tf_op jit(solution)/shard_map/fg,gxyz->fxyz/dot_general | solution.py:38
  25.2 6.5 %collective-permute-start.6 = (f32[9,1,16,128]{3,0,2,1:T(8,128)S(1)}, f32[9,1,16,128]{3,0,2,1:T(8,128)S(1)}, u32[]{:S(2)}, u32[]{:S(2)}) collective-permute-start(f32[9,1,16,128]{3,0,2,1:T(8,128)S(1)} %get-tuple-element.67), channel_id=1, source_target_pairs={{16,0},{32,16},{48,32},{64,48},{80,64},{96,80},{112,96},{128,112},... | collective-permute-start | bytes 221192 | tf_op jit(solution)/shard_map/ppermute | solution.py:22
  31.7 4.1 %collective-permute-start.7 = (f32[9,8,1,128]{3,0,2,1:T(8,128)S(1)}, f32[9,8,1,128]{3,0,2,1:T(8,128)S(1)}, u32[]{:S(2)}, u32[]{:S(2)}) collective-permute-start(f32[9,8,1,128]{3,0,2,1:T(8,128)S(1)} %get-tuple-element.65), channel_id=1, source_target_pairs={{1,0},{2,1},{3,2},{4,3},{5,4},{6,5},{7,6},{8,7},{9,8},{10,9},{11,1... | collective-permute-start | bytes 110600 | tf_op jit(solution)/shard_map/ppermute | solution.py:24
  35.8 0.6 select_reduce_fusion.2
  40.2 1.4 constant_dynamic-slice_fusion.18
  44.1 1.2 constant_dynamic-slice_fusion.19
  50.4 1.1 fusion.1
  51.6 0.7 dynamic-slice_reduce_fusion.6
  52.3 0.7 dynamic-slice_reduce_fusion.4
  56.3 3.3 %broadcast_select_fusion = f32[16,1,28800]{2,1,0:T(1,128)} fusion(pred[16]{0:T(512)(128)(4,1)S(1)} %copy-done.25, pred[16]{0:T(512)(128)(4,1)S(1)} %copy-done.26, f32[28800]{0:T(1024)S(1)} %broadcast_in_dim.250, f32[28800]{0:T(1024)S(1)} %broadcast_in_dim.247), kind=kLoop, calls=%fused_computation.2 | loop fusion | flops 921600 | bytes 2073632 | tf_op jit(solution)/shard_map/jit(_where)/select_n | solution.py:176
  59.6 9.1 %all-to-all-start = ((f32[16,1,28800]{2,1,0:T(1,128)}), f32[16,1,28800]{2,1,0:T(1,128)}, u32[]{:S(2)}, u32[]{:S(2)}) async-start(f32[16,1,28800]{2,1,0:T(1,128)} %broadcast_select_fusion), calls=%async_computation | async-start | bytes 3686400 | tf_op jit(solution)/shard_map/all_to_all | solution.py:181
  74.8 1.2 iota_compare_fusion.9
  77.8 1.7 convolution_multiply_fusion.3
  79.5 1.4 fusion.60
  80.9 1.5 fusion.61
  82.4 1.7 fusion.58
  84.1 1.7 fusion.59
  85.8 23.8 %all-to-all-done = f32[16,1,28800]{2,1,0:T(1,128)} async-done(((f32[16,1,28800]{2,1,0:T(1,128)}), f32[16,1,28800]{2,1,0:T(1,128)}, u32[]{:S(2)}, u32[]{:S(2)}) %all-to-all-start) | async-done | bytes 1843232 | tf_op jit(solution)/shard_map/all_to_all | solution.py:181
  109.6 1.2 dynamic-slice_reduce_fusion.8
  111.6 0.7 fusion.68
  116.1 4.9 %fusion.7 = f32[9,16,8,128]{3,0,2,1:T(8,128)S(1)} fusion(f32[9,16,8,128]{3,0,2,1:T(8,128)} %convolution_multiply_fusion.3, f32[9,15,8,128]{3,0,2,1:T(8,128)} %get-tuple-element.63, f32[9,1,8,128]{3,0,2,1:T(8,128)S(1)} %copy.415, f32[9,1,8,128]{3,0,2,1:T(8,128)S(1)} %copy.417, f32[9,15,8,128]{3,0,2,1:T(8,128)} %get-tuple-element.62, ...), kind=kOutput, calls=%fused_computation.23 | convolution fusion | flops 10911825 | bytes 5317960 | tf_op jit(solution)/shard_map/fg,gxyz->fxyz/dot_general | solution.py:38
  121.0 1.7 fusion.54
  122.7 1.7 fusion.55
  124.3 1.5 fusion.57
  125.9 1.4 fusion.56
  127.3 1.5 convolution_multiply_fusion.1
  132.0 5.4 %bitcast_reduce_fusion = (f32[9,8,8,128]{3,0,2,1:T(8,128)S(1)}, f32[9,16,8,128]{3,0,2,1:T(8,128)}) fusion(f32[9,16,8,128]{3,0,2,1:T(8,128)} %convolution_multiply_fusion.1, f32[9,16,8,128]{3,0,2,1:T(8,128)S(1)} %fusion.7, s32[9]{0:T(128)S(1)} %copy-done.16, f32[9,16,8,1]{3,0,2,1:T(8,128)} %get-tuple-element.50, f32[9,16,8,127]{3,0,2,1:T(8,128)} %get-tuple-element.48, ...), kind=kOutput, calls=%fused_computation.65 | convolution fusion | flops 10985553 | bytes 5612872 | tf_op jit(solution)/shard_map/fg,gxyz->fxyz/dot_general | solution.py:38
  138.0 1.7 broadcast_select_fusion.2
  139.8 6.0 %all-to-all-start.1 = ((f32[16,1,18432]{2,1,0:T(1,128)}), f32[16,1,18432]{2,1,0:T(1,128)S(1)}, u32[]{:S(2)}, u32[]{:S(2)}) async-start(f32[16,1,18432]{2,1,0:T(1,128)} %broadcast_select_fusion.2), calls=%async_computation.1 | async-start | bytes 2359296 | tf_op jit(solution)/shard_map/all_to_all | solution.py:195
  152.1 0.6 compare_and_fusion.4
  152.9 1.0 copy.447
  153.9 19.4 %all-to-all-done.1 = f32[16,1,18432]{2,1,0:T(1,128)S(1)} async-done(((f32[16,1,18432]{2,1,0:T(1,128)}), f32[16,1,18432]{2,1,0:T(1,128)S(1)}, u32[]{:S(2)}, u32[]{:S(2)}) %all-to-all-start.1) | async-done | bytes 1179680 | tf_op jit(solution)/shard_map/all_to_all | solution.py:195
  174.1 0.6 tile.22
  175.2 0.6 tile.25
  175.9 0.7 copy_select_fusion
  176.6 1.0 copy.446
  (242 shorter events, 21.5 us)
Async XLA Ops:
  0.6 12.9 %copy-start.21 = (s32[1,16,2]{1,2,0:T(2,128)S(1)}, s32[1,16,2]{1,2,0:T(2,128)}, u32[]{:S(2)}) copy-start(s32[1,16,2]{1,2,0:T(2,128)} %param.9) | copy-start | bytes 388
  2.1 19.6 %collective-permute-start.1 = (f32[9,1,16,128]{3,0,2,1:T(8,128)S(1)}, f32[9,1,16,128]{3,0,2,1:T(8,128)S(1)}, u32[]{:S(2)}, u32[]{:S(2)}) collective-permute-start(f32[9,1,16,128]{3,0,2,1:T(8,128)S(1)} %get-tuple-element.75), channel_id=1, source_target_pairs={{0,16},{16,32},{32,48},{48,64},{64,80},{80,96},{96,112},{112,128},... | collective-permute-start | bytes 221192 | tf_op jit(solution)/shard_map/ppermute | solution.py:21
  2.2 19.9 %collective-permute-start.2 = (f32[9,1,16,128]{3,0,2,1:T(8,128)S(1)}, f32[9,1,16,128]{3,0,2,1:T(8,128)S(1)}, u32[]{:S(2)}, u32[]{:S(2)}) collective-permute-start(f32[9,1,16,128]{3,0,2,1:T(8,128)S(1)} %get-tuple-element.74), channel_id=1, source_target_pairs={{16,0},{32,16},{48,32},{64,48},{80,64},{96,80},{112,96},{128,112},... | collective-permute-start | bytes 221192 | tf_op jit(solution)/shard_map/ppermute | solution.py:22
  9.4 12.8 %collective-permute-start = (f32[9,8,1,128]{3,0,2,1:T(8,128)}, f32[9,8,1,128]{3,0,2,1:T(8,128)}, u32[]{:S(2)}, u32[]{:S(2)}) collective-permute-start(f32[9,8,1,128]{3,0,2,1:T(8,128)} %get-tuple-element.72), channel_id=1, source_target_pairs={{0,1},{1,2},{2,3},{3,4},{4,5},{5,6},{6,7},{7,8},{8,9},{9,10},{10,1... | collective-permute-start | bytes 110600 | tf_op jit(solution)/shard_map/ppermute | solution.py:23
  11.0 11.2 %collective-permute-start.3 = (f32[9,8,1,128]{3,0,2,1:T(8,128)}, f32[9,8,1,128]{3,0,2,1:T(8,128)}, u32[]{:S(2)}, u32[]{:S(2)}) collective-permute-start(f32[9,8,1,128]{3,0,2,1:T(8,128)} %get-tuple-element.73), channel_id=1, source_target_pairs={{1,0},{2,1},{3,2},{4,3},{5,4},{6,5},{7,6},{8,7},{9,8},{10,9},{11,1... | collective-permute-start | bytes 110600 | tf_op jit(solution)/shard_map/ppermute | solution.py:24
  15.8 1.6 copy-start.17
  15.8 3.9 %copy-start.27 = (s32[9,2]{0,1:T(2,128)S(1)}, s32[9,2]{0,1:T(2,128)}, u32[]{:S(2)}) copy-start(s32[9,2]{0,1:T(2,128)} %param.11) | copy-start | bytes 220
  15.8 3.9 %copy-start.19 = (f32[9]{0:T(128)S(1)}, f32[9]{0:T(128)}, u32[]{:S(2)}) copy-start(f32[9]{0:T(128)} %param.13) | copy-start | bytes 112
  17.5 2.2 %copy-start.1 = (f32[9,8,16,128]{3,2,1,0:T(8,128)S(1)}, f32[9,8,16,128]{3,2,1,0:T(8,128)}, u32[]{:S(2)}) copy-start(f32[9,8,16,128]{3,2,1,0:T(8,128)} %param.7) | copy-start | bytes 1769476
  17.6 2.8 %copy-start.32 = (s32[16]{0:T(128)}, s32[16]{0:T(128)S(1)}, u32[]{:S(2)}) copy-start(s32[16]{0:T(128)S(1)} %get-tuple-element.105) | copy-start | bytes 196
  19.7 3.1 %copy-start.14 = (s32[9]{0:T(128)}, s32[9]{0:T(128)S(1)}, u32[]{:S(2)}) copy-start(s32[9]{0:T(128)S(1)} %get-tuple-element.95) | copy-start | bytes 112
  19.7 58.1 %copy-start.12 = (s32[9]{0:T(128)}, s32[9]{0:T(128)S(1)}, u32[]{:S(2)}) copy-start(s32[9]{0:T(128)S(1)} %get-tuple-element.96) | copy-start | bytes 112
  19.7 3.1 %copy-start.5 = (f32[9,8,16,1]{3,0,2,1:T(8,128)S(1)}, f32[9,8,16,1]{3,0,2,1:T(8,128)}, u32[]{:S(2)}) copy-start(f32[9,8,16,1]{3,0,2,1:T(8,128)} %get-tuple-element.70) | copy-start | bytes 13828
  19.7 3.1 %copy-start.6 = (f32[9,8,16,1]{3,0,2,1:T(8,128)S(1)}, f32[9,8,16,1]{3,0,2,1:T(8,128)}, u32[]{:S(2)}) copy-start(f32[9,8,16,1]{3,0,2,1:T(8,128)} %get-tuple-element.71) | copy-start | bytes 13828
  20.5 2.3 %copy-start.3 = (f32[9,8,16,127]{3,0,2,1:T(8,128)S(1)}, f32[9,8,16,127]{3,0,2,1:T(8,128)}, u32[]{:S(2)}) copy-start(f32[9,8,16,127]{3,0,2,1:T(8,128)} %get-tuple-element.68) | copy-start | bytes 1755652
  20.5 2.3 %copy-start.4 = (f32[9,8,16,127]{3,0,2,1:T(8,128)S(1)}, f32[9,8,16,127]{3,0,2,1:T(8,128)}, u32[]{:S(2)}) copy-start(f32[9,8,16,127]{3,0,2,1:T(8,128)} %get-tuple-element.69) | copy-start | bytes 1755652
  20.5 2.3 %copy-start.34 = (f32[9]{0:T(128)S(1)}, f32[9]{0:T(128)}, u32[]{:S(2)}) copy-start(f32[9]{0:T(128)} %param.12) | copy-start | bytes 112
  22.1 0.7 copy-start.7
  25.1 25.3 %collective-permute-start.5 = (f32[9,1,16,128]{3,0,2,1:T(8,128)S(1)}, f32[9,1,16,128]{3,0,2,1:T(8,128)S(1)}, u32[]{:S(2)}, u32[]{:S(2)}) collective-permute-start(f32[9,1,16,128]{3,0,2,1:T(8,128)S(1)} %get-tuple-element.66), channel_id=1, source_target_pairs={{0,16},{16,32},{32,48},{48,64},{64,80},{80,96},{96,112},{112,128},... | collective-permute-start | bytes 221192 | tf_op jit(solution)/shard_map/ppermute | solution.py:21
  25.2 25.3 %collective-permute-start.6 = (f32[9,1,16,128]{3,0,2,1:T(8,128)S(1)}, f32[9,1,16,128]{3,0,2,1:T(8,128)S(1)}, u32[]{:S(2)}, u32[]{:S(2)}) collective-permute-start(f32[9,1,16,128]{3,0,2,1:T(8,128)S(1)} %get-tuple-element.67), channel_id=1, source_target_pairs={{16,0},{32,16},{48,32},{64,48},{80,64},{96,80},{112,96},{128,112},... | collective-permute-start | bytes 221192 | tf_op jit(solution)/shard_map/ppermute | solution.py:22
  31.7 18.7 %collective-permute-start.4 = (f32[9,8,1,128]{3,0,2,1:T(8,128)S(1)}, f32[9,8,1,128]{3,0,2,1:T(8,128)S(1)}, u32[]{:S(2)}, u32[]{:S(2)}) collective-permute-start(f32[9,8,1,128]{3,0,2,1:T(8,128)S(1)} %get-tuple-element.64), channel_id=1, source_target_pairs={{0,1},{1,2},{2,3},{3,4},{4,5},{5,6},{6,7},{7,8},{8,9},{9,10},{10,1... | collective-permute-start | bytes 110600 | tf_op jit(solution)/shard_map/ppermute | solution.py:23
  31.7 18.7 %collective-permute-start.7 = (f32[9,8,1,128]{3,0,2,1:T(8,128)S(1)}, f32[9,8,1,128]{3,0,2,1:T(8,128)S(1)}, u32[]{:S(2)}, u32[]{:S(2)}) collective-permute-start(f32[9,8,1,128]{3,0,2,1:T(8,128)S(1)} %get-tuple-element.65), channel_id=1, source_target_pairs={{1,0},{2,1},{3,2},{4,3},{5,4},{6,5},{7,6},{8,7},{9,8},{10,9},{11,1... | collective-permute-start | bytes 110600 | tf_op jit(solution)/shard_map/ppermute | solution.py:24
  54.8 1.5 copy-start.25
  54.8 1.5 copy-start.26
  59.6 9.2 %copy-start.33 = (s32[16]{0:T(128)S(1)}, s32[16]{0:T(128)}, u32[]{:S(2)}) copy-start(s32[16]{0:T(128)} %copy-done.32) | copy-start | bytes 196
  59.6 13.6 %copy-start = (f32[1,1,9,16,8,128]{5,4,3,2,1,0:T(8,128)S(1)}, f32[1,1,9,16,8,128]{5,4,3,2,1,0:T(8,128)}, u32[]{:S(2)}) copy-start(f32[1,1,9,16,8,128]{5,4,3,2,1,0:T(8,128)} %param.8) | copy-start | bytes 1769476
  59.6 50.0 %all-to-all-start = ((f32[16,1,28800]{2,1,0:T(1,128)}), f32[16,1,28800]{2,1,0:T(1,128)}, u32[]{:S(2)}, u32[]{:S(2)}) async-start(f32[16,1,28800]{2,1,0:T(1,128)} %broadcast_select_fusion), calls=%async_computation | async-start | bytes 3686400 | tf_op jit(solution)/shard_map/all_to_all | solution.py:181
  68.8 8.5 %copy-start.35 = (f32[9]{0:T(128)S(1)}, f32[9]{0:T(128)}, u32[]{:S(2)}) copy-start(f32[9]{0:T(128)} %param.12) | copy-start | bytes 112
  68.8 9.0 %copy-start.20 = (f32[9]{0:T(128)S(1)}, f32[9]{0:T(128)}, u32[]{:S(2)}) copy-start(f32[9]{0:T(128)} %param.13) | copy-start | bytes 112
  115.0 1.1 copy-start.15
  125.9 1.4 copy-start.13
  127.3 1.5 copy-start.9
  128.8 0.7 copy-start.8
  130.8 0.9 copy-start.11
  130.8 0.9 copy-start.10
  130.9 1.0 copy-start.16
  131.0 1.0 copy-start.22
  131.0 1.0 copy-start.23
  131.0 1.0 copy-start.24
  132.0 5.5 %copy-start.29 = (pred[128]{0:T(512)(128)(4,1)S(1)}, pred[128]{0:T(512)(128)(4,1)}, u32[]{:S(2)}) copy-start(pred[128]{0:T(512)(128)(4,1)} %get-tuple-element.107) | copy-start | bytes 388
  132.0 5.5 %copy-start.30 = (s32[128]{0:T(128)S(1)}, s32[128]{0:T(128)}, u32[]{:S(2)}) copy-start(s32[128]{0:T(128)} %get-tuple-element.109) | copy-start | bytes 1540
  132.0 5.5 %copy-start.31 = (s32[128]{0:T(128)S(1)}, s32[128]{0:T(128)}, u32[]{:S(2)}) copy-start(s32[128]{0:T(128)} %get-tuple-element.110) | copy-start | bytes 1540
  137.4 0.7 copy-start.28
  139.8 6.0 %copy-start.18 = (s32[1,16]{1,0:T(1,128)S(1)}, s32[1,16]{1,0:T(1,128)}, u32[]{:S(2)}) copy-start(s32[1,16]{1,0:T(1,128)} %param.10) | copy-start | bytes 196
  139.8 13.1 %copy-start.2 = (f32[9,16,8,128]{3,0,2,1:T(8,128)S(1)}, f32[9,16,8,128]{3,0,2,1:T(8,128)}, u32[]{:S(2)}) copy-start(f32[9,16,8,128]{3,0,2,1:T(8,128)} %get-tuple-element.104) | copy-start | bytes 1769476
  139.8 33.5 %all-to-all-start.1 = ((f32[16,1,18432]{2,1,0:T(1,128)}), f32[16,1,18432]{2,1,0:T(1,128)S(1)}, u32[]{:S(2)}, u32[]{:S(2)}) async-start(f32[16,1,18432]{2,1,0:T(1,128)} %broadcast_select_fusion.2), calls=%async_computation.1 | async-start | bytes 2359296 | tf_op jit(solution)/shard_map/all_to_all | solution.py:195

commit v6 on v4

--- a/solution.py
+++ b/solution.py
@@ -76,6 +76,32 @@
         + 2.0 * viscosity[:, None, None, None] * (neighbours - 6.0 * fine_box)
         + 0.5 * reaction(fine_box, reaction_rates, left_ids, right_ids)
     )
+
+
+def face_terms(faces, shape):
+    low_x, high_x, low_y, high_y, low_z, high_z = faces
+    fields, cells_x, cells_y, cells_z = shape
+    along_x = jnp.concatenate(
+        [low_x[:, None], jnp.zeros((fields, cells_x - 2, cells_y, cells_z)), high_x[:, None]],
+        axis=1,
+    )
+    along_y = jnp.concatenate(
+        [
+            low_y[:, :, None],
+            jnp.zeros((fields, cells_x, cells_y - 2, cells_z)),
+            high_y[:, :, None],
+        ],
+        axis=2,
+    )
+    along_z = jnp.concatenate(
+        [
+            low_z[:, :, :, None],
+            jnp.zeros((fields, cells_x, cells_y, cells_z - 2)),
+            high_z[:, :, :, None],
+        ],
+        axis=3,
+    )
+    return along_x + along_y + along_z
 
 
 def coarsen(fine_box):
@@ -186,7 +212,12 @@
     mid_faces = [0.5 * (wide[0] + wide[1]) for wide in wide_pair]
 
     fine_box = fine_level[0, 0]
-    fine_box = fine_advance(fine_box, old_faces, viscosity, reaction_rates, left_ids, right_ids)
+    open_faces = [jnp.zeros_like(wide) for wide in old_faces]
+    fine_box = fine_advance(fine_box, open_faces, viscosity, reaction_rates, left_ids, right_ids)
+    fine_box = lax.optimization_barrier(fine_box)
+    fine_box = fine_box + 2.0 * viscosity[:, None, None, None] * face_terms(
+        old_faces, fine_box.shape
+    )
     fine_box = fine_advance(fine_box, mid_faces, viscosity, reaction_rates, left_ids, right_ids)
     averaged = coarsen(fine_box)
 

time: 179 us -> 188 us (1.050)
  local copies, waits for them, and re-layouts: 43.7 us -> 48.4 us
  waiting for transfers between devices: 43.1 us -> 47.5 us
  matrix products: 17.3 us -> 14.5 us
  other arithmetic: 16.5 us -> 19.1 us
  starting transfers between devices: 36.6 us -> 34.5 us
    ppermute x2, starting transfers between devices: 13.1 us -> 6.79 us  [with_halo(): high_x = lax.ppermute(block[:, :1], 'base', x_backward)]
    broadcast_in_dim x40 -> x44, local copies, waits for them, and re-layouts: 4.84 us -> 10.1 us  [widen_face(): return jnp.repeat(jnp.repeat(face, 2, axis=-2), 2, axis=-1)]
    all_to_all x1, starting transfers between devices: 9.15 us -> 12.7 us  [per_device(): arrived = lax.all_to_all(rows, 'fine', 0, 0, tiled=True)]
    all_to_all x1, waiting for transfers between devices: 23.6 us -> 26.4 us  [per_device(): arrived = lax.all_to_all(rows, 'fine', 0, 0, tiled=True)]
    slice x4, local copies, waits for them, and re-layouts: 6.72 us -> 4.05 us  [fine_advance(): above = jnp.where(z_pos == cells_z - 1, high_z, jnp.roll(fine_box, -1, 3))]
    add x0 -> x1, other arithmetic: none -> 2.43 us  [per_device(): fine_box + 2.0 * viscosity[:, None, None, None] * face_terms(old_faces, f...]
    concatenate x0 -> x3, local copies, waits for them, and re-layouts: none -> 1.9 us  [the longest x1 0.67 us: face_terms(): jnp.concatenate([low_y[:, :, None], jnp.zeros((fields, cells_x, cells_y -...]
    unnamed x78 -> x96, local copies, waits for them, and re-layouts: 5.16 us -> 5.68 us
  transfers between devices with their start and end apart: 10 -> 10, of which waited for: 2 -> 2; matrix products, arithmetic and copies ran while one was open for 17% -> 15% of each run, Pallas kernels for 0% -> 0%
where the time goes in v6:
time: 188 us; the launch traced here: 186 us
  local copies, waits for them, and re-layouts  48.4 us (26%)
  waiting for transfers between devices  47.5 us (25%)
  starting transfers between devices  34.5 us (18%)
  between operations  21.7 us (12%)
  other arithmetic  19.1 us (10%)
  matrix products  14.5 us (8%)
    all_to_all x1, waiting for transfers between devices, per_device(): arrived = lax.all_to_all(rows, 'fine', 0, 0, tiled=True)  26.4 us
    all_to_all x1, waiting for transfers between devices, per_device(): rows_in = lax.all_to_all(sent, 'fine', 0, 0, tiled=True)  21.1 us
    all_to_all x1, starting transfers between devices, per_device(): arrived = lax.all_to_all(rows, 'fine', 0, 0, tiled=True)  12.7 us
    dot_general x3, matrix products, reaction(): jnp.einsum('fg,gxyz->fxyz', pick_right, values, precision=lax.Precision.H...  10.8 us
    broadcast_in_dim x44, local copies, waits for them, and re-layouts, widen_face(): return jnp.repeat(jnp.repeat(face, 2, axis=-2), 2, axis=-1)  10.1 us
    all_to_all x1, starting transfers between devices, per_device(): rows_in = lax.all_to_all(sent, 'fine', 0, 0, tiled=True)  6.81 us
    ppermute x2, starting transfers between devices, with_halo(): high_x = lax.ppermute(block[:, :1], 'base', x_backward)  6.79 us
    ppermute x2, starting transfers between devices, with_halo(): high_y = lax.ppermute(block[:, :, :1], 'fine', y_backward)  6.77 us
  transfers between devices with their start and end apart: 10, of which 2 were waited for; matrix products, arithmetic and copies ran while one was open for 15% of the time, Pallas kernels for 0%

profile of v6, /device:TPU:34, one launch (start us, length us, event | category | flops | bytes accessed | tf_op | source)
XLA Modules:
  0.0 185.7 jit_solution(15299498943990754883)
XLA Ops:
  0.6 1.4 copy.419
  2.1 0.7 fusion.64
  2.7 2.6 %collective-permute-start.3 = (f32[9,8,1,128]{3,0,2,1:T(8,128)}, f32[9,8,1,128]{3,0,2,1:T(8,128)}, u32[]{:S(2)}, u32[]{:S(2)}) collective-permute-start(f32[9,8,1,128]{3,0,2,1:T(8,128)} %get-tuple-element.65), channel_id=1, source_target_pairs={{1,0},{2,1},{3,2},{4,3},{5,4},{6,5},{7,6},{8,7},{9,8},{10,9},{11,1... | collective-permute-start | bytes 110600 | tf_op jit(solution)/shard_map/ppermute | solution.py:24
  5.4 6.5 %collective-permute-start.2 = (f32[9,1,16,128]{3,0,2,1:T(8,128)S(1)}, f32[9,1,16,128]{3,0,2,1:T(8,128)S(1)}, u32[]{:S(2)}, u32[]{:S(2)}) collective-permute-start(f32[9,1,16,128]{3,0,2,1:T(8,128)S(1)} %get-tuple-element.66), channel_id=1, source_target_pairs={{16,0},{32,16},{48,32},{64,48},{80,64},{96,80},{112,96},{128,112},... | collective-permute-start | bytes 221192 | tf_op jit(solution)/shard_map/ppermute | solution.py:22
  12.5 1.7 fusion.62
  14.2 1.7 fusion.63
  16.6 0.7 gather_fusion
  17.3 0.7 gather_fusion.1
  17.9 0.7 fusion.55
  19.2 0.9 convolution_multiply_fusion.3
  20.2 0.7 select_reduce_fusion.2
  22.0 2.4 %fusion.6 = f32[9,8,16,128]{3,0,2,1:T(8,128)S(1)} fusion(f32[9,8,16,128]{3,0,2,1:T(8,128)S(1)} %convolution_multiply_fusion.3, f32[9,8,16,128]{3,0,2,1:T(8,128)S(1)} %copy.419, f32[9,10,16,128]{3,0,2,1:T(8,128)S(1)} %constant_dynamic-update-slice_fusion, f32[9,1,1,128]{3,0,2,1:T(8,128)S(1)} %broadcast.504, f32[9,8,1,128]{3,0,2,1:T(8,128)} %collective-permute-done.3, ...), kind=kOutput, calls=%fused_computation.22 | convolution fusion | flops 19021904 | bytes 3912264 | tf_op jit(solution)/shard_map/fg,gxyz->fxyz/dot_general | solution.py:38
  24.4 4.2 %collective-permute-start.7 = (f32[9,8,1,128]{3,0,2,1:T(8,128)S(1)}, f32[9,8,1,128]{3,0,2,1:T(8,128)S(1)}, u32[]{:S(2)}, u32[]{:S(2)}) collective-permute-start(f32[9,8,1,128]{3,0,2,1:T(8,128)S(1)} %get-tuple-element.57), channel_id=1, source_target_pairs={{1,0},{2,1},{3,2},{4,3},{5,4},{6,5},{7,6},{8,7},{9,8},{10,9},{11,1... | collective-permute-start | bytes 110600 | tf_op jit(solution)/shard_map/ppermute | solution.py:24
  29.2 1.1 collective-permute-start.4
  34.9 1.3 constant_dynamic-slice_fusion.19
  37.5 1.4 constant_dynamic-slice_fusion.18
  45.7 1.2 fusion.1
  47.4 0.7 dynamic-slice_reduce_fusion.4
  48.1 0.7 dynamic-slice_reduce_fusion.6
  51.6 3.3 %broadcast_select_fusion = f32[16,1,28800]{2,1,0:T(1,128)} fusion(pred[16]{0:T(512)(128)(4,1)S(1)} %copy-done.34, pred[16]{0:T(512)(128)(4,1)S(1)} %copy-done.35, f32[28800]{0:T(1024)S(1)} %broadcast_in_dim.255, f32[28800]{0:T(1024)S(1)} %broadcast_in_dim.252), kind=kLoop, calls=%fused_computation.2 | loop fusion | flops 921600 | bytes 2073632 | tf_op jit(solution)/shard_map/jit(_where)/select_n | solution.py:202
  54.9 12.7 %all-to-all-start = ((f32[16,1,28800]{2,1,0:T(1,128)}), f32[16,1,28800]{2,1,0:T(1,128)S(1)}, u32[]{:S(2)}, u32[]{:S(2)}) async-start(f32[16,1,28800]{2,1,0:T(1,128)} %broadcast_select_fusion), calls=%async_computation | async-start | bytes 3686400 | tf_op jit(solution)/shard_map/all_to_all | solution.py:207
  73.1 0.9 convolution_multiply_fusion.5
  75.3 3.0 %fusion.8 = f32[9,16,8,128]{3,0,2,1:T(8,128)} fusion(f32[9,16,8,128]{3,0,2,1:T(8,128)S(1)} %convolution_multiply_fusion.5, f32[9,16,8,127]{3,0,2,1:T(8,128)S(1)} %get-tuple-element.73, f32[9,16,8,1]{3,0,2,1:T(8,128)S(1)} %get-tuple-element.75, f32[9,16,8,1]{3,0,2,1:T(8,128)S(1)} %get-tuple-element.74, f32[9,16,8,127]{3,0,2,1:T(8,128)S(1)} %get-tuple-element.72, ...), kind=kOutput, calls=%fused_computation.26 | convolution fusion | flops 18284624 | bytes 5087560 | tf_op jit(solution)/shard_map/fg,gxyz->fxyz/dot_general | solution.py:38
  79.0 0.7 pad.20.clone
  80.9 1.2 iota_compare_fusion.9
  82.7 26.4 %all-to-all-done = f32[16,1,28800]{2,1,0:T(1,128)S(1)} async-done(((f32[16,1,28800]{2,1,0:T(1,128)}), f32[16,1,28800]{2,1,0:T(1,128)S(1)}, u32[]{:S(2)}, u32[]{:S(2)}) %all-to-all-start) | async-done | bytes 1843232 | tf_op jit(solution)/shard_map/all_to_all | solution.py:207
  110.8 0.7 fusion.70
  111.8 0.8 copy.461
  113.1 0.8 copy.460
  115.8 1.9 copy.473
  118.4 1.8 copy.472
  120.2 2.4 %fusion.23 = f32[9,16,8,128]{3,0,2,1:T(8,128)S(1)} fusion(f32[9,16,8,128]{3,0,2,1:T(8,128)} %fusion.8, f32[9,1,8,128]{3,0,2,1:T(8,128)} %copy.461, f32[9,1,8,128]{3,0,2,1:T(8,128)} %copy.460, f32[9,16,1,128]{3,0,2,1:T(8,128)S(1)} %copy.465, f32[9,16,1,128]{3,0,2,1:T(8,128)S(1)} %copy.464, f32[9,16,8,1]{3,0,2,1:T(8,128)} %copy.473, ...), kind=kLoop, calls=%fused_computation.55 | loop fusion | flops 1474560 | bytes 1410692 | tf_op jit(solution)/shard_map/add | solution.py:218
  122.6 1.6 convolution_multiply_fusion.1
  124.3 1.6 fusion.57
  125.9 1.7 fusion.56
  127.8 1.5 fusion.58
  129.7 1.5 fusion.59
  132.5 0.8 slice.391
  135.6 5.4 %bitcast_reduce_fusion = (f32[9,8,8,128]{3,0,2,1:T(8,128)}, f32[9,16,8,128]{3,0,2,1:T(8,128)S(1)}) fusion(f32[9,16,8,128]{3,0,2,1:T(8,128)} %convolution_multiply_fusion.1, f32[9,16,8,128]{3,0,2,1:T(8,128)S(1)} %fusion.23, s32[9]{0:T(128)S(1)} %copy-done.23, f32[9,16,8,1]{3,0,2,1:T(8,128)} %get-tuple-element.50, f32[9,16,8,127]{3,0,2,1:T(8,128)} %get-tuple-element.48, ...), kind=kOutput, calls=%fused_computation.66 | convolution fusion | flops 18948176 | bytes 5612872 | tf_op jit(solution)/shard_map/fg,gxyz->fxyz/dot_general | solution.py:38
  141.1 1.1 reduce_sum.62
  142.6 1.7 broadcast_select_fusion.2
  144.4 6.8 %all-to-all-start.1 = ((f32[16,1,18432]{2,1,0:T(1,128)}), f32[16,1,18432]{2,1,0:T(1,128)}, u32[]{:S(2)}, u32[]{:S(2)}) async-start(f32[16,1,18432]{2,1,0:T(1,128)} %broadcast_select_fusion.2), calls=%async_computation.1 | async-start | bytes 2359296 | tf_op jit(solution)/shard_map/all_to_all | solution.py:226
  156.3 0.7 iota_compare_fusion.11
  158.4 1.0 copy.501
  159.4 21.1 %all-to-all-done.1 = f32[16,1,18432]{2,1,0:T(1,128)} async-done(((f32[16,1,18432]{2,1,0:T(1,128)}), f32[16,1,18432]{2,1,0:T(1,128)}, u32[]{:S(2)}, u32[]{:S(2)}) %all-to-all-start.1) | async-done | bytes 1179680 | tf_op jit(solution)/shard_map/all_to_all | solution.py:226
  180.5 1.3 dynamic-slice_reduce_fusion.9
  184.0 0.7 copy_select_fusion
  184.7 1.0 copy.500
  (277 shorter events, 26.5 us)
Async XLA Ops:
  0.6 11.3 %copy-start.29 = (s32[1,16,2]{1,2,0:T(2,128)S(1)}, s32[1,16,2]{1,2,0:T(2,128)}, u32[]{:S(2)}) copy-start(s32[1,16,2]{1,2,0:T(2,128)} %param.9) | copy-start | bytes 388
  2.7 18.6 %collective-permute-start.3 = (f32[9,8,1,128]{3,0,2,1:T(8,128)}, f32[9,8,1,128]{3,0,2,1:T(8,128)}, u32[]{:S(2)}, u32[]{:S(2)}) collective-permute-start(f32[9,8,1,128]{3,0,2,1:T(8,128)} %get-tuple-element.65), channel_id=1, source_target_pairs={{1,0},{2,1},{3,2},{4,3},{5,4},{6,5},{7,6},{8,7},{9,8},{10,9},{11,1... | collective-permute-start | bytes 110600 | tf_op jit(solution)/shard_map/ppermute | solution.py:24
  5.3 15.6 %collective-permute-start.1 = (f32[9,1,16,128]{3,0,2,1:T(8,128)S(1)}, f32[9,1,16,128]{3,0,2,1:T(8,128)S(1)}, u32[]{:S(2)}, u32[]{:S(2)}) collective-permute-start(f32[9,1,16,128]{3,0,2,1:T(8,128)S(1)} %get-tuple-element.67), channel_id=1, source_target_pairs={{0,16},{16,32},{32,48},{48,64},{64,80},{80,96},{96,112},{112,128},... | collective-permute-start | bytes 221192 | tf_op jit(solution)/shard_map/ppermute | solution.py:21
  5.4 15.9 %collective-permute-start.2 = (f32[9,1,16,128]{3,0,2,1:T(8,128)S(1)}, f32[9,1,16,128]{3,0,2,1:T(8,128)S(1)}, u32[]{:S(2)}, u32[]{:S(2)}) collective-permute-start(f32[9,1,16,128]{3,0,2,1:T(8,128)S(1)} %get-tuple-element.66), channel_id=1, source_target_pairs={{16,0},{32,16},{48,32},{64,48},{80,64},{96,80},{112,96},{128,112},... | collective-permute-start | bytes 221192 | tf_op jit(solution)/shard_map/ppermute | solution.py:22
  11.9 9.4 %collective-permute-start = (f32[9,8,1,128]{3,0,2,1:T(8,128)}, f32[9,8,1,128]{3,0,2,1:T(8,128)}, u32[]{:S(2)}, u32[]{:S(2)}) collective-permute-start(f32[9,8,1,128]{3,0,2,1:T(8,128)} %get-tuple-element.64), channel_id=1, source_target_pairs={{0,1},{1,2},{2,3},{3,4},{4,5},{5,6},{6,7},{7,8},{8,9},{9,10},{10,1... | collective-permute-start | bytes 110600 | tf_op jit(solution)/shard_map/ppermute | solution.py:23
  14.2 1.7 copy-start.36
  14.2 2.2 %copy-start.24 = (s32[1,16]{1,0:T(1,128)S(1)}, s32[1,16]{1,0:T(1,128)}, u32[]{:S(2)}) copy-start(s32[1,16]{1,0:T(1,128)} %param.10) | copy-start | bytes 196
  14.2 5.0 %copy-start.26 = (f32[9]{0:T(128)S(1)}, f32[9]{0:T(128)}, u32[]{:S(2)}) copy-start(f32[9]{0:T(128)} %param.13) | copy-start | bytes 112
  15.9 3.3 %copy-start.1 = (f32[9,8,16,128]{3,2,1,0:T(8,128)S(1)}, f32[9,8,16,128]{3,2,1,0:T(8,128)}, u32[]{:S(2)}) copy-start(f32[9,8,16,128]{3,2,1,0:T(8,128)} %param.7) | copy-start | bytes 1769476
  19.2 2.7 %copy-start.8 = (f32[9,8,16,1]{3,0,2,1:T(8,128)S(1)}, f32[9,8,16,1]{3,0,2,1:T(8,128)}, u32[]{:S(2)}) copy-start(f32[9,8,16,1]{3,0,2,1:T(8,128)} %get-tuple-element.62) | copy-start | bytes 13828
  19.2 2.7 %copy-start.9 = (f32[9,8,16,1]{3,0,2,1:T(8,128)S(1)}, f32[9,8,16,1]{3,0,2,1:T(8,128)}, u32[]{:S(2)}) copy-start(f32[9,8,16,1]{3,0,2,1:T(8,128)} %get-tuple-element.63) | copy-start | bytes 13828
  20.2 1.8 copy-start.6
  20.2 1.8 copy-start.7
  20.2 1.8 copy-start.21
  20.2 1.8 copy-start.43
  24.4 21.2 %collective-permute-start.7 = (f32[9,8,1,128]{3,0,2,1:T(8,128)S(1)}, f32[9,8,1,128]{3,0,2,1:T(8,128)S(1)}, u32[]{:S(2)}, u32[]{:S(2)}) collective-permute-start(f32[9,8,1,128]{3,0,2,1:T(8,128)S(1)} %get-tuple-element.57), channel_id=1, source_target_pairs={{1,0},{2,1},{3,2},{4,3},{5,4},{6,5},{7,6},{8,7},{9,8},{10,9},{11,1... | collective-permute-start | bytes 110600 | tf_op jit(solution)/shard_map/ppermute | solution.py:24
  28.6 17.0 %collective-permute-start.6 = (f32[9,1,16,128]{3,0,2,1:T(8,128)S(1)}, f32[9,1,16,128]{3,0,2,1:T(8,128)S(1)}, u32[]{:S(2)}, u32[]{:S(2)}) collective-permute-start(f32[9,1,16,128]{3,0,2,1:T(8,128)S(1)} %get-tuple-element.59), channel_id=1, source_target_pairs={{16,0},{32,16},{48,32},{64,48},{80,64},{96,80},{112,96},{128,112},... | collective-permute-start | bytes 221192 | tf_op jit(solution)/shard_map/ppermute | solution.py:22
  28.9 16.7 %collective-permute-start.5 = (f32[9,1,16,128]{3,0,2,1:T(8,128)S(1)}, f32[9,1,16,128]{3,0,2,1:T(8,128)S(1)}, u32[]{:S(2)}, u32[]{:S(2)}) collective-permute-start(f32[9,1,16,128]{3,0,2,1:T(8,128)S(1)} %get-tuple-element.58), channel_id=1, source_target_pairs={{0,16},{16,32},{32,48},{48,64},{64,80},{80,96},{96,112},{112,128},... | collective-permute-start | bytes 221192 | tf_op jit(solution)/shard_map/ppermute | solution.py:21
  29.2 16.5 %collective-permute-start.4 = (f32[9,8,1,128]{3,0,2,1:T(8,128)S(1)}, f32[9,8,1,128]{3,0,2,1:T(8,128)S(1)}, u32[]{:S(2)}, u32[]{:S(2)}) collective-permute-start(f32[9,8,1,128]{3,0,2,1:T(8,128)S(1)} %get-tuple-element.56), channel_id=1, source_target_pairs={{0,1},{1,2},{2,3},{3,4},{4,5},{5,6},{6,7},{7,8},{8,9},{9,10},{10,1... | collective-permute-start | bytes 110600 | tf_op jit(solution)/shard_map/ppermute | solution.py:23
  50.1 1.5 copy-start.34
  50.1 1.5 copy-start.35
  54.9 12.7 %copy-start.42 = (s32[16]{0:T(128)S(1)}, s32[16]{0:T(128)}, u32[]{:S(2)}) copy-start(s32[16]{0:T(128)} %copy-done.41) | copy-start | bytes 196
  54.9 17.1 %copy-start = (f32[1,1,9,16,8,128]{5,4,3,2,1,0:T(8,128)S(1)}, f32[1,1,9,16,8,128]{5,4,3,2,1,0:T(8,128)}, u32[]{:S(2)}) copy-start(f32[1,1,9,16,8,128]{5,4,3,2,1,0:T(8,128)} %param.8) | copy-start | bytes 1769476
  54.9 54.2 %all-to-all-start = ((f32[16,1,28800]{2,1,0:T(1,128)}), f32[16,1,28800]{2,1,0:T(1,128)S(1)}, u32[]{:S(2)}, u32[]{:S(2)}) async-start(f32[16,1,28800]{2,1,0:T(1,128)} %broadcast_select_fusion), calls=%async_computation | async-start | bytes 3686400 | tf_op jit(solution)/shard_map/all_to_all | solution.py:207
  67.6 5.5 %copy-start.44 = (f32[9]{0:T(128)S(1)}, f32[9]{0:T(128)}, u32[]{:S(2)}) copy-start(f32[9]{0:T(128)} %param.12) | copy-start | bytes 112
  67.6 5.5 %copy-start.27 = (f32[9]{0:T(128)S(1)}, f32[9]{0:T(128)}, u32[]{:S(2)}) copy-start(f32[9]{0:T(128)} %param.13) | copy-start | bytes 112
  72.4 2.6 %copy-start.30 = (pred[128]{0:T(512)(128)(4,1)}, pred[128]{0:T(512)(128)(4,1)S(1)}, u32[]{:S(2)}) copy-start(pred[128]{0:T(512)(128)(4,1)S(1)} %iota_compare_fusion.7) | copy-start | bytes 388
  73.0 2.0 %copy-start.32 = (pred[128]{0:T(512)(128)(4,1)}, pred[128]{0:T(512)(128)(4,1)S(1)}, u32[]{:S(2)}) copy-start(pred[128]{0:T(512)(128)(4,1)S(1)} %get-tuple-element.108) | copy-start | bytes 388
  111.8 2.3 %copy-start.2 = (f32[9,8,64,2]{0,1,3,2:T(8,128)}, f32[9,8,64,2]{0,1,3,2:T(8,128)S(1)}, u32[]{:S(2)}) copy-start(f32[9,8,64,2]{0,1,3,2:T(8,128)S(1)} %broadcast_in_dim.265) | copy-start | bytes 110596
  113.0 1.9 %copy-start.4 = (f32[9,8,64,2]{0,1,3,2:T(8,128)}, f32[9,8,64,2]{0,1,3,2:T(8,128)S(1)}, u32[]{:S(2)}) copy-start(f32[9,8,64,2]{0,1,3,2:T(8,128)S(1)} %broadcast_in_dim.260) | copy-start | bytes 110596
  115.0 2.6 %copy-start.19 = (f32[1,9,32]{2,1,0:T(8,128)S(1)}, f32[1,9,32]{2,1,0:T(8,128)}, u32[]{:S(2)}) copy-start(f32[1,9,32]{2,1,0:T(8,128)} %get-tuple-element.79) | copy-start | bytes 3460
  115.6 2.1 %copy-start.12 = (f32[9,8,2,4]{0,2,1,3:T(2,128)}, f32[9,8,2,4]{0,2,1,3:T(2,128)S(1)}, u32[]{:S(2)}) copy-start(f32[9,8,2,4]{0,2,1,3:T(2,128)S(1)} %broadcast_in_dim.281) | copy-start | bytes 6916
  120.2 2.4 %copy-start.28 = (f32[9]{0:T(128)S(1)}, f32[9]{0:T(128)}, u32[]{:S(2)}) copy-start(f32[9]{0:T(128)} %param.13) | copy-start | bytes 112
  127.8 1.6 copy-start.3
  129.7 1.6 copy-start.5
  129.7 1.8 copy-start.18
  129.7 1.9 %copy-start.13 = (f32[9,8,2,4]{0,2,1,3:T(2,128)S(1)}, f32[9,8,2,4]{0,2,1,3:T(2,128)}, u32[]{:S(2)}) copy-start(f32[9,8,2,4]{0,2,1,3:T(2,128)} %copy-done.12) | copy-start | bytes 6916
  129.7 2.1 %copy-start.11 = (f32[9,8,2,4]{0,2,1,3:T(2,128)S(1)}, f32[9,8,2,4]{0,2,1,3:T(2,128)}, u32[]{:S(2)}) copy-start(f32[9,8,2,4]{0,2,1,3:T(2,128)} %copy-done.10) | copy-start | bytes 6916
  129.7 2.1 %copy-start.15 = (f32[1,9,512]{2,1,0:T(8,128)S(1)}, f32[1,9,512]{2,1,0:T(8,128)}, u32[]{:S(2)}) copy-start(f32[1,9,512]{2,1,0:T(8,128)} %get-tuple-element.80) | copy-start | bytes 55300
  132.5 1.6 copy-start.17
  134.4 1.2 copy-start.23
  134.4 1.2 copy-start.31
  135.6 6.6 %copy-start.37 = (pred[128]{0:T(512)(128)(4,1)S(1)}, pred[128]{0:T(512)(128)(4,1)}, u32[]{:S(2)}) copy-start(pred[128]{0:T(512)(128)(4,1)} %get-tuple-element.107) | copy-start | bytes 388
  135.6 6.6 %copy-start.39 = (s32[128]{0:T(128)S(1)}, s32[128]{0:T(128)}, u32[]{:S(2)}) copy-start(s32[128]{0:T(128)} %get-tuple-element.109) | copy-start | bytes 1540
  135.6 6.6 %copy-start.40 = (s32[128]{0:T(128)S(1)}, s32[128]{0:T(128)}, u32[]{:S(2)}) copy-start(s32[128]{0:T(128)} %get-tuple-element.110) | copy-start | bytes 1540
  141.0 1.6 copy-start.38
  144.4 6.8 %copy-start.25 = (s32[1,16]{1,0:T(1,128)S(1)}, s32[1,16]{1,0:T(1,128)}, u32[]{:S(2)}) copy-start(s32[1,16]{1,0:T(1,128)} %param.10) | copy-start | bytes 196
  144.4 36.1 %all-to-all-start.1 = ((f32[16,1,18432]{2,1,0:T(1,128)}), f32[16,1,18432]{2,1,0:T(1,128)}, u32[]{:S(2)}, u32[]{:S(2)}) async-start(f32[16,1,18432]{2,1,0:T(1,128)} %broadcast_select_fusion.2), calls=%async_computation.1 | async-start | bytes 2359296 | tf_op jit(solution)/shard_map/all_to_all | solution.py:226
  (7 other events, 6.0 us)

commit v7 on v4

--- a/solution.py
+++ b/solution.py
@@ -178,7 +178,7 @@
         slots[0].reshape(1, -1),
         jnp.where(dest_here[:, None], slots[1].reshape(1, -1), 0.0),
     )
-    arrived = lax.all_to_all(rows, "fine", 0, 0, tiled=True)
+    arrived = lax.all_to_all(rows.reshape(devices_fine, -1, 128), "fine", 0, 0, tiled=True)
     shell_pair = lax.dynamic_index_in_dim(arrived, source_of_mine, 0, keepdims=False)
     shell_pair = shell_pair.reshape(slots[0].shape)
     wide_pair = unpack_faces(shell_pair, cells_x)
@@ -192,7 +192,7 @@
 
     dest_ids = lax.broadcasted_iota(jnp.int32, (devices_fine, 1), 0)
     sent = jnp.where(dest_ids == source_of_mine, averaged.reshape(1, -1), 0.0)
-    rows_in = lax.all_to_all(sent, "fine", 0, 0, tiled=True)
+    rows_in = lax.all_to_all(sent.reshape(devices_fine, -1, 128), "fine", 0, 0, tiled=True)
     y_ids = lax.broadcasted_iota(jnp.int32, (height, cells_z), 0)
     z_ids = lax.broadcasted_iota(jnp.int32, (height, cells_z), 1)
     coarse_out = coarse_next

time: 179 us -> 179 us (level)
  other arithmetic: 16.5 us -> 14.7 us
  transfers between devices with their start and end apart: 10 -> 10, of which waited for: 2 -> 2; matrix products, arithmetic and copies ran while one was open for 17% -> 16% of each run, Pallas kernels for 0% -> 0%
where the time goes in v7:
time: 179 us; the launch traced here: 178 us
  local copies, waits for them, and re-layouts  44.9 us (25%)
  waiting for transfers between devices  44.1 us (25%)
  starting transfers between devices  36.9 us (21%)
  between operations  20.8 us (12%)
  matrix products  16.5 us (9%)
  other arithmetic  14.7 us (8%)
    all_to_all x1, waiting for transfers between devices, per_device(): lax.all_to_all(rows.reshape(devices_fine, -1, 128), 'fine', 0, 0, tiled=T...  24.6 us
    all_to_all x1, waiting for transfers between devices, per_device(): lax.all_to_all(sent.reshape(devices_fine, -1, 128), 'fine', 0, 0, tiled=T...  19.4 us
    ppermute x2, starting transfers between devices, with_halo(): high_x = lax.ppermute(block[:, :1], 'base', x_backward)  13.1 us
    dot_general x3, matrix products, reaction(): jnp.einsum('fg,gxyz->fxyz', pick_right, values, precision=lax.Precision.H...  11.7 us
    all_to_all x1, starting transfers between devices, per_device(): lax.all_to_all(rows.reshape(devices_fine, -1, 128), 'fine', 0, 0, tiled=T...  9.25 us
    slice x4, local copies, waits for them, and re-layouts, fine_advance(): above = jnp.where(z_pos == cells_z - 1, high_z, jnp.roll(fine_box, -1, 3))  6.76 us
    ppermute x2, starting transfers between devices, with_halo(): high_y = lax.ppermute(block[:, :, :1], 'fine', y_backward)  6.69 us
    unnamed x78, local copies, waits for them, and re-layouts  6.21 us
  transfers between devices with their start and end apart: 10, of which 2 were waited for; matrix products, arithmetic and copies ran while one was open for 16% of the time, Pallas kernels for 0%

profile of v7, /device:TPU:34, one launch (start us, length us, event | category | flops | bytes accessed | tf_op | source)
XLA Modules:
  0.0 177.8 jit_solution(18361862642579076834)
XLA Ops:
  0.6 1.4 copy.375
  2.2 6.5 %collective-permute-start.2 = (f32[9,1,16,128]{3,0,2,1:T(8,128)S(1)}, f32[9,1,16,128]{3,0,2,1:T(8,128)S(1)}, u32[]{:S(2)}, u32[]{:S(2)}) collective-permute-start(f32[9,1,16,128]{3,0,2,1:T(8,128)S(1)} %get-tuple-element.74), channel_id=1, source_target_pairs={{16,0},{32,16},{48,32},{64,48},{80,64},{96,80},{112,96},{128,112},... | collective-permute-start | bytes 221192 | tf_op jit(solution)/shard_map/ppermute | solution.py:22
  8.8 1.7 collective-permute-start
  10.4 2.6 %collective-permute-start.3 = (f32[9,8,1,128]{3,0,2,1:T(8,128)S(1)}, f32[9,8,1,128]{3,0,2,1:T(8,128)S(1)}, u32[]{:S(2)}, u32[]{:S(2)}) collective-permute-start(f32[9,8,1,128]{3,0,2,1:T(8,128)S(1)} %get-tuple-element.73), channel_id=1, source_target_pairs={{1,0},{2,1},{3,2},{4,3},{5,4},{6,5},{7,6},{8,7},{9,8},{10,9},{11,1... | collective-permute-start | bytes 110600 | tf_op jit(solution)/shard_map/ppermute | solution.py:24
  13.5 1.3 fusion.64
  14.8 1.7 fusion.65
  17.4 0.7 gather_fusion
  18.0 0.7 gather_fusion.1
  18.7 0.7 fusion.53
  19.5 0.9 convolution_multiply_fusion.5
  21.0 0.7 select_reduce_fusion.3
  22.2 1.4 fusion.8
  23.7 6.5 %collective-permute-start.6 = (f32[9,1,16,128]{3,0,2,1:T(8,128)S(1)}, f32[9,1,16,128]{3,0,2,1:T(8,128)S(1)}, u32[]{:S(2)}, u32[]{:S(2)}) collective-permute-start(f32[9,1,16,128]{3,0,2,1:T(8,128)S(1)} %get-tuple-element.67), channel_id=1, source_target_pairs={{16,0},{32,16},{48,32},{64,48},{80,64},{96,80},{112,96},{128,112},... | collective-permute-start | bytes 221192 | tf_op jit(solution)/shard_map/ppermute | solution.py:22
  30.3 4.1 %collective-permute-start.7 = (f32[9,8,1,128]{3,0,2,1:T(8,128)S(1)}, f32[9,8,1,128]{3,0,2,1:T(8,128)S(1)}, u32[]{:S(2)}, u32[]{:S(2)}) collective-permute-start(f32[9,8,1,128]{3,0,2,1:T(8,128)S(1)} %get-tuple-element.65), channel_id=1, source_target_pairs={{1,0},{2,1},{3,2},{4,3},{5,4},{6,5},{7,6},{8,7},{9,8},{10,9},{11,1... | collective-permute-start | bytes 110600 | tf_op jit(solution)/shard_map/ppermute | solution.py:24
  38.8 1.4 constant_dynamic-slice_fusion.21
  42.7 1.3 constant_dynamic-slice_fusion.22
  49.1 1.6 fusion.1
  50.7 1.2 copy-done.2
  51.9 1.3 dynamic-slice_reduce_fusion.4
  53.3 1.2 constant_dynamic-slice_fusion.19
  54.7 0.9 constant_dynamic-slice_fusion.3
  58.1 1.6 select_select_fusion
  59.6 9.3 %all-to-all-start = ((f32[16,225,128]{2,1,0:T(8,128)}), f32[16,225,128]{2,1,0:T(8,128)}, u32[]{:S(2)}, u32[]{:S(2)}) async-start(f32[16,225,128]{2,1,0:T(8,128)} %select_select_fusion), calls=%async_computation | async-start | bytes 3801088 | tf_op jit(solution)/shard_map/all_to_all | solution.py:181
  74.9 1.2 iota_compare_fusion.9
  77.8 1.9 %convolution_multiply_fusion.3 = f32[9,16,8,128]{3,0,2,1:T(8,128)} fusion(f32[9]{0:T(128)S(1)} %copy-done.18, f32[1,1,9,16,8,128]{5,4,3,2,1,0:T(8,128)S(1)} %copy-done, s32[9]{0:T(128)S(1)} %get-tuple-element.96), kind=kOutput, calls=%fused_computation.22 | convolution fusion | flops 16072785 | bytes 1179720 | tf_op jit(solution)/shard_map/fg,gxyz->fxyz/dot_general | solution.py:37
  79.7 1.5 fusion.60
  81.2 1.5 fusion.61
  82.7 1.7 fusion.58
  84.4 1.7 fusion.59
  86.1 24.6 %all-to-all-done = f32[16,225,128]{2,1,0:T(8,128)} async-done(((f32[16,225,128]{2,1,0:T(8,128)}), f32[16,225,128]{2,1,0:T(8,128)}, u32[]{:S(2)}, u32[]{:S(2)}) %all-to-all-start) | async-done | bytes 1843232 | tf_op jit(solution)/shard_map/all_to_all | solution.py:181
  110.8 0.9 constant_dynamic-slice_fusion.14
  112.4 0.7 fusion.68
  117.0 4.9 %fusion.7 = f32[9,16,8,128]{3,0,2,1:T(8,128)S(1)} fusion(f32[9,16,8,128]{3,0,2,1:T(8,128)} %convolution_multiply_fusion.3, f32[9,15,8,128]{3,0,2,1:T(8,128)} %get-tuple-element.63, f32[9,1,8,128]{3,0,2,1:T(8,128)S(1)} %copy.415, f32[9,1,8,128]{3,0,2,1:T(8,128)S(1)} %copy.417, f32[9,15,8,128]{3,0,2,1:T(8,128)} %get-tuple-element.62, ...), kind=kOutput, calls=%fused_computation.21 | convolution fusion | flops 18874448 | bytes 5317960 | tf_op jit(solution)/shard_map/fg,gxyz->fxyz/dot_general | solution.py:38
  121.9 1.7 fusion.54
  123.6 1.7 fusion.55
  125.3 1.5 fusion.57
  126.8 1.5 fusion.56
  128.3 1.6 convolution_multiply_fusion.1
  133.1 5.4 %bitcast_reduce_fusion = (f32[9,8,8,128]{3,0,2,1:T(8,128)S(1)}, f32[9,16,8,128]{3,0,2,1:T(8,128)}) fusion(f32[9,16,8,128]{3,0,2,1:T(8,128)} %convolution_multiply_fusion.1, f32[9,16,8,128]{3,0,2,1:T(8,128)S(1)} %fusion.7, s32[9]{0:T(128)S(1)} %copy-done.16, f32[9,16,8,1]{3,0,2,1:T(8,128)} %get-tuple-element.50, f32[9,16,8,127]{3,0,2,1:T(8,128)} %get-tuple-element.48, ...), kind=kOutput, calls=%fused_computation.63 | convolution fusion | flops 18948176 | bytes 5612872 | tf_op jit(solution)/shard_map/fg,gxyz->fxyz/dot_general | solution.py:38
  139.1 1.2 broadcast_select_fusion
  140.3 6.0 %all-to-all-start.1 = ((f32[16,144,128]{2,1,0:T(8,128)}), f32[16,144,128]{2,1,0:T(8,128)S(1)}, u32[]{:S(2)}, u32[]{:S(2)}) async-start(f32[16,144,128]{2,1,0:T(8,128)} %broadcast_select_fusion), calls=%async_computation.1 | async-start | bytes 2359296 | tf_op jit(solution)/shard_map/all_to_all | solution.py:195
  150.8 0.7 iota_compare_fusion.5
  152.1 1.2 compare_and_fusion
  153.5 1.0 copy.447
  154.5 19.4 %all-to-all-done.1 = f32[16,144,128]{2,1,0:T(8,128)S(1)} async-done(((f32[16,144,128]{2,1,0:T(8,128)}), f32[16,144,128]{2,1,0:T(8,128)S(1)}, u32[]{:S(2)}, u32[]{:S(2)}) %all-to-all-start.1) | async-done | bytes 1179680 | tf_op jit(solution)/shard_map/all_to_all | solution.py:195
  174.4 0.6 tile.22
  176.1 0.7 copy_select_fusion
  176.8 1.0 copy.446
  (237 shorter events, 20.5 us)
Async XLA Ops:
  0.6 12.3 %copy-start.19 = (s32[1,16,2]{1,2,0:T(2,128)S(1)}, s32[1,16,2]{1,2,0:T(2,128)}, u32[]{:S(2)}) copy-start(s32[1,16,2]{1,2,0:T(2,128)} %param.9) | copy-start | bytes 388
  2.1 19.6 %collective-permute-start.1 = (f32[9,1,16,128]{3,0,2,1:T(8,128)S(1)}, f32[9,1,16,128]{3,0,2,1:T(8,128)S(1)}, u32[]{:S(2)}, u32[]{:S(2)}) collective-permute-start(f32[9,1,16,128]{3,0,2,1:T(8,128)S(1)} %get-tuple-element.75), channel_id=1, source_target_pairs={{0,16},{16,32},{32,48},{48,64},{64,80},{80,96},{96,112},{112,128},... | collective-permute-start | bytes 221192 | tf_op jit(solution)/shard_map/ppermute | solution.py:21
  2.2 19.8 %collective-permute-start.2 = (f32[9,1,16,128]{3,0,2,1:T(8,128)S(1)}, f32[9,1,16,128]{3,0,2,1:T(8,128)S(1)}, u32[]{:S(2)}, u32[]{:S(2)}) collective-permute-start(f32[9,1,16,128]{3,0,2,1:T(8,128)S(1)} %get-tuple-element.74), channel_id=1, source_target_pairs={{16,0},{32,16},{48,32},{64,48},{80,64},{96,80},{112,96},{128,112},... | collective-permute-start | bytes 221192 | tf_op jit(solution)/shard_map/ppermute | solution.py:22
  8.8 13.3 %collective-permute-start = (f32[9,8,1,128]{3,0,2,1:T(8,128)S(1)}, f32[9,8,1,128]{3,0,2,1:T(8,128)S(1)}, u32[]{:S(2)}, u32[]{:S(2)}) collective-permute-start(f32[9,8,1,128]{3,0,2,1:T(8,128)S(1)} %get-tuple-element.72), channel_id=1, source_target_pairs={{0,1},{1,2},{2,3},{3,4},{4,5},{5,6},{6,7},{7,8},{8,9},{9,10},{10,1... | collective-permute-start | bytes 110600 | tf_op jit(solution)/shard_map/ppermute | solution.py:23
  10.4 11.7 %collective-permute-start.3 = (f32[9,8,1,128]{3,0,2,1:T(8,128)S(1)}, f32[9,8,1,128]{3,0,2,1:T(8,128)S(1)}, u32[]{:S(2)}, u32[]{:S(2)}) collective-permute-start(f32[9,8,1,128]{3,0,2,1:T(8,128)S(1)} %get-tuple-element.73), channel_id=1, source_target_pairs={{1,0},{2,1},{3,2},{4,3},{5,4},{6,5},{7,6},{8,7},{9,8},{10,9},{11,1... | collective-permute-start | bytes 110600 | tf_op jit(solution)/shard_map/ppermute | solution.py:24
  14.8 1.7 copy-start.23
  14.8 4.6 %copy-start.27 = (s32[9,2]{0,1:T(2,128)S(1)}, s32[9,2]{0,1:T(2,128)}, u32[]{:S(2)}) copy-start(s32[9,2]{0,1:T(2,128)} %param.11) | copy-start | bytes 220
  14.8 4.6 %copy-start.17 = (f32[9]{0:T(128)S(1)}, f32[9]{0:T(128)}, u32[]{:S(2)}) copy-start(f32[9]{0:T(128)} %param.13) | copy-start | bytes 112
  16.5 2.9 %copy-start.1 = (f32[9,8,16,128]{3,2,1,0:T(8,128)S(1)}, f32[9,8,16,128]{3,2,1,0:T(8,128)}, u32[]{:S(2)}) copy-start(f32[9,8,16,128]{3,2,1,0:T(8,128)} %param.7) | copy-start | bytes 1769476
  16.6 0.5 copy-start.34
  19.4 2.7 %copy-start.14 = (s32[9]{0:T(128)}, s32[9]{0:T(128)S(1)}, u32[]{:S(2)}) copy-start(s32[9]{0:T(128)S(1)} %get-tuple-element.95) | copy-start | bytes 112
  19.4 58.4 %copy-start.12 = (s32[9]{0:T(128)}, s32[9]{0:T(128)S(1)}, u32[]{:S(2)}) copy-start(s32[9]{0:T(128)S(1)} %get-tuple-element.96) | copy-start | bytes 112
  19.4 2.7 %copy-start.7 = (f32[9,8,16,1]{3,0,2,1:T(8,128)S(1)}, f32[9,8,16,1]{3,0,2,1:T(8,128)}, u32[]{:S(2)}) copy-start(f32[9,8,16,1]{3,0,2,1:T(8,128)} %get-tuple-element.71) | copy-start | bytes 13828
  20.4 1.8 copy-start.5
  20.4 1.8 copy-start.6
  20.4 1.8 copy-start.32
  22.1 1.5 copy-start.4
  23.6 25.5 %collective-permute-start.5 = (f32[9,1,16,128]{3,0,2,1:T(8,128)S(1)}, f32[9,1,16,128]{3,0,2,1:T(8,128)S(1)}, u32[]{:S(2)}, u32[]{:S(2)}) collective-permute-start(f32[9,1,16,128]{3,0,2,1:T(8,128)S(1)} %get-tuple-element.66), channel_id=1, source_target_pairs={{0,16},{16,32},{32,48},{48,64},{64,80},{80,96},{96,112},{112,128},... | collective-permute-start | bytes 221192 | tf_op jit(solution)/shard_map/ppermute | solution.py:21
  23.7 25.4 %collective-permute-start.6 = (f32[9,1,16,128]{3,0,2,1:T(8,128)S(1)}, f32[9,1,16,128]{3,0,2,1:T(8,128)S(1)}, u32[]{:S(2)}, u32[]{:S(2)}) collective-permute-start(f32[9,1,16,128]{3,0,2,1:T(8,128)S(1)} %get-tuple-element.67), channel_id=1, source_target_pairs={{16,0},{32,16},{48,32},{64,48},{80,64},{96,80},{112,96},{128,112},... | collective-permute-start | bytes 221192 | tf_op jit(solution)/shard_map/ppermute | solution.py:22
  30.3 18.8 %collective-permute-start.4 = (f32[9,8,1,128]{3,0,2,1:T(8,128)S(1)}, f32[9,8,1,128]{3,0,2,1:T(8,128)S(1)}, u32[]{:S(2)}, u32[]{:S(2)}) collective-permute-start(f32[9,8,1,128]{3,0,2,1:T(8,128)S(1)} %get-tuple-element.64), channel_id=1, source_target_pairs={{0,1},{1,2},{2,3},{3,4},{4,5},{5,6},{6,7},{7,8},{8,9},{9,10},{10,1... | collective-permute-start | bytes 110600 | tf_op jit(solution)/shard_map/ppermute | solution.py:23
  30.3 18.8 %collective-permute-start.7 = (f32[9,8,1,128]{3,0,2,1:T(8,128)S(1)}, f32[9,8,1,128]{3,0,2,1:T(8,128)S(1)}, u32[]{:S(2)}, u32[]{:S(2)}) collective-permute-start(f32[9,8,1,128]{3,0,2,1:T(8,128)S(1)} %get-tuple-element.65), channel_id=1, source_target_pairs={{1,0},{2,1},{3,2},{4,3},{5,4},{6,5},{7,6},{8,7},{9,8},{10,9},{11,1... | collective-permute-start | bytes 110600 | tf_op jit(solution)/shard_map/ppermute | solution.py:24
  50.7 1.2 copy-start.2
  56.5 1.5 copy-start.25
  56.5 1.5 copy-start.26
  59.6 9.3 %copy-start.35 = (s32[16]{0:T(128)S(1)}, s32[16]{0:T(128)}, u32[]{:S(2)}) copy-start(s32[16]{0:T(128)} %copy-done.34) | copy-start | bytes 196
  59.6 13.7 %copy-start = (f32[1,1,9,16,8,128]{5,4,3,2,1,0:T(8,128)S(1)}, f32[1,1,9,16,8,128]{5,4,3,2,1,0:T(8,128)}, u32[]{:S(2)}) copy-start(f32[1,1,9,16,8,128]{5,4,3,2,1,0:T(8,128)} %param.8) | copy-start | bytes 1769476
  59.6 51.1 %all-to-all-start = ((f32[16,225,128]{2,1,0:T(8,128)}), f32[16,225,128]{2,1,0:T(8,128)}, u32[]{:S(2)}, u32[]{:S(2)}) async-start(f32[16,225,128]{2,1,0:T(8,128)} %select_select_fusion), calls=%async_computation | async-start | bytes 3801088 | tf_op jit(solution)/shard_map/all_to_all | solution.py:181
  68.9 8.3 %copy-start.33 = (f32[9]{0:T(128)S(1)}, f32[9]{0:T(128)}, u32[]{:S(2)}) copy-start(f32[9]{0:T(128)} %param.12) | copy-start | bytes 112
  68.9 8.9 %copy-start.18 = (f32[9]{0:T(128)S(1)}, f32[9]{0:T(128)}, u32[]{:S(2)}) copy-start(f32[9]{0:T(128)} %param.13) | copy-start | bytes 112
  115.9 1.1 copy-start.15
  126.8 1.5 copy-start.13
  128.3 1.6 copy-start.9
  129.9 0.7 copy-start.8
  131.9 0.9 copy-start.11
  132.0 0.9 copy-start.10
  132.1 1.0 copy-start.16
  132.1 1.0 copy-start.20
  132.1 1.0 copy-start.21
  132.1 1.0 copy-start.22
  133.1 5.5 %copy-start.29 = (pred[128]{0:T(512)(128)(4,1)S(1)}, pred[128]{0:T(512)(128)(4,1)}, u32[]{:S(2)}) copy-start(pred[128]{0:T(512)(128)(4,1)} %get-tuple-element.117) | copy-start | bytes 388
  133.1 5.5 %copy-start.30 = (s32[128]{0:T(128)S(1)}, s32[128]{0:T(128)}, u32[]{:S(2)}) copy-start(s32[128]{0:T(128)} %get-tuple-element.121) | copy-start | bytes 1540
  133.1 5.5 %copy-start.31 = (s32[128]{0:T(128)S(1)}, s32[128]{0:T(128)}, u32[]{:S(2)}) copy-start(s32[128]{0:T(128)} %get-tuple-element.122) | copy-start | bytes 1540
  138.5 0.6 copy-start.28
  140.3 6.0 %copy-start.24 = (s32[1,16]{1,0:T(1,128)S(1)}, s32[1,16]{1,0:T(1,128)}, u32[]{:S(2)}) copy-start(s32[1,16]{1,0:T(1,128)} %param.10) | copy-start | bytes 196
  140.3 13.2 %copy-start.3 = (f32[9,16,8,128]{3,0,2,1:T(8,128)S(1)}, f32[9,16,8,128]{3,0,2,1:T(8,128)}, u32[]{:S(2)}) copy-start(f32[9,16,8,128]{3,0,2,1:T(8,128)} %get-tuple-element.104) | copy-start | bytes 1769476
  140.3 33.6 %all-to-all-start.1 = ((f32[16,144,128]{2,1,0:T(8,128)}), f32[16,144,128]{2,1,0:T(8,128)S(1)}, u32[]{:S(2)}, u32[]{:S(2)}) async-start(f32[16,144,128]{2,1,0:T(8,128)} %broadcast_select_fusion), calls=%async_computation.1 | async-start | bytes 2359296 | tf_op jit(solution)/shard_map/all_to_all | solution.py:195

commit v8 on v7

--- a/solution.py
+++ b/solution.py
@@ -15,13 +15,16 @@
     return forward, backward
 
 
-def with_halo(block):
+def with_halo(block, edges=None):
+    if edges is None:
+        edges = (block[:, :1], block[:, -1:], block[:, :, :1], block[:, :, -1:])
+    first_x, last_x, first_y, last_y = edges
     x_forward, x_backward = ring_pairs("base")
     y_forward, y_backward = ring_pairs("fine")
-    low_x = lax.ppermute(block[:, -1:], "base", x_forward)
-    high_x = lax.ppermute(block[:, :1], "base", x_backward)
-    low_y = lax.ppermute(block[:, :, -1:], "fine", y_forward)
-    high_y = lax.ppermute(block[:, :, :1], "fine", y_backward)
+    low_x = lax.ppermute(last_x, "base", x_forward)
+    high_x = lax.ppermute(first_x, "base", x_backward)
+    low_y = lax.ppermute(last_y, "fine", y_forward)
+    high_y = lax.ppermute(first_y, "fine", y_backward)
     corner = jnp.zeros_like(block[:, :1, :1])
     low_y = jnp.concatenate([corner, low_y, corner], axis=1)
     high_y = jnp.concatenate([corner, high_y, corner], axis=1)
@@ -160,15 +163,27 @@
         return packed_faces(extended, y_cell[patch_id] - my_index * height, z_cell[patch_id])
 
     old_ext = with_halo(coarse_level)
-    centre = old_ext[:, 1:-1, 1:-1, :]
-    neighbours = (
-        old_ext[:, :-2, 1:-1, :]
-        + old_ext[:, 2:, 1:-1, :]
-        + (old_ext[:, 1:-1, :-2, :] + old_ext[:, 1:-1, 2:, :])
-        + (jnp.roll(centre, 1, 3) + jnp.roll(centre, -1, 3))
-    )
-    coarse_next = coarse_advance(centre, neighbours, viscosity, reaction_rates, left_ids, right_ids)
-    new_ext = with_halo(coarse_next)
+
+    def advance_region(x0, x1, y0, y1):
+        centre = old_ext[:, 1 + x0 : 1 + x1, 1 + y0 : 1 + y1, :]
+        neighbours = (
+            old_ext[:, x0:x1, 1 + y0 : 1 + y1, :]
+            + old_ext[:, 2 + x0 : 2 + x1, 1 + y0 : 1 + y1, :]
+            + (old_ext[:, 1 + x0 : 1 + x1, y0:y1, :] + old_ext[:, 1 + x0 : 1 + x1, 2 + y0 : 2 + y1, :])
+            + (jnp.roll(centre, 1, 3) + jnp.roll(centre, -1, 3))
+        )
+        return coarse_advance(
+            centre, neighbours, viscosity, reaction_rates, left_ids, right_ids
+        )
+
+    coarse_next = advance_region(0, cells_x, 0, height)
+    edges = (
+        advance_region(0, 1, 0, height),
+        advance_region(cells_x - 1, cells_x, 0, height),
+        advance_region(0, cells_x, 0, 1),
+        advance_region(0, cells_x, height - 1, height),
+    )
+    new_ext = with_halo(coarse_next, edges)
     slots = [
         jnp.stack([slot_faces(old_ext, slot_number), slot_faces(new_ext, slot_number)])
         for slot_number in range(MOST)

time: 179 us -> 193 us (1.078)
  matrix products: 16.5 us -> 22.1 us
  local copies, waits for them, and re-layouts: 44.9 us -> 50.3 us
    slice x6 -> x8, local copies, waits for them, and re-layouts: 3.06 us -> 7.93 us  [the longest x6 6.55 us: advance_region(): jnp.roll(centre, -1, 3)]
    dot_general x3 -> x7, matrix products: 4.47 us -> 7.65 us  [reaction(): jnp.einsum('fg,gxyz->fxyz', pick_left, values, precision=lax.Precision.HI...]
    dot_general x3 -> x7, matrix products: 11.7 us -> 14.2 us  [reaction(): jnp.einsum('fg,gxyz->fxyz', pick_right, values, precision=lax.Precision.H...]
    unnamed x78 -> x111, local copies, waits for them, and re-layouts: 6.21 us -> 6.54 us
  transfers between devices with their start and end apart: 10 -> 10, of which waited for: 2 -> 2; matrix products, arithmetic and copies ran while one was open for 16% -> 24% of each run, Pallas kernels for 0% -> 0%
where the time goes in v8:
time: 193 us; the launch traced here: 192 us
  local copies, waits for them, and re-layouts  50.3 us (26%)
  waiting for transfers between devices  43.3 us (22%)
  starting transfers between devices  38.5 us (20%)
  matrix products  22.1 us (11%)
  between operations  21.2 us (11%)
  other arithmetic  16.3 us (8%)
    all_to_all x1, waiting for transfers between devices, per_device(): lax.all_to_all(rows.reshape(devices_fine, -1, 128), 'fine', 0, 0, tiled=T...  23.9 us
    all_to_all x1, waiting for transfers between devices, per_device(): lax.all_to_all(sent.reshape(devices_fine, -1, 128), 'fine', 0, 0, tiled=T...  19.4 us
    dot_general x7, matrix products, reaction(): jnp.einsum('fg,gxyz->fxyz', pick_right, values, precision=lax.Precision.H...  14.2 us
    ppermute x2, starting transfers between devices, with_halo(): high_x = lax.ppermute(first_x, 'base', x_backward)  13.2 us
    all_to_all x1, starting transfers between devices, per_device(): lax.all_to_all(rows.reshape(devices_fine, -1, 128), 'fine', 0, 0, tiled=T...  10.8 us
    dot_general x7, matrix products, reaction(): jnp.einsum('fg,gxyz->fxyz', pick_left, values, precision=lax.Precision.HI...  7.65 us
    ppermute x2, starting transfers between devices, with_halo(): high_y = lax.ppermute(first_y, 'fine', y_backward)  6.91 us
    slice x4, local copies, waits for them, and re-layouts, fine_advance(): above = jnp.where(z_pos == cells_z - 1, high_z, jnp.roll(fine_box, -1, 3))  6.72 us
  transfers between devices with their start and end apart: 10, of which 2 were waited for; matrix products, arithmetic and copies ran while one was open for 24% of the time, Pallas kernels for 0%

profile of v8, /device:TPU:34, one launch (start us, length us, event | category | flops | bytes accessed | tf_op | source)
XLA Modules:
  0.0 191.8 jit_solution(9692358417842572799)
XLA Ops:
  0.6 1.5 copy.581
  2.8 1.6 collective-permute-start
  4.4 2.6 %collective-permute-start.3 = (f32[9,8,1,128]{3,0,1,2:T(8,128)}, f32[9,8,1,128]{3,0,1,2:T(8,128)}, u32[]{:S(2)}, u32[]{:S(2)}) collective-permute-start(f32[9,8,1,128]{3,0,1,2:T(8,128)} %get-tuple-element.84), channel_id=1, source_target_pairs={{1,0},{2,1},{3,2},{4,3},{5,4},{6,5},{7,6},{8,7},{9,8},{10,9},{11,1... | collective-permute-start | bytes 110600 | tf_op jit(solution)/shard_map/ppermute | solution.py:27
  8.0 6.5 %collective-permute-start.2 = (f32[9,1,16,128]{3,0,2,1:T(8,128)}, f32[9,1,16,128]{3,0,2,1:T(8,128)S(1)}, u32[]{:S(2)}, u32[]{:S(2)}) collective-permute-start(f32[9,1,16,128]{3,0,2,1:T(8,128)} %get-tuple-element.87), channel_id=1, source_target_pairs={{16,0},{32,16},{48,32},{64,48},{80,64},{96,80},{112,96},{128,112},... | collective-permute-start | bytes 221192 | tf_op jit(solution)/shard_map/ppermute | solution.py:25
  15.2 1.7 fusion.135
  16.9 1.7 fusion.136
  19.1 1.9 %convolution_multiply_fusion.5 = f32[9,8,16,128]{3,0,1,2:T(8,128)} fusion(f32[9]{0:T(128)S(1)} %copy-done.32, f32[9,8,16,128]{3,2,1,0:T(8,128)S(1)} %copy-done, s32[9]{0:T(128)S(1)} %get-tuple-element.108), kind=kOutput, calls=%fused_computation.19 | convolution fusion | flops 16072785 | bytes 1179720 | tf_op jit(solution)/shard_map/fg,gxyz->fxyz/dot_general | solution.py:40
  21.3 0.8 fusion.133
  22.1 0.9 fusion.134
  23.2 0.8 convolution_multiply_fusion.14
  24.1 0.8 fusion.131
  24.8 0.8 fusion.132
  25.6 0.8 convolution_multiply_fusion.12
  26.4 0.8 select_reduce_fusion
  27.8 1.2 gather_fusion
  29.0 1.2 gather_fusion.1
  30.3 1.4 fusion.122
  32.3 1.2 compare_and_fusion.3
  38.0 1.4 constant_dynamic-slice_fusion.25
  47.8 0.9 fusion.54
  50.2 0.9 fusion.7
  51.5 6.6 %collective-permute-start.6 = (f32[9,1,16,128]{3,0,1,2:T(8,128)S(1)}, f32[9,1,16,128]{3,0,1,2:T(8,128)S(1)}, u32[]{:S(2)}, u32[]{:S(2)}) collective-permute-start(f32[9,1,16,128]{3,0,1,2:T(8,128)S(1)} %fusion.8), channel_id=1, source_target_pairs={{16,0},{32,16},{48,32},{64,48},{80,64},{96,80},{112,96},{128,112},... | collective-permute-start | bytes 221192 | tf_op jit(solution)/shard_map/ppermute | solution.py:25
  58.1 1.1 fusion.11
  59.6 4.4 %collective-permute-start.7 = (f32[9,8,1,128]{3,0,1,2:T(8,128)S(1)}, f32[9,8,1,128]{3,0,1,2:T(8,128)S(1)}, u32[]{:S(2)}, u32[]{:S(2)}) collective-permute-start(f32[9,8,1,128]{3,0,1,2:T(8,128)S(1)} %fusion.12), channel_id=1, source_target_pairs={{1,0},{2,1},{3,2},{4,3},{5,4},{6,5},{7,6},{8,7},{9,8},{10,9},{11,1... | collective-permute-start | bytes 110600 | tf_op jit(solution)/shard_map/ppermute | solution.py:27
  63.9 1.4 fusion.4
  71.1 1.6 select_select_fusion
  72.7 10.8 %all-to-all-start = ((f32[16,225,128]{2,1,0:T(8,128)}), f32[16,225,128]{2,1,0:T(8,128)}, u32[]{:S(2)}, u32[]{:S(2)}) async-start(f32[16,225,128]{2,1,0:T(8,128)} %select_select_fusion), calls=%async_computation | async-start | bytes 3801088 | tf_op jit(solution)/shard_map/all_to_all | solution.py:196
  89.6 1.2 iota_compare_fusion.9
  92.4 1.9 convolution_multiply_fusion.3
  94.3 1.4 fusion.129
  95.8 1.5 fusion.130
  97.3 1.7 fusion.127
  98.9 1.7 fusion.128
  100.7 23.9 %all-to-all-done = f32[16,225,128]{2,1,0:T(8,128)} async-done(((f32[16,225,128]{2,1,0:T(8,128)}), f32[16,225,128]{2,1,0:T(8,128)}, u32[]{:S(2)}, u32[]{:S(2)}) %all-to-all-start) | async-done | bytes 1843232 | tf_op jit(solution)/shard_map/all_to_all | solution.py:196
  124.6 0.9 constant_dynamic-slice_fusion.14
  130.8 4.9 %fusion.3 = f32[9,16,8,128]{3,0,2,1:T(8,128)S(1)} fusion(f32[9,16,8,128]{3,0,2,1:T(8,128)} %convolution_multiply_fusion.3, f32[9,15,8,128]{3,0,2,1:T(8,128)} %get-tuple-element.63, f32[9,1,8,128]{3,0,2,1:T(8,128)S(1)} %copy.656, f32[9,1,8,128]{3,0,2,1:T(8,128)S(1)} %copy.658, f32[9,15,8,128]{3,0,2,1:T(8,128)} %get-tuple-element.62, ...), kind=kOutput, calls=%fused_computation.15 | convolution fusion | flops 18874448 | bytes 5317960 | tf_op jit(solution)/shard_map/fg,gxyz->fxyz/dot_general | solution.py:41
  135.7 1.7 fusion.123
  137.4 1.7 fusion.124
  139.0 1.5 fusion.126
  140.6 1.4 fusion.125
  142.0 1.6 convolution_multiply_fusion.1
  146.8 5.4 %bitcast_reduce_fusion = (f32[9,8,8,128]{3,0,2,1:T(8,128)S(1)}, f32[9,16,8,128]{3,0,2,1:T(8,128)}) fusion(f32[9,16,8,128]{3,0,2,1:T(8,128)} %convolution_multiply_fusion.1, f32[9,16,8,128]{3,0,2,1:T(8,128)S(1)} %fusion.3, s32[9]{0:T(128)S(1)} %copy-done.27, f32[9,16,8,1]{3,0,2,1:T(8,128)} %get-tuple-element.50, f32[9,16,8,127]{3,0,2,1:T(8,128)} %get-tuple-element.48, ...), kind=kOutput, calls=%fused_computation.73 | convolution fusion | flops 18948176 | bytes 5612872 | tf_op jit(solution)/shard_map/fg,gxyz->fxyz/dot_general | solution.py:41
  152.8 1.2 broadcast_select_fusion
  154.0 6.0 %all-to-all-start.1 = ((f32[16,144,128]{2,1,0:T(8,128)}), f32[16,144,128]{2,1,0:T(8,128)S(1)}, u32[]{:S(2)}, u32[]{:S(2)}) async-start(f32[16,144,128]{2,1,0:T(8,128)} %broadcast_select_fusion), calls=%async_computation.1 | async-start | bytes 2359296 | tf_op jit(solution)/shard_map/all_to_all | solution.py:210
  167.3 1.0 copy.688
  168.3 19.4 %all-to-all-done.1 = f32[16,144,128]{2,1,0:T(8,128)S(1)} async-done(((f32[16,144,128]{2,1,0:T(8,128)}), f32[16,144,128]{2,1,0:T(8,128)S(1)}, u32[]{:S(2)}, u32[]{:S(2)}) %all-to-all-start.1) | async-done | bytes 1179680 | tf_op jit(solution)/shard_map/all_to_all | solution.py:210
  189.8 0.8 copy_select_fusion
  190.6 1.2 copy.687
  (291 shorter events, 31.4 us)
Async XLA Ops:
  0.6 6.3 %copy-start = (f32[9,8,16,128]{3,2,1,0:T(8,128)S(1)}, f32[9,8,16,128]{3,2,1,0:T(8,128)}, u32[]{:S(2)}) copy-start(f32[9,8,16,128]{3,2,1,0:T(8,128)} %param.7) | copy-start | bytes 1769476
  2.1 12.5 %copy-start.39 = (s32[1,16,2]{1,2,0:T(2,128)S(1)}, s32[1,16,2]{1,2,0:T(2,128)}, u32[]{:S(2)}) copy-start(s32[1,16,2]{1,2,0:T(2,128)} %param.9) | copy-start | bytes 388
  2.8 45.0 %collective-permute-start = (f32[9,8,1,128]{3,0,1,2:T(8,128)}, f32[9,8,1,128]{3,0,1,2:T(8,128)S(1)}, u32[]{:S(2)}, u32[]{:S(2)}) collective-permute-start(f32[9,8,1,128]{3,0,1,2:T(8,128)} %get-tuple-element.85), channel_id=1, source_target_pairs={{0,1},{1,2},{2,3},{3,4},{4,5},{5,6},{6,7},{7,8},{8,9},{9,10},{10,1... | collective-permute-start | bytes 110600 | tf_op jit(solution)/shard_map/ppermute | solution.py:26
  4.4 43.4 %collective-permute-start.3 = (f32[9,8,1,128]{3,0,1,2:T(8,128)}, f32[9,8,1,128]{3,0,1,2:T(8,128)}, u32[]{:S(2)}, u32[]{:S(2)}) collective-permute-start(f32[9,8,1,128]{3,0,1,2:T(8,128)} %get-tuple-element.84), channel_id=1, source_target_pairs={{1,0},{2,1},{3,2},{4,3},{5,4},{6,5},{7,6},{8,7},{9,8},{10,9},{11,1... | collective-permute-start | bytes 110600 | tf_op jit(solution)/shard_map/ppermute | solution.py:27
  8.0 40.6 %collective-permute-start.1 = (f32[9,1,16,128]{3,0,2,1:T(8,128)}, f32[9,1,16,128]{3,0,2,1:T(8,128)S(1)}, u32[]{:S(2)}, u32[]{:S(2)}) collective-permute-start(f32[9,1,16,128]{3,0,2,1:T(8,128)} %get-tuple-element.86), channel_id=1, source_target_pairs={{0,16},{16,32},{32,48},{48,64},{64,80},{80,96},{96,112},{112,128},... | collective-permute-start | bytes 221192 | tf_op jit(solution)/shard_map/ppermute | solution.py:24
  8.0 41.0 %collective-permute-start.2 = (f32[9,1,16,128]{3,0,2,1:T(8,128)}, f32[9,1,16,128]{3,0,2,1:T(8,128)S(1)}, u32[]{:S(2)}, u32[]{:S(2)}) collective-permute-start(f32[9,1,16,128]{3,0,2,1:T(8,128)} %get-tuple-element.87), channel_id=1, source_target_pairs={{16,0},{32,16},{48,32},{64,48},{80,64},{96,80},{112,96},{128,112},... | collective-permute-start | bytes 221192 | tf_op jit(solution)/shard_map/ppermute | solution.py:25
  16.9 1.7 copy-start.45
  16.9 2.2 %copy-start.32 = (f32[9]{0:T(128)S(1)}, f32[9]{0:T(128)}, u32[]{:S(2)}) copy-start(f32[9]{0:T(128)} %param.13) | copy-start | bytes 112
  19.1 6.5 %copy-start.30 = (s32[9]{0:T(128)}, s32[9]{0:T(128)S(1)}, u32[]{:S(2)}) copy-start(s32[9]{0:T(128)S(1)} %get-tuple-element.108) | copy-start | bytes 112
  22.1 4.4 %copy-start.37 = (s32[1,16]{1,0:T(1,128)S(1)}, s32[1,16]{1,0:T(1,128)}, u32[]{:S(2)}) copy-start(s32[1,16]{1,0:T(1,128)} %param.10) | copy-start | bytes 196
  49.1 8.9 %copy-start.20 = (f32[9,8,1,127]{3,0,1,2:T(8,128)S(1)}, f32[9,8,1,127]{3,0,1,2:T(8,128)}, u32[]{:S(2)}) copy-start(f32[9,8,1,127]{3,0,1,2:T(8,128)} %get-tuple-element.64) | copy-start | bytes 109732
  49.2 8.9 %copy-start.21 = (f32[9,8,1,127]{3,0,1,2:T(8,128)S(1)}, f32[9,8,1,127]{3,0,1,2:T(8,128)}, u32[]{:S(2)}) copy-start(f32[9,8,1,127]{3,0,1,2:T(8,128)} %get-tuple-element.66) | copy-start | bytes 109732
  49.2 8.9 %copy-start.22 = (f32[9,8,1,1]{3,0,1,2:T(8,128)S(1)}, f32[9,8,1,1]{3,0,1,2:T(8,128)}, u32[]{:S(2)}) copy-start(f32[9,8,1,1]{3,0,1,2:T(8,128)} %get-tuple-element.68) | copy-start | bytes 868
  49.2 8.9 %copy-start.23 = (f32[9,8,1,1]{3,0,1,2:T(8,128)S(1)}, f32[9,8,1,1]{3,0,1,2:T(8,128)}, u32[]{:S(2)}) copy-start(f32[9,8,1,1]{3,0,1,2:T(8,128)} %get-tuple-element.70) | copy-start | bytes 868
  49.2 10.1 %copy-start.19 = (f32[9,8,1,1]{3,0,1,2:T(8,128)S(1)}, f32[9,8,1,1]{3,0,1,2:T(8,128)}, u32[]{:S(2)}) copy-start(f32[9,8,1,1]{3,0,1,2:T(8,128)} %get-tuple-element.71) | copy-start | bytes 868
  49.3 1.8 copy-start.8
  49.3 1.8 copy-start.9
  50.2 9.1 %copy-start.16 = (f32[9,8,1,127]{3,0,1,2:T(8,128)S(1)}, f32[9,8,1,127]{3,0,1,2:T(8,128)}, u32[]{:S(2)}) copy-start(f32[9,8,1,127]{3,0,1,2:T(8,128)} %get-tuple-element.65) | copy-start | bytes 109732
  50.2 9.1 %copy-start.17 = (f32[9,8,1,127]{3,0,1,2:T(8,128)S(1)}, f32[9,8,1,127]{3,0,1,2:T(8,128)}, u32[]{:S(2)}) copy-start(f32[9,8,1,127]{3,0,1,2:T(8,128)} %get-tuple-element.67) | copy-start | bytes 109732
  50.2 9.1 %copy-start.18 = (f32[9,8,1,1]{3,0,1,2:T(8,128)S(1)}, f32[9,8,1,1]{3,0,1,2:T(8,128)}, u32[]{:S(2)}) copy-start(f32[9,8,1,1]{3,0,1,2:T(8,128)} %get-tuple-element.69) | copy-start | bytes 868
  50.2 13.7 %copy-start.6 = (f32[9,8,16,1]{3,0,1,2:T(8,128)S(1)}, f32[9,8,16,1]{3,0,1,2:T(8,128)}, u32[]{:S(2)}) copy-start(f32[9,8,16,1]{3,0,1,2:T(8,128)} %get-tuple-element.82) | copy-start | bytes 13828
  50.2 13.7 %copy-start.7 = (f32[9,8,16,1]{3,0,1,2:T(8,128)S(1)}, f32[9,8,16,1]{3,0,1,2:T(8,128)}, u32[]{:S(2)}) copy-start(f32[9,8,16,1]{3,0,1,2:T(8,128)} %get-tuple-element.83) | copy-start | bytes 13828
  51.2 7.0 %copy-start.15 = (f32[9,8,128]{2,0,1:T(8,128)S(1)}, f32[9,8,128]{2,0,1:T(8,128)}, u32[]{:S(2)}) copy-start(f32[9,8,128]{2,0,1:T(8,128)} %convolution_multiply_fusion.14) | copy-start | bytes 110596
  51.2 16.4 %collective-permute-start.5 = (f32[9,1,16,128]{3,0,2,1:T(8,128)}, f32[9,1,16,128]{3,0,2,1:T(8,128)S(1)}, u32[]{:S(2)}, u32[]{:S(2)}) collective-permute-start(f32[9,1,16,128]{3,0,2,1:T(8,128)} %fusion.7), channel_id=1, source_target_pairs={{0,16},{16,32},{32,48},{48,64},{64,80},{80,96},{96,112},{112,128},... | collective-permute-start | bytes 221192 | tf_op jit(solution)/shard_map/ppermute | solution.py:24
  51.2 8.1 %copy-start.14 = (f32[9,8,128]{2,0,1:T(8,128)S(1)}, f32[9,8,128]{2,0,1:T(8,128)}, u32[]{:S(2)}) copy-start(f32[9,8,128]{2,0,1:T(8,128)} %convolution_multiply_fusion.12) | copy-start | bytes 110596
  51.2 12.7 %copy-start.3 = (f32[9,8,16,128]{3,0,1,2:T(8,128)S(1)}, f32[9,8,16,128]{3,0,1,2:T(8,128)}, u32[]{:S(2)}) copy-start(f32[9,8,16,128]{3,0,1,2:T(8,128)} %convolution_multiply_fusion.5) | copy-start | bytes 1769476
  51.2 12.7 %copy-start.4 = (f32[9,8,16,127]{3,0,1,2:T(8,128)S(1)}, f32[9,8,16,127]{3,0,1,2:T(8,128)}, u32[]{:S(2)}) copy-start(f32[9,8,16,127]{3,0,1,2:T(8,128)} %get-tuple-element.80) | copy-start | bytes 1755652
  51.2 12.7 %copy-start.5 = (f32[9,8,16,127]{3,0,1,2:T(8,128)S(1)}, f32[9,8,16,127]{3,0,1,2:T(8,128)}, u32[]{:S(2)}) copy-start(f32[9,8,16,127]{3,0,1,2:T(8,128)} %get-tuple-element.81) | copy-start | bytes 1755652
  51.5 16.1 %collective-permute-start.6 = (f32[9,1,16,128]{3,0,1,2:T(8,128)S(1)}, f32[9,1,16,128]{3,0,1,2:T(8,128)S(1)}, u32[]{:S(2)}, u32[]{:S(2)}) collective-permute-start(f32[9,1,16,128]{3,0,1,2:T(8,128)S(1)} %fusion.8), channel_id=1, source_target_pairs={{16,0},{32,16},{48,32},{64,48},{80,64},{96,80},{112,96},{128,112},... | collective-permute-start | bytes 221192 | tf_op jit(solution)/shard_map/ppermute | solution.py:25
  59.2 8.4 %collective-permute-start.4 = (f32[9,8,1,128]{3,0,1,2:T(8,128)S(1)}, f32[9,8,1,128]{3,0,1,2:T(8,128)S(1)}, u32[]{:S(2)}, u32[]{:S(2)}) collective-permute-start(f32[9,8,1,128]{3,0,1,2:T(8,128)S(1)} %fusion.11), channel_id=1, source_target_pairs={{0,1},{1,2},{2,3},{3,4},{4,5},{5,6},{6,7},{7,8},{8,9},{9,10},{10,1... | collective-permute-start | bytes 110600 | tf_op jit(solution)/shard_map/ppermute | solution.py:26
  59.6 8.0 %collective-permute-start.7 = (f32[9,8,1,128]{3,0,1,2:T(8,128)S(1)}, f32[9,8,1,128]{3,0,1,2:T(8,128)S(1)}, u32[]{:S(2)}, u32[]{:S(2)}) collective-permute-start(f32[9,8,1,128]{3,0,1,2:T(8,128)S(1)} %fusion.12), channel_id=1, source_target_pairs={{1,0},{2,1},{3,2},{4,3},{5,4},{6,5},{7,6},{8,7},{9,8},{10,9},{11,1... | collective-permute-start | bytes 110600 | tf_op jit(solution)/shard_map/ppermute | solution.py:27
  69.6 1.5 copy-start.43
  69.6 1.5 copy-start.44
  72.7 10.8 %copy-start.51 = (s32[16]{0:T(128)S(1)}, s32[16]{0:T(128)}, u32[]{:S(2)}) copy-start(s32[16]{0:T(128)} %copy-done.50) | copy-start | bytes 196
  72.7 15.2 %copy-start.1 = (f32[1,1,9,16,8,128]{5,4,3,2,1,0:T(8,128)S(1)}, f32[1,1,9,16,8,128]{5,4,3,2,1,0:T(8,128)}, u32[]{:S(2)}) copy-start(f32[1,1,9,16,8,128]{5,4,3,2,1,0:T(8,128)} %param.8) | copy-start | bytes 1769476
  72.7 51.8 %all-to-all-start = ((f32[16,225,128]{2,1,0:T(8,128)}), f32[16,225,128]{2,1,0:T(8,128)}, u32[]{:S(2)}, u32[]{:S(2)}) async-start(f32[16,225,128]{2,1,0:T(8,128)} %select_select_fusion), calls=%async_computation | async-start | bytes 3801088 | tf_op jit(solution)/shard_map/all_to_all | solution.py:196
  83.5 8.4 %copy-start.36 = (f32[9]{0:T(128)S(1)}, f32[9]{0:T(128)}, u32[]{:S(2)}) copy-start(f32[9]{0:T(128)} %param.12) | copy-start | bytes 112
  83.5 8.9 %copy-start.31 = (s32[9]{0:T(128)S(1)}, s32[9]{0:T(128)}, u32[]{:S(2)}) copy-start(s32[9]{0:T(128)} %copy-done.30) | copy-start | bytes 112
  83.5 8.9 %copy-start.33 = (f32[9]{0:T(128)S(1)}, f32[9]{0:T(128)}, u32[]{:S(2)}) copy-start(f32[9]{0:T(128)} %param.13) | copy-start | bytes 112
  129.7 1.1 copy-start.27
  140.6 1.4 copy-start.34
  142.0 1.6 copy-start.25
  146.8 5.5 %copy-start.47 = (pred[128]{0:T(512)(128)(4,1)S(1)}, pred[128]{0:T(512)(128)(4,1)}, u32[]{:S(2)}) copy-start(pred[128]{0:T(512)(128)(4,1)} %get-tuple-element.119) | copy-start | bytes 388
  146.8 5.5 %copy-start.48 = (s32[128]{0:T(128)S(1)}, s32[128]{0:T(128)}, u32[]{:S(2)}) copy-start(s32[128]{0:T(128)} %get-tuple-element.121) | copy-start | bytes 1540
  146.8 5.5 %copy-start.49 = (s32[128]{0:T(128)S(1)}, s32[128]{0:T(128)}, u32[]{:S(2)}) copy-start(s32[128]{0:T(128)} %get-tuple-element.122) | copy-start | bytes 1540
  154.0 6.1 %copy-start.38 = (s32[1,16]{1,0:T(1,128)S(1)}, s32[1,16]{1,0:T(1,128)}, u32[]{:S(2)}) copy-start(s32[1,16]{1,0:T(1,128)} %param.10) | copy-start | bytes 196
  154.0 13.3 %copy-start.2 = (f32[9,16,8,128]{3,0,2,1:T(8,128)S(1)}, f32[9,16,8,128]{3,0,2,1:T(8,128)}, u32[]{:S(2)}) copy-start(f32[9,16,8,128]{3,0,2,1:T(8,128)} %get-tuple-element.116) | copy-start | bytes 1769476
  154.0 33.7 %all-to-all-start.1 = ((f32[16,144,128]{2,1,0:T(8,128)}), f32[16,144,128]{2,1,0:T(8,128)S(1)}, u32[]{:S(2)}, u32[]{:S(2)}) async-start(f32[16,144,128]{2,1,0:T(8,128)} %broadcast_select_fusion), calls=%async_computation.1 | async-start | bytes 2359296 | tf_op jit(solution)/shard_map/all_to_all | solution.py:210
  (14 other events, 12.6 us)
